TPU v7x, 256 devices: a whole 4x4x8 slice. The times are simulated.
256 devices in a mesh: tp: 2 (over core), row: 16 (over y, x), col: 8 (over z).
Axes of the slice: x: 4, y: 4, z: 8, core: 2. Of those that a mesh axis runs over, the one named last changes fastest.
Arguments:
- acts: bfloat16 [1024, 128, 4096], P(('row', 'col'), None, 'tp'), may hold values from -6 to 6
- grads: bfloat16 [1024, 128, 4096], P(('row', 'col'), None, 'tp'), may hold values from -6 to 6
- proj_in: bfloat16 [4096, 192], P('tp'), may hold values from -0.09375 to 0.09375
- proj_out: bfloat16 [4096, 64], P('tp'), may hold values from -0.09375 to 0.09375
- curvature: float32 [12288, 12288], P('row', ('tp', 'col')), may hold values from -1 to 7, as said below
Outputs:
- trailing: float32 [12288, 12288], P('row', ('tp', 'col'))
- panel: float32 [12288, 512], P('row', 'tp')
Inputs may be any that keep to these rules, and one draw needn't show every extreme that they name: curvature is symmetric.
All inputs are finite; a program needn't handle non-finite values.
Results may differ from a plain program's by a relative error of at most 0.0021.
Values may be sent and summed in bfloat16 or wider, within the bound.
No kernel may reach another device: no remote copies, remote signals or barrier semaphores. Data moves between devices by JAX's collectives and lax.ppermute only.
A program may use at most 64 MiB of HBM per device.

v0:
```python
import jax
import jax.numpy as jnp
from jax import lax
from jax.experimental import pallas as pl
from jax.experimental.pallas import tpu as pltpu
from jax.sharding import PartitionSpec as P


PANEL = 512
NB = 128
PW = 16
f32 = jnp.float32
bf16 = jnp.bfloat16
HIGHEST = lax.Precision.HIGHEST
HIGH = lax.Precision.HIGH


def halves(x):
    hi = x.astype(bf16)
    return hi, (x - hi.astype(f32)).astype(bf16)


def dot3(a, b, dims):
    ah, al = halves(a)
    bh, bl = halves(b)

    def d(x, y):
        return lax.dot_general(x, y, (dims, ((), ())), preferred_element_type=f32)

    return d(ah, bh) + (d(ah, bl) + d(al, bh))


def factor_rows(rows, j):
    sub = lax.broadcasted_iota(jnp.int32, (PW, NB), 0)
    cols = [jnp.broadcast_to(rows[:, j + k : j + k + 1], (PW, NB)) for k in range(PW)]
    pivots = jnp.ones((PW, NB), f32)
    left, right = rows[:, :NB], rows[:, NB:]
    for k in range(PW):
        p = jnp.broadcast_to(cols[k][k : k + 1, :], (PW, NB))
        pivots = jnp.where(sub == k, p, pivots)
        if k == PW - 1:
            break
        m = jnp.where(sub > k, cols[k] * (1.0 / p), 0.0)
        left = left - m * left[k : k + 1, :]
        right = right - m * right[k : k + 1, :]
        for q in range(k + 1, PW):
            cols[q] = cols[q] - m * cols[q][k : k + 1, :]
    s = lax.rsqrt(pivots)
    return jnp.concatenate([left * s, right * s], axis=1)


def factor_block(x_ref):
    for j in range(0, NB, PW):
        rows = factor_rows(x_ref[j : j + PW, :], j)
        x_ref[j : j + PW, :] = rows
        if j + PW < NB:
            mh, ml = halves(rows[:, :NB])
            rh, rl = halves(rows)
            lhs = jnp.concatenate([mh, mh, ml], axis=0)
            rhs = jnp.concatenate([rh, rl, rh], axis=0)
            upd = lax.dot_general(
                lhs, rhs, (((0,), (0,)), ((), ())), preferred_element_type=f32
            )
            x_ref[j + PW :, :] = x_ref[j + PW :, :] - upd[j + PW :, :]


def factor_kernel(a_ref, o_ref, s_ref, x_ref):
    n = PANEL
    eye = (
        lax.broadcasted_iota(jnp.int32, (n, n), 0)
        == lax.broadcasted_iota(jnp.int32, (n, n), 1)
    ).astype(f32)
    s_ref[:, :n] = a_ref[...]
    s_ref[:, n:] = eye
    for o in range(0, n, NB):
        end = o + NB
        x_ref[:, :NB] = s_ref[o:end, o:end]
        x_ref[:, NB:] = eye[:NB, :NB]
        factor_block(x_ref)
        w = dot3(x_ref[:, NB:], s_ref[o:end, o : n + end], ((1,), (0,)))
        o_ref[o:end, :end] = w[:, n - o :]
        if end < n:
            o_ref[o:end, end:] = jnp.zeros((NB, n - end), f32)
            s_ref[end:, end : n + end] = s_ref[end:, end : n + end] - dot3(
                w[:, NB : n - o], w[:, NB:], ((0,), (0,))
            )


def inverse_factor(a):
    return pl.pallas_call(
        factor_kernel,
        out_shape=jax.ShapeDtypeStruct((PANEL, PANEL), f32),
        in_specs=[pl.BlockSpec(memory_space=pltpu.VMEM)],
        out_specs=pl.BlockSpec(memory_space=pltpu.VMEM),
        scratch_shapes=[
            pltpu.VMEM((PANEL, 2 * PANEL), f32),
            pltpu.VMEM((NB, 2 * NB), f32),
        ],
        compiler_params=pltpu.CompilerParams(vmem_limit_bytes=32 << 20),
        name="inverse_factor",
    )(a)


def wire_halves(x):
    hi = lax.reduce_precision(x, 8, 7)
    return hi.astype(bf16), (x - hi).astype(bf16)


def gather(x, axis):
    n = lax.axis_size(axis)
    return lax.all_to_all(jnp.broadcast_to(x[None], (n,) + x.shape), axis, 0, 0, tiled=True)


def gather_ring(x, axis):
    n = lax.axis_size(axis)
    me = lax.axis_index(axis)
    out = jnp.zeros((n,) + x.shape, x.dtype)
    out = lax.dynamic_update_index_in_dim(out, x, me, 0)
    for k in range(1, n):
        got = lax.ppermute(x, axis, [(i, (i + k) % n) for i in range(n)])
        out = lax.dynamic_update_index_in_dim(out, got, lax.rem(me + n - k, n), 0)
    return out


def gram(a, b):
    return lax.dot_general(a, b, (((0,), (0,)), ((), ())), preferred_element_type=f32)


def per_device(acts, grads, proj_in, proj_out, curvature):
    tp_n, row_n, col_n = (lax.axis_size(a) for a in ("tp", "row", "col"))
    tp = lax.axis_index("tp")
    ex_dev, seq_len, width = acts.shape
    rows_blk, cols_blk = curvature.shape
    act_width, grad_width = proj_in.shape[1], proj_out.shape[1]
    scale = (seq_len * ex_dev * row_n * col_n) ** (-0.5)
    blocks = tp_n * col_n
    piece = PANEL // row_n
    ex = ex_dev // tp_n
    axes = ("tp", "row", "col")
    swap = [(0, 1), (1, 0)]
    first = tp == 0

    def flat(r, b):
        return ((b // col_n) * row_n + r) * col_n + b % col_n

    turn = [(flat(r, b), flat(b, r)) for r in range(row_n) for b in range(blocks)]

    lead = curvature[:PANEL].reshape(row_n, piece, cols_blk)
    piece_col = lax.all_to_all(lead, "row", 0, 0, tiled=True)[0]

    part = jnp.concatenate(
        [
            jnp.dot(acts.reshape(-1, width), proj_in, preferred_element_type=f32),
            jnp.dot(grads.reshape(-1, width), proj_out, preferred_element_type=f32),
        ],
        axis=1,
    ).reshape(tp_n, ex, seq_len, act_width + grad_width)
    keep = jnp.where(first, part[0], part[1])
    give = jnp.where(first, part[1], part[0])
    proj = keep + lax.ppermute(give, "tp", swap)
    feats = (
        jnp.einsum(
            "esi,esj->eij", proj[..., :act_width], proj[..., act_width:], precision=HIGHEST
        )
        * scale
    ).astype(bf16)
    feats = feats.reshape(ex, act_width * grad_width)

    by_block = feats.reshape(ex, blocks, cols_blk).transpose(1, 0, 2)
    lead_feats = jnp.broadcast_to(feats[None, :, :PANEL], (blocks, ex, PANEL))
    out = jnp.concatenate([by_block, lead_feats], axis=2)
    got = lax.all_to_all(out, ("tp", "col"), 0, 0, tiled=True)
    got = got.reshape(blocks * ex, cols_blk + PANEL)

    block = tp * col_n + lax.axis_index("col")
    diag_piece = jnp.where(block == 0, piece_col[:, :PANEL], 0.0)
    diag_piece = diag_piece + lax.ppermute(diag_piece, "tp", [(0, 1)])
    step = col_n // 2
    while step:
        pairs = [(i, i + step) for i in range(0, col_n, 2 * step)]
        diag_piece = diag_piece + lax.ppermute(diag_piece, "col", pairs)
        step //= 2

    n_ex = got.shape[0]
    sent = jnp.concatenate([got, jnp.concatenate(wire_halves(diag_piece), axis=0)], axis=1)
    col_all = gather(sent, "row")
    diag = col_all[:, :, cols_blk + PANEL :].astype(f32)
    diag = (diag[:, :piece] + diag[:, piece:]).reshape(PANEL, PANEL)
    col_all = col_all.reshape(row_n * n_ex, -1)
    col_feats, lead_feats = col_all[:, :cols_blk], col_all[:, cols_blk : cols_blk + PANEL]

    piece_row = lax.ppermute(piece_col, axes, turn)
    turned = lax.ppermute(got[:, :cols_blk], axes, turn)
    mine = jnp.concatenate([turned, *wire_halves(piece_row)], axis=0)
    mine = gather_ring(mine, "col")
    lead_col = gather(piece_col, "row").reshape(-1, cols_blk)

    theirs = lax.ppermute(mine, "tp", swap)
    low, high = jnp.where(first, mine, theirs), jnp.where(first, theirs, mine)
    row_feats, lead_row = [], []
    for x in (low, high):
        row_feats.append(x[:, :n_ex].reshape(-1, rows_blk))
        x = x[:, n_ex:].astype(f32)
        lead_row.append((x[:, :piece] + x[:, piece:]).reshape(-1, rows_blk))
    row_feats, lead_row = jnp.concatenate(row_feats), jnp.concatenate(lead_row)

    inv = inverse_factor(diag + gram(lead_feats, lead_feats))
    panel_row = jnp.dot(inv, lead_row + gram(lead_feats, row_feats), precision=HIGH)
    panel_col = jnp.dot(inv, lead_col + gram(lead_feats, col_feats), precision=HIGH)
    trailing = (
        curvature
        + gram(row_feats, col_feats)
        - lax.dot_general(
            panel_row, panel_col, (((0,), (0,)), ((), ())), precision=HIGH
        )
    )
    half = PANEL // tp_n
    panel = lax.dynamic_slice_in_dim(panel_row, tp * half, half, 0).T
    return (trailing, panel)


def solution(mesh):
    in_specs = (
        P(("row", "col"), None, "tp"),
        P(("row", "col"), None, "tp"),
        P("tp", None),
        P("tp", None),
        P("row", ("tp", "col")),
    )
    out_specs = (P("row", ("tp", "col")), P("row", "tp"))

    return jax.shard_map(
        per_device, mesh=mesh, in_specs=in_specs, out_specs=out_specs, check_vma=False
    )
```

profile of v0, /device:TPU:66, one launch (start us, length us, event | category | flops | bytes accessed | tf_op | source)
XLA Modules:
  0.0 227.7 jit_solution(5449801332981708003)
XLA Ops:
  0.6 2.7 %slice.76 = f32[512,768]{1,0:T(8,128)} slice(f32[768,768]{1,0:T(8,128)} %param.9), slice={[0:512], [0:768]} | slice | bytes 3145728 | tf_op jit(solution)/shard_map/slice | solution.py:148
  3.4 7.5 %all-to-all-start.1 = ((f32[16,32,768]{2,1,0:T(8,128)}), f32[16,32,768]{2,1,0:T(8,128)S(1)}, u32[]{:S(2)}, u32[]{:S(2)}) async-start(f32[16,32,768]{2,1,0:T(8,128)} %bitcast.3), calls=%async_computation.1 | async-start | bytes 3145728 | tf_op jit(solution)/shard_map/all_to_all | solution.py:149
  10.9 4.7 %fusion.19 = f32[1024,192]{0,1:T(8,128)} fusion(bf16[1024,2048]{1,0:T(8,128)(2,1)} %bitcast.59, bf16[2048,192]{0,1:T(8,128)(2,1)S(1)} %copy-done), kind=kOutput, calls=%fused_computation.58 | convolution fusion | flops 805306368 | bytes 5767168 | tf_op jit(solution)/shard_map/dot_general | solution.py:153
  23.6 8.7 %all-to-all-done.1 = f32[16,32,768]{2,1,0:T(8,128)S(1)} async-done(((f32[16,32,768]{2,1,0:T(8,128)}), f32[16,32,768]{2,1,0:T(8,128)S(1)}, u32[]{:S(2)}, u32[]{:S(2)}) %all-to-all-start.1) | async-done | bytes 1572896 | tf_op jit(solution)/shard_map/all_to_all | solution.py:149
  32.4 8.1 %all-to-all-start = ((bf16[16,4,1280]{2,1,0:T(4,128)(2,1)}), bf16[16,4,1280]{2,1,0:T(4,128)(2,1)S(1)}, u32[]{:S(2)}, u32[]{:S(2)}) async-start(bf16[16,4,1280]{2,1,0:T(4,128)(2,1)} %copy.25), calls=%async_computation | async-start | bytes 327680 | tf_op jit(solution)/shard_map/all_to_all | solution.py:172
  42.6 5.9 %all-to-all-done = bf16[16,4,1280]{2,1,0:T(4,128)(2,1)S(1)} async-done(((bf16[16,4,1280]{2,1,0:T(4,128)(2,1)}), bf16[16,4,1280]{2,1,0:T(4,128)(2,1)S(1)}, u32[]{:S(2)}, u32[]{:S(2)}) %all-to-all-start) | async-done | bytes 163872 | tf_op jit(solution)/shard_map/all_to_all | solution.py:172
  48.6 3.1 %collective-permute-start.1 = (bf16[64,768]{1,0:T(8,128)(2,1)S(1)}, bf16[64,768]{1,0:T(8,128)(2,1)S(1)}, u32[]{:S(2)}, u32[]{:S(2)}) collective-permute-start(bf16[64,768]{1,0:T(8,128)(2,1)S(1)} %slice.97), channel_id=1, source_target_pairs={{0,0},{1,8},{2,16},{3,24},{4,32},{5,40},{6,48},{7,56},{128,64},{12... | collective-permute-start | bytes 294920 | tf_op jit(solution)/shard_map/ppermute | solution.py:193
  51.7 3.7 %collective-permute-start.2 = (f32[32,768]{1,0:T(8,128)S(1)}, f32[32,768]{1,0:T(8,128)S(1)}, u32[]{:S(2)}, u32[]{:S(2)}) collective-permute-start(f32[32,768]{1,0:T(8,128)S(1)} %slice_bitcast_fusion), channel_id=1, source_target_pairs={{0,0},{1,8},{2,16},{3,24},{4,32},{5,40},{6,48},{7,56},{128,64},{12... | collective-permute-start | bytes 294920 | tf_op jit(solution)/shard_map/ppermute | solution.py:192
  56.0 12.9 %collective-permute-done.2 = f32[32,768]{1,0:T(8,128)S(1)} collective-permute-done((f32[32,768]{1,0:T(8,128)S(1)}, f32[32,768]{1,0:T(8,128)S(1)}, u32[]{:S(2)}, u32[]{:S(2)}) %collective-permute-start.2) | collective-permute-done | bytes 98336 | tf_op jit(solution)/shard_map/ppermute | solution.py:192
  70.4 10.4 %collective-permute-start.4 = (bf16[128,768]{1,0:T(8,128)(2,1)S(1)}, bf16[128,768]{1,0:T(8,128)(2,1)}, u32[]{:S(2)}, u32[]{:S(2)}) collective-permute-start(bf16[128,768]{1,0:T(8,128)(2,1)S(1)} %pad_maximum_fusion.4), channel_id=1, source_target_pairs={{0,2},{1,3},{2,4},{3,5},{4,6},{5,7},{6,0},{7,1},{8,10},{9,11},{10,... | collective-permute-start | bytes 589832 | tf_op jit(solution)/shard_map/ppermute | solution.py:120
  80.8 6.4 %collective-permute-start.6 = (bf16[128,768]{1,0:T(8,128)(2,1)S(1)}, bf16[128,768]{1,0:T(8,128)(2,1)S(1)}, u32[]{:S(2)}, u32[]{:S(2)}) collective-permute-start(bf16[128,768]{1,0:T(8,128)(2,1)S(1)} %pad_maximum_fusion.4), channel_id=1, source_target_pairs={{0,4},{1,5},{2,6},{3,7},{4,0},{5,1},{6,2},{7,3},{8,12},{9,13},{10,... | collective-permute-start | bytes 589832 | tf_op jit(solution)/shard_map/ppermute | solution.py:120
  89.3 22.3 %collective-permute-done.14 = f32[32,512]{1,0:T(8,128)S(1)} collective-permute-done((f32[32,512]{1,0:T(8,128)S(1)}, f32[32,512]{1,0:T(8,128)S(1)}, u32[]{:S(2)}, u32[]{:S(2)}) %collective-permute-start.14) | collective-permute-done | bytes 65568 | tf_op jit(solution)/shard_map/ppermute | solution.py:181
  115.3 7.7 %all-to-all-start.2 = ((bf16[16,64,1792]{2,1,0:T(8,128)(2,1)}), bf16[16,64,1792]{2,1,0:T(8,128)(2,1)}, u32[]{:S(2)}, u32[]{:S(2)}) async-start(bf16[16,64,1792]{2,1,0:T(8,128)(2,1)} %broadcast_in_dim.60), calls=%async_computation.2 | async-start | bytes 7340032 | tf_op jit(solution)/shard_map/all_to_all | solution.py:111
  123.1 4.4 %collective-permute-start.8 = (bf16[128,768]{1,0:T(8,128)(2,1)S(1)}, bf16[128,768]{1,0:T(8,128)(2,1)S(1)}, u32[]{:S(2)}, u32[]{:S(2)}) collective-permute-start(bf16[128,768]{1,0:T(8,128)(2,1)S(1)} %pad_maximum_fusion.4), channel_id=1, source_target_pairs={{0,6},{1,7},{2,0},{3,1},{4,2},{5,3},{6,4},{7,5},{8,14},{9,15},{10,... | collective-permute-start | bytes 589832 | tf_op jit(solution)/shard_map/ppermute | solution.py:120
  131.4 4.4 %collective-permute-done.8 = bf16[128,768]{1,0:T(8,128)(2,1)S(1)} collective-permute-done((bf16[128,768]{1,0:T(8,128)(2,1)S(1)}, bf16[128,768]{1,0:T(8,128)(2,1)S(1)}, u32[]{:S(2)}, u32[]{:S(2)}) %collective-permute-start.8) | collective-permute-done | bytes 196640 | tf_op jit(solution)/shard_map/ppermute | solution.py:120
  135.8 3.3 %collective-permute-done.9 = bf16[128,768]{1,0:T(8,128)(2,1)S(1)} collective-permute-done((bf16[128,768]{1,0:T(8,128)(2,1)S(1)}, bf16[128,768]{1,0:T(8,128)(2,1)S(1)}, u32[]{:S(2)}, u32[]{:S(2)}) %collective-permute-start.9) | collective-permute-done | bytes 196640 | tf_op jit(solution)/shard_map/ppermute | solution.py:120
  139.2 3.5 %collective-permute-done.10 = bf16[8,128,768]{2,1,0:T(8,128)(2,1)} collective-permute-done((bf16[8,128,768]{2,1,0:T(8,128)(2,1)S(1)}, bf16[8,128,768]{2,1,0:T(8,128)(2,1)}, u32[]{:S(2)}, u32[]{:S(2)}) %collective-permute-start.10) | collective-permute-done | bytes 1572896 | tf_op jit(solution)/shard_map/ppermute | solution.py:198
  148.1 26.4 %all-to-all-done.2 = bf16[16,64,1792]{2,1,0:T(8,128)(2,1)} async-done(((bf16[16,64,1792]{2,1,0:T(8,128)(2,1)}), bf16[16,64,1792]{2,1,0:T(8,128)(2,1)}, u32[]{:S(2)}, u32[]{:S(2)}) %all-to-all-start.2) | async-done | bytes 3670048 | tf_op jit(solution)/shard_map/all_to_all | solution.py:111
  175.8 8.8 %all-to-all-start.3 = ((f32[16,32,768]{2,1,0:T(8,128)}), f32[16,32,768]{2,1,0:T(8,128)S(1)}, u32[]{:S(2)}, u32[]{:S(2)}) async-start(f32[16,32,768]{2,1,0:T(8,128)} %broadcast_in_dim.61), calls=%async_computation.3 | async-start | bytes 3145728 | tf_op jit(solution)/shard_map/all_to_all | solution.py:111
  188.8 16.0 %inverse_factor.1 = f32[512,512]{1,0:T(8,128)S(1)} custom-call(f32[512,512]{1,0:T(8,128)S(1)} %convolution_add_fusion.a_ref), custom_call_target="tpu_custom_call" | custom-call | tf_op jit(solution)/shard_map/inverse_factor/pallas_call | solution.py:90
  204.9 3.4 %fusion.7 = f32[512,768]{1,0:T(8,128)} fusion(bf16[512,768]{1,0:T(8,128)(2,1)S(1)} %bitcast.54, bf16[512,768]{1,0:T(8,128)(2,1)S(1)} %bitcast.56, bf16[1024,1792]{1,0:T(8,128)(2,1)} %bitcast.15), kind=kOutput, calls=%fused_computation.19 | convolution fusion | flops 808452096 | bytes 4194304 | tf_op jit(solution)/shard_map/dot_general | solution.py:126
  208.3 4.3 %fusion.4 = f32[768,768]{1,0:T(8,128)} fusion(bf16[1024,1792]{1,0:T(8,128)(2,1)} %bitcast.15, bf16[512,768]{1,0:T(8,128)(2,1)S(1)} %bitcast.55, bf16[512,768]{1,0:T(8,128)(2,1)S(1)} %bitcast.57), kind=kOutput, calls=%fused_computation.10 | convolution fusion | flops 1211105280 | bytes 5505024 | tf_op jit(solution)/shard_map/dot_general | solution.py:126
  212.6 3.0 %bitcast_add_fusion = f32[512,768]{1,0:T(8,128)S(1)} fusion(f32[16,32,768]{2,1,0:T(8,128)S(1)} %all-to-all-done.3, bf16[1024,1792]{1,0:T(8,128)(2,1)} %bitcast.15), kind=kOutput, calls=%fused_computation.6 | convolution fusion | flops 805699584 | bytes 5767168 | tf_op jit(solution)/shard_map/dot_general | solution.py:126
  221.1 6.6 %add_subtract_fusion = f32[768,768]{1,0:T(8,128)} fusion(f32[768,768]{1,0:T(8,128)} %param.9, f32[768,768]{1,0:T(8,128)} %fusion.4, f32[512,768]{1,0:T(8,128)S(1)} %fusion, f32[512,768]{1,0:T(8,128)} %fusion.21), kind=kOutput, calls=%fused_computation | convolution fusion | flops 1813118976 | bytes 10223616 | tf_op jit(solution)/shard_map/dot_general | solution.py:213
  (82 shorter events, 38.2 us)
Async XLA Ops:
  0.6 10.2 %copy-start = (bf16[2048,192]{0,1:T(8,128)(2,1)S(1)}, bf16[2048,192]{0,1:T(8,128)(2,1)}, u32[]{:S(2)}) copy-start(bf16[2048,192]{0,1:T(8,128)(2,1)} %param.7) | copy-start | bytes 2359300
  3.4 29.0 %all-to-all-start.1 = ((f32[16,32,768]{2,1,0:T(8,128)}), f32[16,32,768]{2,1,0:T(8,128)S(1)}, u32[]{:S(2)}, u32[]{:S(2)}) async-start(f32[16,32,768]{2,1,0:T(8,128)} %bitcast.3), calls=%async_computation.1 | async-start | bytes 3145728 | tf_op jit(solution)/shard_map/all_to_all | solution.py:149
  10.9 4.8 %copy-start.1 = (bf16[8,128,2048]{2,1,0:T(8,128)(2,1)S(1)}, bf16[8,128,2048]{2,1,0:T(8,128)(2,1)}, u32[]{:S(2)}) copy-start(bf16[8,128,2048]{2,1,0:T(8,128)(2,1)} %param.6) | copy-start | bytes 12582916
  10.9 4.8 %copy-start.7 = (bf16[2048,64]{0,1:T(8,128)(2,1)S(1)}, bf16[2048,64]{0,1:T(8,128)(2,1)}, u32[]{:S(2)}) copy-start(bf16[2048,64]{0,1:T(8,128)(2,1)} %param.8) | copy-start | bytes 786436
  19.2 2.1 collective-permute-start
  32.4 16.2 %all-to-all-start = ((bf16[16,4,1280]{2,1,0:T(4,128)(2,1)}), bf16[16,4,1280]{2,1,0:T(4,128)(2,1)S(1)}, u32[]{:S(2)}, u32[]{:S(2)}) async-start(bf16[16,4,1280]{2,1,0:T(4,128)(2,1)} %copy.25), calls=%async_computation | async-start | bytes 327680 | tf_op jit(solution)/shard_map/all_to_all | solution.py:172
  40.5 14.8 %collective-permute-start.11 = (f32[32,512]{1,0:T(8,128)S(1)}, f32[32,512]{1,0:T(8,128)S(1)}, u32[]{:S(2)}, u32[]{:S(2)}) collective-permute-start(f32[32,512]{1,0:T(8,128)S(1)} %slice_select_fusion), channel_id=1, source_target_pairs={{0,128},{1,129},{2,130},{3,131},{4,132},{5,133},{6,134},{7,135},{8... | collective-permute-start | bytes 196616 | tf_op jit(solution)/shard_map/ppermute | solution.py:177
  48.6 21.7 %collective-permute-start.1 = (bf16[64,768]{1,0:T(8,128)(2,1)S(1)}, bf16[64,768]{1,0:T(8,128)(2,1)S(1)}, u32[]{:S(2)}, u32[]{:S(2)}) collective-permute-start(bf16[64,768]{1,0:T(8,128)(2,1)S(1)} %slice.97), channel_id=1, source_target_pairs={{0,0},{1,8},{2,16},{3,24},{4,32},{5,40},{6,48},{7,56},{128,64},{12... | collective-permute-start | bytes 294920 | tf_op jit(solution)/shard_map/ppermute | solution.py:193
  51.7 17.3 %collective-permute-start.2 = (f32[32,768]{1,0:T(8,128)S(1)}, f32[32,768]{1,0:T(8,128)S(1)}, u32[]{:S(2)}, u32[]{:S(2)}) collective-permute-start(f32[32,768]{1,0:T(8,128)S(1)} %slice_bitcast_fusion), channel_id=1, source_target_pairs={{0,0},{1,8},{2,16},{3,24},{4,32},{5,40},{6,48},{7,56},{128,64},{12... | collective-permute-start | bytes 294920 | tf_op jit(solution)/shard_map/ppermute | solution.py:192
  55.4 13.6 %collective-permute-start.12 = (f32[32,512]{1,0:T(8,128)S(1)}, f32[32,512]{1,0:T(8,128)S(1)}, u32[]{:S(2)}, u32[]{:S(2)}) collective-permute-start(f32[32,512]{1,0:T(8,128)S(1)} %fusion.31), channel_id=1, source_target_pairs={{0,4},{8,12},{16,20},{24,28},{32,36},{40,44},{48,52},{56,60},{64,6... | collective-permute-start | bytes 196616 | tf_op jit(solution)/shard_map/ppermute | solution.py:181
  69.0 18.2 %collective-permute-start.13 = (f32[32,512]{1,0:T(8,128)S(1)}, f32[32,512]{1,0:T(8,128)S(1)}, u32[]{:S(2)}, u32[]{:S(2)}) collective-permute-start(f32[32,512]{1,0:T(8,128)S(1)} %add.106), channel_id=1, source_target_pairs={{0,2},{4,6},{8,10},{12,14},{16,18},{20,22},{24,26},{28,30},{32,34}... | collective-permute-start | bytes 196616 | tf_op jit(solution)/shard_map/ppermute | solution.py:181
  70.3 52.8 %collective-permute-start.3 = (bf16[128,768]{1,0:T(8,128)(2,1)S(1)}, bf16[128,768]{1,0:T(8,128)(2,1)}, u32[]{:S(2)}, u32[]{:S(2)}) collective-permute-start(bf16[128,768]{1,0:T(8,128)(2,1)S(1)} %pad_maximum_fusion.4), channel_id=1, source_target_pairs={{0,1},{1,2},{2,3},{3,4},{4,5},{5,6},{6,7},{7,0},{8,9},{9,10},{10,1... | collective-permute-start | bytes 589832 | tf_op jit(solution)/shard_map/ppermute | solution.py:120
  70.4 58.0 %collective-permute-start.4 = (bf16[128,768]{1,0:T(8,128)(2,1)S(1)}, bf16[128,768]{1,0:T(8,128)(2,1)}, u32[]{:S(2)}, u32[]{:S(2)}) collective-permute-start(bf16[128,768]{1,0:T(8,128)(2,1)S(1)} %pad_maximum_fusion.4), channel_id=1, source_target_pairs={{0,2},{1,3},{2,4},{3,5},{4,6},{5,7},{6,0},{7,1},{8,10},{9,11},{10,... | collective-permute-start | bytes 589832 | tf_op jit(solution)/shard_map/ppermute | solution.py:120
  80.8 48.7 %collective-permute-start.5 = (bf16[128,768]{1,0:T(8,128)(2,1)S(1)}, bf16[128,768]{1,0:T(8,128)(2,1)}, u32[]{:S(2)}, u32[]{:S(2)}) collective-permute-start(bf16[128,768]{1,0:T(8,128)(2,1)S(1)} %pad_maximum_fusion.4), channel_id=1, source_target_pairs={{0,3},{1,4},{2,5},{3,6},{4,7},{5,0},{6,1},{7,2},{8,11},{9,12},{10,... | collective-permute-start | bytes 589832 | tf_op jit(solution)/shard_map/ppermute | solution.py:120
  80.8 49.7 %collective-permute-start.6 = (bf16[128,768]{1,0:T(8,128)(2,1)S(1)}, bf16[128,768]{1,0:T(8,128)(2,1)S(1)}, u32[]{:S(2)}, u32[]{:S(2)}) collective-permute-start(bf16[128,768]{1,0:T(8,128)(2,1)S(1)} %pad_maximum_fusion.4), channel_id=1, source_target_pairs={{0,4},{1,5},{2,6},{3,7},{4,0},{5,1},{6,2},{7,3},{8,12},{9,13},{10,... | collective-permute-start | bytes 589832 | tf_op jit(solution)/shard_map/ppermute | solution.py:120
  87.2 24.5 %collective-permute-start.14 = (f32[32,512]{1,0:T(8,128)S(1)}, f32[32,512]{1,0:T(8,128)S(1)}, u32[]{:S(2)}, u32[]{:S(2)}) collective-permute-start(f32[32,512]{1,0:T(8,128)S(1)} %add.107), channel_id=1, source_target_pairs={{0,1},{2,3},{4,5},{6,7},{8,9},{10,11},{12,13},{14,15},{16,17},{18,... | collective-permute-start | bytes 196616 | tf_op jit(solution)/shard_map/ppermute | solution.py:181
  111.7 18.8 %collective-permute-start.7 = (bf16[128,768]{1,0:T(8,128)(2,1)S(1)}, bf16[128,768]{1,0:T(8,128)(2,1)}, u32[]{:S(2)}, u32[]{:S(2)}) collective-permute-start(bf16[128,768]{1,0:T(8,128)(2,1)S(1)} %pad_maximum_fusion.4), channel_id=1, source_target_pairs={{0,5},{1,6},{2,7},{3,0},{4,1},{5,2},{6,3},{7,4},{8,13},{9,14},{10,... | collective-permute-start | bytes 589832 | tf_op jit(solution)/shard_map/ppermute | solution.py:120
  115.3 59.1 %all-to-all-start.2 = ((bf16[16,64,1792]{2,1,0:T(8,128)(2,1)}), bf16[16,64,1792]{2,1,0:T(8,128)(2,1)}, u32[]{:S(2)}, u32[]{:S(2)}) async-start(bf16[16,64,1792]{2,1,0:T(8,128)(2,1)} %broadcast_in_dim.60), calls=%async_computation.2 | async-start | bytes 7340032 | tf_op jit(solution)/shard_map/all_to_all | solution.py:111
  123.1 12.8 %collective-permute-start.8 = (bf16[128,768]{1,0:T(8,128)(2,1)S(1)}, bf16[128,768]{1,0:T(8,128)(2,1)S(1)}, u32[]{:S(2)}, u32[]{:S(2)}) collective-permute-start(bf16[128,768]{1,0:T(8,128)(2,1)S(1)} %pad_maximum_fusion.4), channel_id=1, source_target_pairs={{0,6},{1,7},{2,0},{3,1},{4,2},{5,3},{6,4},{7,5},{8,14},{9,15},{10,... | collective-permute-start | bytes 589832 | tf_op jit(solution)/shard_map/ppermute | solution.py:120
  128.4 10.7 %collective-permute-start.9 = (bf16[128,768]{1,0:T(8,128)(2,1)S(1)}, bf16[128,768]{1,0:T(8,128)(2,1)S(1)}, u32[]{:S(2)}, u32[]{:S(2)}) collective-permute-start(bf16[128,768]{1,0:T(8,128)(2,1)S(1)} %pad_maximum_fusion.4), channel_id=1, source_target_pairs={{0,7},{1,0},{2,1},{3,2},{4,3},{5,4},{6,5},{7,6},{8,15},{9,8},{10,9... | collective-permute-start | bytes 589832 | tf_op jit(solution)/shard_map/ppermute | solution.py:120
  139.1 3.6 %collective-permute-start.10 = (bf16[8,128,768]{2,1,0:T(8,128)(2,1)S(1)}, bf16[8,128,768]{2,1,0:T(8,128)(2,1)}, u32[]{:S(2)}, u32[]{:S(2)}) collective-permute-start(bf16[8,128,768]{2,1,0:T(8,128)(2,1)S(1)} %bitcast_dynamic-update-slice_fusion), channel_id=1, source_target_pairs={{0,128},{128,0},{1,129},{129,1},{2,130},{130,2},{3,131},{131,3},{4... | collective-permute-start | bytes 4718600 | tf_op jit(solution)/shard_map/ppermute | solution.py:198
  175.8 36.8 %all-to-all-start.3 = ((f32[16,32,768]{2,1,0:T(8,128)}), f32[16,32,768]{2,1,0:T(8,128)S(1)}, u32[]{:S(2)}, u32[]{:S(2)}) async-start(f32[16,32,768]{2,1,0:T(8,128)} %broadcast_in_dim.61), calls=%async_computation.3 | async-start | bytes 3145728 | tf_op jit(solution)/shard_map/all_to_all | solution.py:111
  188.8 16.0 %copy-start.5 = (bf16[8,64,768]{2,1,0:T(8,128)(2,1)S(1)}, bf16[8,64,768]{2,1,0:T(8,128)(2,1)}, u32[]{:S(2)}) copy-start(bf16[8,64,768]{2,1,0:T(8,128)(2,1)} %get-tuple-element.15) | copy-start | bytes 2359300
  188.8 16.0 %copy-start.6 = (bf16[8,64,768]{2,1,0:T(8,128)(2,1)S(1)}, bf16[8,64,768]{2,1,0:T(8,128)(2,1)}, u32[]{:S(2)}) copy-start(bf16[8,64,768]{2,1,0:T(8,128)(2,1)} %get-tuple-element.22) | copy-start | bytes 2359300
  (3 other events, 8.2 us)
where the time goes:
time: 229 us; the launch traced here: 228 us
  waiting for transfers between devices  89.6 us (39%)
  starting transfers between devices  67.8 us (30%)
  matrix products  31 us (14%)
  Pallas kernels  16 us (7%)
  local copies, waits for them, and re-layouts  13.6 us (6%)
  other arithmetic  8.59 us (4%)
    all_to_all x2, waiting for transfers between devices, gather(): lax.all_to_all(jnp.broadcast_to(x[None], (n,) + x.shape), axis, 0, 0, til...  26.4 us
    ppermute x7, starting transfers between devices, gather_ring(): got = lax.ppermute(x, axis, [(i, (i + k) % n) for i in range(n)])  22.8 us
    ppermute x3, waiting for transfers between devices, per_device(): diag_piece = diag_piece + lax.ppermute(diag_piece, 'col', pairs)  22.4 us
    all_to_all x2, starting transfers between devices, gather(): lax.all_to_all(jnp.broadcast_to(x[None], (n,) + x.shape), axis, 0, 0, til...  16.6 us
    pallas_call x1, Pallas kernels, inverse_factor(): pl.pallas_call(factor_kernel, out_shape=jax.ShapeDtypeStruct((PANEL, PANE...  16 us
    dot_general x4, matrix products, gram(): lax.dot_general(a, b, (((0,), (0,)), ((), ())), preferred_element_type=f32)  13.2 us
    ppermute x1, waiting for transfers between devices, per_device(): piece_row = lax.ppermute(piece_col, axes, turn)  12.9 us
    all_to_all x1, waiting for transfers between devices, per_device(): piece_col = lax.all_to_all(lead, 'row', 0, 0, tiled=True)[0]  8.73 us
  transfers between devices with their start and end apart: 19, of which 9 were waited for; matrix products, arithmetic and copies ran while one was open for 15% of the time, Pallas kernels for 7%

commit v1 on v0

--- a/solution.py
+++ b/solution.py
@@ -72,18 +72,24 @@
     ).astype(f32)
     s_ref[:, :n] = a_ref[...]
     s_ref[:, n:] = eye
-    for o in range(0, n, NB):
-        end = o + NB
-        x_ref[:, :NB] = s_ref[o:end, o:end]
+    lane = lax.broadcasted_iota(jnp.int32, (NB, n), 1)
+
+    def block(b, carry):
+        o = pl.multiple_of(b * NB, NB)
+        x_ref[:, :NB] = s_ref[pl.ds(o, NB), pl.ds(o, NB)]
         x_ref[:, NB:] = eye[:NB, :NB]
         factor_block(x_ref)
-        w = dot3(x_ref[:, NB:], s_ref[o:end, o : n + end], ((1,), (0,)))
-        o_ref[o:end, :end] = w[:, n - o :]
-        if end < n:
-            o_ref[o:end, end:] = jnp.zeros((NB, n - end), f32)
-            s_ref[end:, end : n + end] = s_ref[end:, end : n + end] - dot3(
-                w[:, NB : n - o], w[:, NB:], ((0,), (0,))
-            )
+        w = dot3(x_ref[:, NB:], s_ref[pl.ds(o, NB), :], ((1,), (0,)))
+        o_ref[pl.ds(o, NB), :] = w[:, n:]
+
+        @pl.when(b < n // NB - 1)
+        def _():
+            u = jnp.where(lane >= o + NB, w[:, :n], 0.0)
+            s_ref[...] = s_ref[...] - dot3(u, w, ((0,), (0,)))
+
+        return carry
+
+    lax.fori_loop(0, n // NB, block, 0)
 
 
 def inverse_factor(a):
@@ -114,11 +120,23 @@
 def gather_ring(x, axis):
     n = lax.axis_size(axis)
     me = lax.axis_index(axis)
+
+    def shift(v, k):
+        return lax.ppermute(v, axis, [(i, (i + k) % n) for i in range(n)])
+
+    def put(out, v, k):
+        return lax.dynamic_update_index_in_dim(out, v, lax.rem(me + n - k, n), 0)
+
+    parts = {0: x}
+    for k in (2, -2, 1, -1):
+        parts[k] = shift(x, k)
+    parts[3] = shift(parts[2], 1)
+    parts[-3] = shift(parts[-2], -1)
+    h = x.shape[0] // 2
+    parts[4] = jnp.concatenate([shift(parts[2][:h], 2), shift(parts[-2][h:], -2)])
     out = jnp.zeros((n,) + x.shape, x.dtype)
-    out = lax.dynamic_update_index_in_dim(out, x, me, 0)
-    for k in range(1, n):
-        got = lax.ppermute(x, axis, [(i, (i + k) % n) for i in range(n)])
-        out = lax.dynamic_update_index_in_dim(out, got, lax.rem(me + n - k, n), 0)
+    for k, v in parts.items():
+        out = put(out, v, k)
     return out
 
 
@@ -128,7 +146,7 @@
 
 def per_device(acts, grads, proj_in, proj_out, curvature):
     tp_n, row_n, col_n = (lax.axis_size(a) for a in ("tp", "row", "col"))
-    tp = lax.axis_index("tp")
+    tp, col = lax.axis_index("tp"), lax.axis_index("col")
     ex_dev, seq_len, width = acts.shape
     rows_blk, cols_blk = curvature.shape
     act_width, grad_width = proj_in.shape[1], proj_out.shape[1]
@@ -145,8 +163,16 @@
 
     turn = [(flat(r, b), flat(b, r)) for r in range(row_n) for b in range(blocks)]
 
-    lead = curvature[:PANEL].reshape(row_n, piece, cols_blk)
-    piece_col = lax.all_to_all(lead, "row", 0, 0, tiled=True)[0]
+    side = int(row_n**0.5)
+    lead = curvature[:PANEL].reshape(side, side, piece, cols_blk)
+    row = lax.axis_index("row")
+    got = sum(lax.ppermute(lead[k], "row", [(0, side * k)]) for k in range(1, side))
+    lead = jnp.where(row == 0, lead[0], got)
+    got = sum(
+        lax.ppermute(lead[k], "row", [(side * j, side * j + k) for j in range(side)])
+        for k in range(1, side)
+    )
+    piece_col = jnp.where(lax.rem(row, side) == 0, lead[0], got)
 
     part = jnp.concatenate(
         [
@@ -172,14 +198,11 @@
     got = lax.all_to_all(out, ("tp", "col"), 0, 0, tiled=True)
     got = got.reshape(blocks * ex, cols_blk + PANEL)
 
-    block = tp * col_n + lax.axis_index("col")
-    diag_piece = jnp.where(block == 0, piece_col[:, :PANEL], 0.0)
-    diag_piece = diag_piece + lax.ppermute(diag_piece, "tp", [(0, 1)])
-    step = col_n // 2
-    while step:
-        pairs = [(i, i + step) for i in range(0, col_n, 2 * step)]
-        diag_piece = diag_piece + lax.ppermute(diag_piece, "col", pairs)
-        step //= 2
+    diag_piece = piece_col[:, :PANEL]
+    got_diag = lax.ppermute(diag_piece, "tp", [(0, 1)])
+    diag_piece = jnp.where(first, diag_piece, got_diag)
+    got_diag = sum(lax.ppermute(diag_piece, "col", [(0, k)]) for k in range(1, col_n))
+    diag_piece = jnp.where(col == 0, diag_piece, got_diag)
 
     n_ex = got.shape[0]
     sent = jnp.concatenate([got, jnp.concatenate(wire_halves(diag_piece), axis=0)], axis=1)

time: 229 us -> 196 us (0.86)
  waiting for transfers between devices: 89.6 us -> 60.8 us
  local copies, waits for them, and re-layouts: 13.6 us -> 8.82 us
  Pallas kernels: 16 us -> 18.7 us
    ppermute x1, waiting for transfers between devices: 12.9 us -> 0.01 us  [per_device(): piece_row = lax.ppermute(piece_col, axes, turn)]
    all_to_all x1 -> x0, waiting for transfers between devices: 8.73 us -> none  [per_device(): piece_col = lax.all_to_all(lead, 'row', 0, 0, tiled=True)[0]]
    ppermute x11 -> x22, starting transfers between devices: 28.8 us -> 36.6 us  [the longest x8 20.5 us: shift(): return lax.ppermute(v, axis, [(i, (i + k) % n) for i in range(n)])]
    all_to_all x1 -> x0, starting transfers between devices: 7.48 us -> none  [per_device(): piece_col = lax.all_to_all(lead, 'row', 0, 0, tiled=True)[0]]
    all_to_all x1, waiting for transfers between devices: 5.93 us -> 0.01 us  [per_device(): got = lax.all_to_all(out, ('tp', 'col'), 0, 0, tiled=True)]
    ppermute x1, waiting for transfers between devices: 0.01 us -> 4 us  [per_device(): turned = lax.ppermute(got[:, :cols_blk], axes, turn)]
    dynamic_update_slice x7 -> x6, local copies, waits for them, and re-layouts: 3.84 us -> 0.11 us  [put(): return lax.dynamic_update_index_in_dim(out, v, lax.rem(me + n - k, n), 0)]
    all_to_all x2, waiting for transfers between devices: 26.4 us -> 23.4 us  [gather(): lax.all_to_all(jnp.broadcast_to(x[None], (n,) + x.shape), axis, 0, 0, til...]
  transfers between devices with their start and end apart: 19 -> 29, of which waited for: 9 -> 7; matrix products, arithmetic and copies ran while one was open for 15% -> 15% of each run, Pallas kernels for 7% -> 10%
where the time goes in v1:
time: 196 us; the launch traced here: 195 us
  starting transfers between devices  67 us (34%)
  waiting for transfers between devices  60.8 us (31%)
  matrix products  29.8 us (15%)
  Pallas kernels  18.7 us (10%)
  local copies, waits for them, and re-layouts  8.82 us (4%)
  other arithmetic  8.68 us (4%)
    all_to_all x2, waiting for transfers between devices, gather(): lax.all_to_all(jnp.broadcast_to(x[None], (n,) + x.shape), axis, 0, 0, til...  23.4 us
    ppermute x8, starting transfers between devices, shift(): return lax.ppermute(v, axis, [(i, (i + k) % n) for i in range(n)])  20.5 us
    pallas_call x1, Pallas kernels, inverse_factor(): pl.pallas_call(factor_kernel, out_shape=jax.ShapeDtypeStruct((PANEL, PANE...  18.7 us
    all_to_all x2, starting transfers between devices, gather(): lax.all_to_all(jnp.broadcast_to(x[None], (n,) + x.shape), axis, 0, 0, til...  15.9 us
    ppermute x3, waiting for transfers between devices, per_device(): lax.ppermute(lead[k], 'row', [(side * j, side * j + k) for j in range(sid...  15.1 us
    dot_general x4, matrix products, gram(): lax.dot_general(a, b, (((0,), (0,)), ((), ())), preferred_element_type=f32)  12.8 us
    ppermute x7, waiting for transfers between devices, per_device(): lax.ppermute(diag_piece, 'col', [(0, k)])  9.87 us
    all_to_all x1, starting transfers between devices, per_device(): got = lax.all_to_all(out, ('tp', 'col'), 0, 0, tiled=True)  7.99 us
  transfers between devices with their start and end apart: 29, of which 7 were waited for; matrix products, arithmetic and copies ran while one was open for 15% of the time, Pallas kernels for 10%

profile of v1, /device:TPU:66, one launch (start us, length us, event | category | flops | bytes accessed | tf_op | source)
XLA Modules:
  0.0 195.2 jit_solution(12476388381642034795)
XLA Ops:
  0.6 2.5 %fusion.24 = (f32[128,768]{1,0:T(8,128)}, f32[128,768]{1,0:T(8,128)}, f32[128,768]{1,0:T(8,128)S(1)}, f32[128,768]{1,0:T(8,128)S(1)}) fusion(f32[768,768]{1,0:T(8,128)} %param.9), kind=kLoop, calls=%fused_computation.66 | loop fusion | bytes 3145728 | tf_op jit(solution)/shard_map/slice | solution.py:169
  7.3 3.9 %fusion.25 = f32[1024,192]{0,1:T(8,128)S(1)} fusion(bf16[1024,2048]{1,0:T(8,128)(2,1)} %bitcast.75, bf16[2048,192]{0,1:T(8,128)(2,1)S(1)} %copy-done), kind=kOutput, calls=%fused_computation.67 | convolution fusion | flops 805306368 | bytes 5767168 | tf_op jit(solution)/shard_map/dot_general | solution.py:179
  17.0 15.1 %collective-permute-done.5 = f32[32,768]{1,0:T(8,128)S(1)} collective-permute-done((f32[32,768]{1,0:T(8,128)S(1)}, f32[32,768]{1,0:T(8,128)S(1)}, u32[]{:S(2)}, u32[]{:S(2)}) %collective-permute-start.5) | collective-permute-done | bytes 98336 | tf_op jit(solution)/shard_map/ppermute | solution.py:172
  34.0 4.0 %collective-permute-start.18 = (f32[32,512]{1,0:T(8,128)S(1)}, f32[32,512]{1,0:T(8,128)S(1)}, u32[]{:S(2)}, u32[]{:S(2)}) collective-permute-start(f32[32,512]{1,0:T(8,128)S(1)} %slice.147), channel_id=1, source_target_pairs={{0,128},{1,129},{2,130},{3,131},{4,132},{5,133},{6,134},{7,135},{8... | collective-permute-start | bytes 196616 | tf_op jit(solution)/shard_map/ppermute | solution.py:202
  41.7 8.0 %all-to-all-start = ((bf16[16,4,1280]{2,1,0:T(4,128)(2,1)}), bf16[16,4,1280]{2,1,0:T(4,128)(2,1)S(1)}, u32[]{:S(2)}, u32[]{:S(2)}) async-start(bf16[16,4,1280]{2,1,0:T(4,128)(2,1)} %copy.25), calls=%async_computation | async-start | bytes 327680 | tf_op jit(solution)/shard_map/all_to_all | solution.py:198
  53.7 9.9 %collective-permute-done.20 = f32[32,512]{1,0:T(8,128)S(1)} collective-permute-done((f32[32,512]{1,0:T(8,128)S(1)}, f32[32,512]{1,0:T(8,128)S(1)}, u32[]{:S(2)}, u32[]{:S(2)}) %collective-permute-start.20) | collective-permute-done | bytes 65568 | tf_op jit(solution)/shard_map/ppermute | solution.py:204
  63.7 4.4 %collective-permute-start.1 = (bf16[64,768]{1,0:T(8,128)(2,1)S(1)}, bf16[64,768]{1,0:T(8,128)(2,1)S(1)}, u32[]{:S(2)}, u32[]{:S(2)}) collective-permute-start(bf16[64,768]{1,0:T(8,128)(2,1)S(1)} %slice.138), channel_id=1, source_target_pairs={{0,0},{1,8},{2,16},{3,24},{4,32},{5,40},{6,48},{7,56},{128,64},{12... | collective-permute-start | bytes 294920 | tf_op jit(solution)/shard_map/ppermute | solution.py:216
  68.1 4.0 %collective-permute-done.1 = bf16[64,768]{1,0:T(8,128)(2,1)S(1)} collective-permute-done((bf16[64,768]{1,0:T(8,128)(2,1)S(1)}, bf16[64,768]{1,0:T(8,128)(2,1)S(1)}, u32[]{:S(2)}, u32[]{:S(2)}) %collective-permute-start.1) | collective-permute-done | bytes 98336 | tf_op jit(solution)/shard_map/ppermute | solution.py:216
  72.2 8.7 %collective-permute-start.9 = (bf16[128,768]{1,0:T(8,128)(2,1)S(1)}, bf16[128,768]{1,0:T(8,128)(2,1)S(1)}, u32[]{:S(2)}, u32[]{:S(2)}) collective-permute-start(bf16[128,768]{1,0:T(8,128)(2,1)S(1)} %pad_maximum_fusion.4), channel_id=1, source_target_pairs={{0,2},{1,3},{2,4},{3,5},{4,6},{5,7},{6,0},{7,1},{8,10},{9,11},{10,... | collective-permute-start | bytes 589832 | tf_op jit(solution)/shard_map/ppermute | solution.py:125
  83.1 9.0 %all-to-all-start.1 = ((bf16[16,64,1792]{2,1,0:T(8,128)(2,1)}), bf16[16,64,1792]{2,1,0:T(8,128)(2,1)}, u32[]{:S(2)}, u32[]{:S(2)}) async-start(bf16[16,64,1792]{2,1,0:T(8,128)(2,1)} %broadcast_in_dim.56), calls=%async_computation.1 | async-start | bytes 7340032 | tf_op jit(solution)/shard_map/all_to_all | solution.py:117
  92.1 4.6 %collective-permute-start.11 = (bf16[128,768]{1,0:T(8,128)(2,1)S(1)}, bf16[128,768]{1,0:T(8,128)(2,1)S(1)}, u32[]{:S(2)}, u32[]{:S(2)}) collective-permute-start(bf16[128,768]{1,0:T(8,128)(2,1)S(1)} %pad_maximum_fusion.4), channel_id=1, source_target_pairs={{0,1},{1,2},{2,3},{3,4},{4,5},{5,6},{6,7},{7,0},{8,9},{9,10},{10,1... | collective-permute-start | bytes 589832 | tf_op jit(solution)/shard_map/ppermute | solution.py:125
  97.5 3.8 %collective-permute-start.15 = (bf16[64,768]{1,0:T(8,128)(2,1)S(1)}, bf16[64,768]{1,0:T(8,128)(2,1)S(1)}, u32[]{:S(2)}, u32[]{:S(2)}) collective-permute-start(bf16[64,768]{1,0:T(8,128)(2,1)S(1)} %slice.143), channel_id=1, source_target_pairs={{0,2},{1,3},{2,4},{3,5},{4,6},{5,7},{6,0},{7,1},{8,10},{9,11},{10,... | collective-permute-start | bytes 294920 | tf_op jit(solution)/shard_map/ppermute | solution.py:125
  103.1 2.8 %collective-permute-start.13 = (bf16[128,768]{1,0:T(8,128)(2,1)S(1)}, bf16[128,768]{1,0:T(8,128)(2,1)S(1)}, u32[]{:S(2)}, u32[]{:S(2)}) collective-permute-start(bf16[128,768]{1,0:T(8,128)(2,1)S(1)} %collective-permute-done.9), channel_id=1, source_target_pairs={{0,1},{1,2},{2,3},{3,4},{4,5},{5,6},{6,7},{7,0},{8,9},{9,10},{10,1... | collective-permute-start | bytes 589832 | tf_op jit(solution)/shard_map/ppermute | solution.py:125
  106.0 3.1 %collective-permute-done.13 = bf16[128,768]{1,0:T(8,128)(2,1)S(1)} collective-permute-done((bf16[128,768]{1,0:T(8,128)(2,1)S(1)}, bf16[128,768]{1,0:T(8,128)(2,1)S(1)}, u32[]{:S(2)}, u32[]{:S(2)}) %collective-permute-start.13) | collective-permute-done | bytes 196640 | tf_op jit(solution)/shard_map/ppermute | solution.py:125
  109.3 3.5 %collective-permute-done.17 = bf16[8,128,768]{2,1,0:T(8,128)(2,1)} collective-permute-done((bf16[8,128,768]{2,1,0:T(8,128)(2,1)S(1)}, bf16[8,128,768]{2,1,0:T(8,128)(2,1)}, u32[]{:S(2)}, u32[]{:S(2)}) %collective-permute-start.17) | collective-permute-done | bytes 1572896 | tf_op jit(solution)/shard_map/ppermute | solution.py:221
  118.1 23.4 %all-to-all-done.1 = bf16[16,64,1792]{2,1,0:T(8,128)(2,1)} async-done(((bf16[16,64,1792]{2,1,0:T(8,128)(2,1)}), bf16[16,64,1792]{2,1,0:T(8,128)(2,1)}, u32[]{:S(2)}, u32[]{:S(2)}) %all-to-all-start.1) | async-done | bytes 3670048 | tf_op jit(solution)/shard_map/all_to_all | solution.py:117
  142.9 6.9 %all-to-all-start.2 = ((f32[16,32,768]{2,1,0:T(8,128)}), f32[16,32,768]{2,1,0:T(8,128)S(1)}, u32[]{:S(2)}, u32[]{:S(2)}) async-start(f32[16,32,768]{2,1,0:T(8,128)} %broadcast_in_dim.57), calls=%async_computation.2 | async-start | bytes 3145728 | tf_op jit(solution)/shard_map/all_to_all | solution.py:117
  151.5 2.3 %convolution_add_fusion.a_ref = f32[512,512]{1,0:T(8,128)S(1)} fusion(f32[512,512]{1,0:T(8,128)S(1)} %bitcast.67, bf16[1024,1792]{1,0:T(8,128)(2,1)} %bitcast.21), kind=kOutput, calls=%fused_computation.13 | convolution fusion | flops 537133056 | bytes 3145728 | tf_op jit(solution)/shard_map/dot_general | solution.py:144
  153.9 18.7 %inverse_factor.1 = f32[512,512]{1,0:T(8,128)S(1)} custom-call(f32[512,512]{1,0:T(8,128)S(1)} %convolution_add_fusion.a_ref), custom_call_target="tpu_custom_call" | custom-call | tf_op jit(solution)/shard_map/inverse_factor/pallas_call | solution.py:96
  172.6 3.4 %fusion.10 = f32[512,768]{1,0:T(8,128)} fusion(bf16[512,768]{1,0:T(8,128)(2,1)S(1)} %bitcast.68, bf16[512,768]{1,0:T(8,128)(2,1)S(1)} %bitcast.70, bf16[1024,1792]{1,0:T(8,128)(2,1)} %bitcast.21), kind=kOutput, calls=%fused_computation.20 | convolution fusion | flops 808452096 | bytes 4194304 | tf_op jit(solution)/shard_map/dot_general | solution.py:144
  176.0 4.3 %fusion.5 = f32[768,768]{1,0:T(8,128)} fusion(bf16[1024,1792]{1,0:T(8,128)(2,1)} %bitcast.21, bf16[512,768]{1,0:T(8,128)(2,1)S(1)} %bitcast.69, bf16[512,768]{1,0:T(8,128)(2,1)S(1)} %bitcast.71), kind=kOutput, calls=%fused_computation.11 | convolution fusion | flops 1211105280 | bytes 5505024 | tf_op jit(solution)/shard_map/dot_general | solution.py:144
  180.3 2.8 %bitcast_add_fusion = f32[512,768]{1,0:T(8,128)S(1)} fusion(f32[16,32,768]{2,1,0:T(8,128)S(1)} %all-to-all-done.2, bf16[1024,1792]{1,0:T(8,128)(2,1)} %bitcast.21), kind=kOutput, calls=%fused_computation.6 | convolution fusion | flops 805699584 | bytes 5767168 | tf_op jit(solution)/shard_map/dot_general | solution.py:144
  183.1 2.7 %fusion.27 = f32[512,768]{1,0:T(8,128)} fusion(f32[512,512]{1,0:T(8,128)S(1)} %inverse_factor.1, f32[512,768]{1,0:T(8,128)S(1)} %bitcast_add_fusion), kind=kOutput, calls=%fused_computation.69 | convolution fusion | flops 1207959552 | bytes 4194304 | tf_op jit(solution)/shard_map/dot_general | solution.py:232
  188.6 6.6 %add_subtract_fusion = f32[768,768]{1,0:T(8,128)} fusion(f32[768,768]{1,0:T(8,128)} %param.9, f32[768,768]{1,0:T(8,128)} %fusion.5, f32[512,768]{1,0:T(8,128)S(1)} %fusion, f32[512,768]{1,0:T(8,128)} %fusion.27), kind=kOutput, calls=%fused_computation | convolution fusion | flops 1813118976 | bytes 10223616 | tf_op jit(solution)/shard_map/dot_general | solution.py:236
  (105 shorter events, 35.5 us)
Async XLA Ops:
  3.1 9.8 %collective-permute-start.2 = (f32[4,32,768]{2,1,0:T(8,128)}, f32[4,32,768]{2,1,0:T(8,128)}, u32[]{:S(2)}, u32[]{:S(2)}) collective-permute-start(f32[4,32,768]{2,1,0:T(8,128)} %bitcast.4), channel_id=1, source_target_pairs={{0,32},{1,33},{2,34},{3,35},{4,36},{5,37},{6,38},{7,39},{128,160},... | collective-permute-start | bytes 1179656 | tf_op jit(solution)/shard_map/ppermute | solution.py:169
  4.5 8.4 %collective-permute-start.3 = (f32[4,32,768]{2,1,0:T(8,128)}, f32[4,32,768]{2,1,0:T(8,128)}, u32[]{:S(2)}, u32[]{:S(2)}) collective-permute-start(f32[4,32,768]{2,1,0:T(8,128)} %bitcast.5), channel_id=1, source_target_pairs={{0,64},{1,65},{2,66},{3,67},{4,68},{5,69},{6,70},{7,71},{128,192},... | collective-permute-start | bytes 1179656 | tf_op jit(solution)/shard_map/ppermute | solution.py:169
  5.9 7.0 %collective-permute-start.4 = (f32[4,32,768]{2,1,0:T(8,128)S(1)}, f32[4,32,768]{2,1,0:T(8,128)}, u32[]{:S(2)}, u32[]{:S(2)}) collective-permute-start(f32[4,32,768]{2,1,0:T(8,128)S(1)} %bitcast.73), channel_id=1, source_target_pairs={{0,96},{1,97},{2,98},{3,99},{4,100},{5,101},{6,102},{7,103},{128,2... | collective-permute-start | bytes 1179656 | tf_op jit(solution)/shard_map/ppermute | solution.py:169
  12.8 25.2 %collective-permute-start = (f32[4,128,256]{1,2,0:T(8,128)S(1)}, f32[4,128,256]{1,2,0:T(8,128)S(1)}, u32[]{:S(2)}, u32[]{:S(2)}) collective-permute-start(f32[4,128,256]{1,2,0:T(8,128)S(1)} %bitcast.72), channel_id=1, source_target_pairs={{0,128},{128,0},{1,129},{129,1},{2,130},{130,2},{3,131},{131,3},{4... | collective-permute-start | bytes 1572872 | tf_op jit(solution)/shard_map/ppermute | solution.py:186
  15.6 16.4 %collective-permute-start.5 = (f32[32,768]{1,0:T(8,128)S(1)}, f32[32,768]{1,0:T(8,128)S(1)}, u32[]{:S(2)}, u32[]{:S(2)}) collective-permute-start(f32[32,768]{1,0:T(8,128)S(1)} %get-tuple-element.26), channel_id=1, source_target_pairs={{0,8},{32,40},{64,72},{96,104},{1,9},{33,41},{65,73},{97,105},{2,1... | collective-permute-start | bytes 294920 | tf_op jit(solution)/shard_map/ppermute | solution.py:172
  32.1 18.9 %collective-permute-start.8 = (f32[32,768]{1,0:T(8,128)S(1)}, f32[32,768]{1,0:T(8,128)S(1)}, u32[]{:S(2)}, u32[]{:S(2)}) collective-permute-start(f32[32,768]{1,0:T(8,128)S(1)} %fusion.19), channel_id=1, source_target_pairs={{0,0},{1,8},{2,16},{3,24},{4,32},{5,40},{6,48},{7,56},{128,64},{12... | collective-permute-start | bytes 294920 | tf_op jit(solution)/shard_map/ppermute | solution.py:215
  34.0 5.5 %collective-permute-start.18 = (f32[32,512]{1,0:T(8,128)S(1)}, f32[32,512]{1,0:T(8,128)S(1)}, u32[]{:S(2)}, u32[]{:S(2)}) collective-permute-start(f32[32,512]{1,0:T(8,128)S(1)} %slice.147), channel_id=1, source_target_pairs={{0,128},{1,129},{2,130},{3,131},{4,132},{5,133},{6,134},{7,135},{8... | collective-permute-start | bytes 196616 | tf_op jit(solution)/shard_map/ppermute | solution.py:202
  39.5 12.1 %collective-permute-start.25 = (f32[32,512]{1,0:T(8,128)S(1)}, f32[32,512]{1,0:T(8,128)S(1)}, u32[]{:S(2)}, u32[]{:S(2)}) collective-permute-start(f32[32,512]{1,0:T(8,128)S(1)} %broadcast_select_fusion.2), channel_id=1, source_target_pairs={{0,7},{8,15},{16,23},{24,31},{32,39},{40,47},{48,55},{56,63},{64,7... | collective-permute-start | bytes 196616 | tf_op jit(solution)/shard_map/ppermute | solution.py:204
  40.2 12.8 %collective-permute-start.24 = (f32[32,512]{1,0:T(8,128)S(1)}, f32[32,512]{1,0:T(8,128)S(1)}, u32[]{:S(2)}, u32[]{:S(2)}) collective-permute-start(f32[32,512]{1,0:T(8,128)S(1)} %broadcast_select_fusion.2), channel_id=1, source_target_pairs={{0,6},{8,14},{16,22},{24,30},{32,38},{40,46},{48,54},{56,62},{64,7... | collective-permute-start | bytes 196616 | tf_op jit(solution)/shard_map/ppermute | solution.py:204
  41.7 22.0 %all-to-all-start = ((bf16[16,4,1280]{2,1,0:T(4,128)(2,1)}), bf16[16,4,1280]{2,1,0:T(4,128)(2,1)S(1)}, u32[]{:S(2)}, u32[]{:S(2)}) async-start(bf16[16,4,1280]{2,1,0:T(4,128)(2,1)} %copy.25), calls=%async_computation | async-start | bytes 327680 | tf_op jit(solution)/shard_map/all_to_all | solution.py:198
  49.7 4.0 %collective-permute-start.23 = (f32[32,512]{1,0:T(8,128)S(1)}, f32[32,512]{1,0:T(8,128)S(1)}, u32[]{:S(2)}, u32[]{:S(2)}) collective-permute-start(f32[32,512]{1,0:T(8,128)S(1)} %broadcast_select_fusion.2), channel_id=1, source_target_pairs={{0,5},{8,13},{16,21},{24,29},{32,37},{40,45},{48,53},{56,61},{64,6... | collective-permute-start | bytes 196616 | tf_op jit(solution)/shard_map/ppermute | solution.py:204
  51.7 11.9 %collective-permute-start.20 = (f32[32,512]{1,0:T(8,128)S(1)}, f32[32,512]{1,0:T(8,128)S(1)}, u32[]{:S(2)}, u32[]{:S(2)}) collective-permute-start(f32[32,512]{1,0:T(8,128)S(1)} %broadcast_select_fusion.2), channel_id=1, source_target_pairs={{0,2},{8,10},{16,18},{24,26},{32,34},{40,42},{48,50},{56,58},{64,6... | collective-permute-start | bytes 196616 | tf_op jit(solution)/shard_map/ppermute | solution.py:204
  53.0 10.6 %collective-permute-start.19 = (f32[32,512]{1,0:T(8,128)S(1)}, f32[32,512]{1,0:T(8,128)S(1)}, u32[]{:S(2)}, u32[]{:S(2)}) collective-permute-start(f32[32,512]{1,0:T(8,128)S(1)} %broadcast_select_fusion.2), channel_id=1, source_target_pairs={{0,1},{8,9},{16,17},{24,25},{32,33},{40,41},{48,49},{56,57},{64,65... | collective-permute-start | bytes 196616 | tf_op jit(solution)/shard_map/ppermute | solution.py:204
  63.7 8.4 %collective-permute-start.1 = (bf16[64,768]{1,0:T(8,128)(2,1)S(1)}, bf16[64,768]{1,0:T(8,128)(2,1)S(1)}, u32[]{:S(2)}, u32[]{:S(2)}) collective-permute-start(bf16[64,768]{1,0:T(8,128)(2,1)S(1)} %slice.138), channel_id=1, source_target_pairs={{0,0},{1,8},{2,16},{3,24},{4,32},{5,40},{6,48},{7,56},{128,64},{12... | collective-permute-start | bytes 294920 | tf_op jit(solution)/shard_map/ppermute | solution.py:216
  72.1 24.8 %collective-permute-start.10 = (bf16[128,768]{1,0:T(8,128)(2,1)S(1)}, bf16[128,768]{1,0:T(8,128)(2,1)S(1)}, u32[]{:S(2)}, u32[]{:S(2)}) collective-permute-start(bf16[128,768]{1,0:T(8,128)(2,1)S(1)} %pad_maximum_fusion.4), channel_id=1, source_target_pairs={{0,6},{1,7},{2,0},{3,1},{4,2},{5,3},{6,4},{7,5},{8,14},{9,15},{10,... | collective-permute-start | bytes 589832 | tf_op jit(solution)/shard_map/ppermute | solution.py:125
  72.2 25.3 %collective-permute-start.9 = (bf16[128,768]{1,0:T(8,128)(2,1)S(1)}, bf16[128,768]{1,0:T(8,128)(2,1)S(1)}, u32[]{:S(2)}, u32[]{:S(2)}) collective-permute-start(bf16[128,768]{1,0:T(8,128)(2,1)S(1)} %pad_maximum_fusion.4), channel_id=1, source_target_pairs={{0,2},{1,3},{2,4},{3,5},{4,6},{5,7},{6,0},{7,1},{8,10},{9,11},{10,... | collective-permute-start | bytes 589832 | tf_op jit(solution)/shard_map/ppermute | solution.py:125
  83.1 58.4 %all-to-all-start.1 = ((bf16[16,64,1792]{2,1,0:T(8,128)(2,1)}), bf16[16,64,1792]{2,1,0:T(8,128)(2,1)}, u32[]{:S(2)}, u32[]{:S(2)}) async-start(bf16[16,64,1792]{2,1,0:T(8,128)(2,1)} %broadcast_in_dim.56), calls=%async_computation.1 | async-start | bytes 7340032 | tf_op jit(solution)/shard_map/all_to_all | solution.py:117
  92.1 11.0 %collective-permute-start.11 = (bf16[128,768]{1,0:T(8,128)(2,1)S(1)}, bf16[128,768]{1,0:T(8,128)(2,1)S(1)}, u32[]{:S(2)}, u32[]{:S(2)}) collective-permute-start(bf16[128,768]{1,0:T(8,128)(2,1)S(1)} %pad_maximum_fusion.4), channel_id=1, source_target_pairs={{0,1},{1,2},{2,3},{3,4},{4,5},{5,6},{6,7},{7,0},{8,9},{9,10},{10,1... | collective-permute-start | bytes 589832 | tf_op jit(solution)/shard_map/ppermute | solution.py:125
  96.8 9.2 %collective-permute-start.12 = (bf16[128,768]{1,0:T(8,128)(2,1)S(1)}, bf16[128,768]{1,0:T(8,128)(2,1)S(1)}, u32[]{:S(2)}, u32[]{:S(2)}) collective-permute-start(bf16[128,768]{1,0:T(8,128)(2,1)S(1)} %pad_maximum_fusion.4), channel_id=1, source_target_pairs={{0,7},{1,0},{2,1},{3,2},{4,3},{5,4},{6,5},{7,6},{8,15},{9,8},{10,9... | collective-permute-start | bytes 589832 | tf_op jit(solution)/shard_map/ppermute | solution.py:125
  96.9 12.2 %collective-permute-start.16 = (bf16[64,768]{1,0:T(8,128)(2,1)S(1)}, bf16[64,768]{1,0:T(8,128)(2,1)S(1)}, u32[]{:S(2)}, u32[]{:S(2)}) collective-permute-start(bf16[64,768]{1,0:T(8,128)(2,1)S(1)} %slice.144), channel_id=1, source_target_pairs={{0,6},{1,7},{2,0},{3,1},{4,2},{5,3},{6,4},{7,5},{8,14},{9,15},{10,... | collective-permute-start | bytes 294920 | tf_op jit(solution)/shard_map/ppermute | solution.py:125
  97.5 11.7 %collective-permute-start.15 = (bf16[64,768]{1,0:T(8,128)(2,1)S(1)}, bf16[64,768]{1,0:T(8,128)(2,1)S(1)}, u32[]{:S(2)}, u32[]{:S(2)}) collective-permute-start(bf16[64,768]{1,0:T(8,128)(2,1)S(1)} %slice.143), channel_id=1, source_target_pairs={{0,2},{1,3},{2,4},{3,5},{4,6},{5,7},{6,0},{7,1},{8,10},{9,11},{10,... | collective-permute-start | bytes 294920 | tf_op jit(solution)/shard_map/ppermute | solution.py:125
  101.2 7.9 %collective-permute-start.14 = (bf16[128,768]{1,0:T(8,128)(2,1)S(1)}, bf16[128,768]{1,0:T(8,128)(2,1)S(1)}, u32[]{:S(2)}, u32[]{:S(2)}) collective-permute-start(bf16[128,768]{1,0:T(8,128)(2,1)S(1)} %collective-permute-done.10), channel_id=1, source_target_pairs={{0,7},{1,0},{2,1},{3,2},{4,3},{5,4},{6,5},{7,6},{8,15},{9,8},{10,9... | collective-permute-start | bytes 589832 | tf_op jit(solution)/shard_map/ppermute | solution.py:125
  103.1 6.0 %collective-permute-start.13 = (bf16[128,768]{1,0:T(8,128)(2,1)S(1)}, bf16[128,768]{1,0:T(8,128)(2,1)S(1)}, u32[]{:S(2)}, u32[]{:S(2)}) collective-permute-start(bf16[128,768]{1,0:T(8,128)(2,1)S(1)} %collective-permute-done.9), channel_id=1, source_target_pairs={{0,1},{1,2},{2,3},{3,4},{4,5},{5,6},{6,7},{7,0},{8,9},{9,10},{10,1... | collective-permute-start | bytes 589832 | tf_op jit(solution)/shard_map/ppermute | solution.py:125
  142.9 37.4 %all-to-all-start.2 = ((f32[16,32,768]{2,1,0:T(8,128)}), f32[16,32,768]{2,1,0:T(8,128)S(1)}, u32[]{:S(2)}, u32[]{:S(2)}) async-start(f32[16,32,768]{2,1,0:T(8,128)} %broadcast_in_dim.57), calls=%async_computation.2 | async-start | bytes 3145728 | tf_op jit(solution)/shard_map/all_to_all | solution.py:117
  (13 other events, 74.6 us)

commit v2 on v1

--- a/solution.py
+++ b/solution.py
@@ -146,7 +146,7 @@
 
 def per_device(acts, grads, proj_in, proj_out, curvature):
     tp_n, row_n, col_n = (lax.axis_size(a) for a in ("tp", "row", "col"))
-    tp, col = lax.axis_index("tp"), lax.axis_index("col")
+    tp = lax.axis_index("tp")
     ex_dev, seq_len, width = acts.shape
     rows_blk, cols_blk = curvature.shape
     act_width, grad_width = proj_in.shape[1], proj_out.shape[1]
@@ -166,8 +166,8 @@
     side = int(row_n**0.5)
     lead = curvature[:PANEL].reshape(side, side, piece, cols_blk)
     row = lax.axis_index("row")
-    got = sum(lax.ppermute(lead[k], "row", [(0, side * k)]) for k in range(1, side))
-    lead = jnp.where(row == 0, lead[0], got)
+    got = [lax.ppermute(lead[k], "row", [(0, side * k)]) for k in range(1, side)]
+    lead = jnp.where(row == 0, lead[0], sum(got))
     got = sum(
         lax.ppermute(lead[k], "row", [(side * j, side * j + k) for j in range(side)])
         for k in range(1, side)
@@ -198,34 +198,48 @@
     got = lax.all_to_all(out, ("tp", "col"), 0, 0, tiled=True)
     got = got.reshape(blocks * ex, cols_blk + PANEL)
 
-    diag_piece = piece_col[:, :PANEL]
-    got_diag = lax.ppermute(diag_piece, "tp", [(0, 1)])
-    diag_piece = jnp.where(first, diag_piece, got_diag)
-    got_diag = sum(lax.ppermute(diag_piece, "col", [(0, k)]) for k in range(1, col_n))
-    diag_piece = jnp.where(col == 0, diag_piece, got_diag)
-
     n_ex = got.shape[0]
-    sent = jnp.concatenate([got, jnp.concatenate(wire_halves(diag_piece), axis=0)], axis=1)
-    col_all = gather(sent, "row")
-    diag = col_all[:, :, cols_blk + PANEL :].astype(f32)
-    diag = (diag[:, :piece] + diag[:, piece:]).reshape(PANEL, PANEL)
-    col_all = col_all.reshape(row_n * n_ex, -1)
-    col_feats, lead_feats = col_all[:, :cols_blk], col_all[:, cols_blk : cols_blk + PANEL]
+    col_all = gather(got, "row").reshape(row_n * n_ex, -1)
+    col_all, lead_piece = lax.optimization_barrier((col_all, piece_col))
+    col_feats, lead_feats = col_all[:, :cols_blk], col_all[:, cols_blk:]
 
     piece_row = lax.ppermute(piece_col, axes, turn)
+    diag = piece_row[:, :PANEL]
+    got_diag = sum(
+        lax.ppermute(diag, "row", [(0, side * k)]) for k in range(1, side)
+    )
+    diag = jnp.where(row == 0, diag, got_diag)
+    got_diag = sum(
+        lax.ppermute(diag, "row", [(side * j, side * j + k) for j in range(side)])
+        for k in range(1, side)
+    )
+    diag = jnp.where(lax.rem(row, side) == 0, diag, got_diag)
+    cut = rows_blk // 3
+    packed = [v[:, i : i + cut] for v in wire_halves(diag) for i in range(0, PANEL, cut)]
+    packed = jnp.concatenate(packed, axis=0)
+    group = 16 * (-(-packed.shape[0] // 48))
+    packed = jnp.pad(packed, ((0, 3 * group - packed.shape[0]), (0, 0)))
+    packed = jnp.concatenate([packed[i * group : (i + 1) * group] for i in range(3)], axis=1)
+
     turned = lax.ppermute(got[:, :cols_blk], axes, turn)
-    mine = jnp.concatenate([turned, *wire_halves(piece_row)], axis=0)
+    mine = jnp.concatenate([turned, *wire_halves(piece_row), packed], axis=0)
     mine = gather_ring(mine, "col")
-    lead_col = gather(piece_col, "row").reshape(-1, cols_blk)
+    lead_col = gather(lead_piece, "row").reshape(-1, cols_blk)
 
     theirs = lax.ppermute(mine, "tp", swap)
     low, high = jnp.where(first, mine, theirs), jnp.where(first, theirs, mine)
-    row_feats, lead_row = [], []
+    row_feats, lead_row, diag = [], [], []
     for x in (low, high):
         row_feats.append(x[:, :n_ex].reshape(-1, rows_blk))
-        x = x[:, n_ex:].astype(f32)
-        lead_row.append((x[:, :piece] + x[:, piece:]).reshape(-1, rows_blk))
-    row_feats, lead_row = jnp.concatenate(row_feats), jnp.concatenate(lead_row)
+        c = x[:, n_ex : n_ex + 2 * piece].astype(f32)
+        lead_row.append((c[:, :piece] + c[:, piece:]).reshape(-1, rows_blk))
+        d = x[:, n_ex + 2 * piece :]
+        d = jnp.concatenate([d[:, :, i * cut : (i + 1) * cut] for i in range(3)], axis=1)
+        d = d[:, : 2 * piece * PANEL // cut].astype(f32)
+        d = d[:, : d.shape[1] // 2] + d[:, d.shape[1] // 2 :]
+        d = jnp.concatenate([d[:, i : i + piece] for i in range(0, d.shape[1], piece)], axis=2)
+        diag.append(d.reshape(-1, PANEL))
+    row_feats, lead_row, diag = (jnp.concatenate(v) for v in (row_feats, lead_row, diag))
 
     inv = inverse_factor(diag + gram(lead_feats, lead_feats))
     panel_row = jnp.dot(inv, lead_row + gram(lead_feats, row_feats), precision=HIGH)

time: 196 us -> 189 us (0.964)
  the two profiles are of different devices: /device:TPU:66 before, /device:TPU:1 now
where the time goes in v2:
time: 189 us; the launch traced here: 188 us
  starting transfers between devices  86 us (46%)
  waiting for transfers between devices  43.5 us (23%)
  matrix products  25.9 us (14%)
  Pallas kernels  18.7 us (10%)
  local copies, waits for them, and re-layouts  7.9 us (4%)
  other arithmetic  4.52 us (2%)
    ppermute x8, starting transfers between devices, shift(): return lax.ppermute(v, axis, [(i, (i + k) % n) for i in range(n)])  24.5 us
    pallas_call x1, Pallas kernels, inverse_factor(): pl.pallas_call(factor_kernel, out_shape=jax.ShapeDtypeStruct((PANEL, PANE...  18.7 us
    ppermute x8, waiting for transfers between devices, shift(): return lax.ppermute(v, axis, [(i, (i + k) % n) for i in range(n)])  17.8 us
    all_to_all x1, starting transfers between devices, per_device(): got = lax.all_to_all(out, ('tp', 'col'), 0, 0, tiled=True)  13.5 us
    dot_general x4, matrix products, gram(): lax.dot_general(a, b, (((0,), (0,)), ((), ())), preferred_element_type=f32)  12.7 us
    all_to_all x2, waiting for transfers between devices, gather(): lax.all_to_all(jnp.broadcast_to(x[None], (n,) + x.shape), axis, 0, 0, til...  10.3 us
    ppermute x3, starting transfers between devices, per_device(): lax.ppermute(lead[k], 'row', [(0, side * k)])  9.85 us
    ppermute x3, starting transfers between devices, per_device(): lax.ppermute(diag, 'row', [(0, side * k)])  9.73 us
  transfers between devices with their start and end apart: 27, of which 12 were waited for; matrix products, arithmetic and copies ran while one was open for 15% of the time, Pallas kernels for 10%

profile of v2, /device:TPU:1, one launch (start us, length us, event | category | flops | bytes accessed | tf_op | source)
XLA Modules:
  0.0 187.9 jit_solution(4643249636158436037)
XLA Ops:
  2.2 4.8 %collective-permute-start.2 = (f32[4,32,768]{2,1,0:T(8,128)S(1)}, f32[4,32,768]{2,1,0:T(8,128)}, u32[]{:S(2)}, u32[]{:S(2)}) collective-permute-start(f32[4,32,768]{2,1,0:T(8,128)S(1)} %bitcast.77), channel_id=1, source_target_pairs={{0,32},{1,33},{2,34},{3,35},{4,36},{5,37},{6,38},{7,39},{128,160},... | collective-permute-start | bytes 1179656 | tf_op jit(solution)/shard_map/ppermute | solution.py:169
  7.0 3.0 %collective-permute-start.3 = (f32[4,32,768]{2,1,0:T(8,128)S(1)}, f32[4,32,768]{2,1,0:T(8,128)}, u32[]{:S(2)}, u32[]{:S(2)}) collective-permute-start(f32[4,32,768]{2,1,0:T(8,128)S(1)} %bitcast.76), channel_id=1, source_target_pairs={{0,64},{1,65},{2,66},{3,67},{4,68},{5,69},{6,70},{7,71},{128,192},... | collective-permute-start | bytes 1179656 | tf_op jit(solution)/shard_map/ppermute | solution.py:169
  12.1 3.9 %fusion.45 = f32[1024,192]{0,1:T(8,128)S(1)} fusion(bf16[1024,2048]{1,0:T(8,128)(2,1)} %bitcast.79, bf16[2048,192]{0,1:T(8,128)(2,1)S(1)} %copy-done), kind=kOutput, calls=%fused_computation.98 | convolution fusion | flops 805306368 | bytes 5767168 | tf_op jit(solution)/shard_map/dot_general | solution.py:179
  18.5 3.9 %collective-permute-done.3 = f32[4,32,768]{2,1,0:T(8,128)} collective-permute-done((f32[4,32,768]{2,1,0:T(8,128)S(1)}, f32[4,32,768]{2,1,0:T(8,128)}, u32[]{:S(2)}, u32[]{:S(2)}) %collective-permute-start.3) | collective-permute-done | bytes 393248 | tf_op jit(solution)/shard_map/ppermute | solution.py:169
  29.4 7.6 %collective-permute-start.8 = (f32[32,768]{1,0:T(8,128)S(1)}, f32[32,768]{1,0:T(8,128)S(1)}, u32[]{:S(2)}, u32[]{:S(2)}) collective-permute-start(f32[32,768]{1,0:T(8,128)S(1)} %fusion.26), channel_id=1, source_target_pairs={{0,0},{1,8},{2,16},{3,24},{4,32},{5,40},{6,48},{7,56},{128,64},{12... | collective-permute-start | bytes 294920 | tf_op jit(solution)/shard_map/ppermute | solution.py:206
  39.3 6.9 %collective-permute-start.11 = (f32[32,512]{1,0:T(8,128)S(1)}, f32[32,512]{1,0:T(8,128)S(1)}, u32[]{:S(2)}, u32[]{:S(2)}) collective-permute-start(f32[32,512]{1,0:T(8,128)S(1)} %slice.235), channel_id=1, source_target_pairs={{0,96},{1,97},{2,98},{3,99},{4,100},{5,101},{6,102},{7,103},{128,2... | collective-permute-start | bytes 196616 | tf_op jit(solution)/shard_map/ppermute | solution.py:209
  49.9 13.5 %all-to-all-start = ((bf16[16,4,1280]{2,1,0:T(4,128)(2,1)}), bf16[16,4,1280]{2,1,0:T(4,128)(2,1)S(1)}, u32[]{:S(2)}, u32[]{:S(2)}) async-start(bf16[16,4,1280]{2,1,0:T(4,128)(2,1)} %copy.25), calls=%async_computation | async-start | bytes 327680 | tf_op jit(solution)/shard_map/all_to_all | solution.py:198
  71.3 2.2 %collective-permute-start.1 = (bf16[64,768]{1,0:T(8,128)(2,1)S(1)}, bf16[64,768]{1,0:T(8,128)(2,1)S(1)}, u32[]{:S(2)}, u32[]{:S(2)}) collective-permute-start(bf16[64,768]{1,0:T(8,128)(2,1)S(1)} %slice.230), channel_id=1, source_target_pairs={{0,0},{1,8},{2,16},{3,24},{4,32},{5,40},{6,48},{7,56},{128,64},{12... | collective-permute-start | bytes 294920 | tf_op jit(solution)/shard_map/ppermute | solution.py:224
  73.6 5.2 %collective-permute-done.1 = bf16[64,768]{1,0:T(8,128)(2,1)S(1)} collective-permute-done((bf16[64,768]{1,0:T(8,128)(2,1)S(1)}, bf16[64,768]{1,0:T(8,128)(2,1)S(1)}, u32[]{:S(2)}, u32[]{:S(2)}) %collective-permute-start.1) | collective-permute-done | bytes 98336 | tf_op jit(solution)/shard_map/ppermute | solution.py:224
  78.8 15.1 %collective-permute-start.16 = (bf16[176,768]{1,0:T(8,128)(2,1)S(1)}, bf16[176,768]{1,0:T(8,128)(2,1)S(1)}, u32[]{:S(2)}, u32[]{:S(2)}) collective-permute-start(bf16[176,768]{1,0:T(8,128)(2,1)S(1)} %fusion.22), channel_id=1, source_target_pairs={{0,6},{1,7},{2,0},{3,1},{4,2},{5,3},{6,4},{7,5},{8,14},{9,15},{10,... | collective-permute-start | bytes 811016 | tf_op jit(solution)/shard_map/ppermute | solution.py:125
  95.7 4.5 %all-to-all-start.1 = ((bf16[16,64,1280]{2,1,0:T(8,128)(2,1)}), bf16[16,64,1280]{2,1,0:T(8,128)(2,1)}, u32[]{:S(2)}, u32[]{:S(2)}) async-start(bf16[16,64,1280]{2,1,0:T(8,128)(2,1)} %broadcast_in_dim.55), calls=%async_computation.1 | async-start | bytes 5242880 | tf_op jit(solution)/shard_map/all_to_all | solution.py:117
  102.0 2.5 %collective-permute-start.18 = (bf16[176,768]{1,0:T(8,128)(2,1)S(1)}, bf16[176,768]{1,0:T(8,128)(2,1)S(1)}, u32[]{:S(2)}, u32[]{:S(2)}) collective-permute-start(bf16[176,768]{1,0:T(8,128)(2,1)S(1)} %fusion.22), channel_id=1, source_target_pairs={{0,7},{1,0},{2,1},{3,2},{4,3},{5,4},{6,5},{7,6},{8,15},{9,8},{10,9... | collective-permute-start | bytes 811016 | tf_op jit(solution)/shard_map/ppermute | solution.py:125
  105.9 2.7 %collective-permute-done.15 = bf16[176,768]{1,0:T(8,128)(2,1)S(1)} collective-permute-done((bf16[176,768]{1,0:T(8,128)(2,1)S(1)}, bf16[176,768]{1,0:T(8,128)(2,1)S(1)}, u32[]{:S(2)}, u32[]{:S(2)}) %collective-permute-start.15) | collective-permute-done | bytes 270368 | tf_op jit(solution)/shard_map/ppermute | solution.py:125
  108.7 3.8 %collective-permute-start.20 = (bf16[176,768]{1,0:T(8,128)(2,1)S(1)}, bf16[176,768]{1,0:T(8,128)(2,1)S(1)}, u32[]{:S(2)}, u32[]{:S(2)}) collective-permute-start(bf16[176,768]{1,0:T(8,128)(2,1)S(1)} %collective-permute-done.16), channel_id=1, source_target_pairs={{0,7},{1,0},{2,1},{3,2},{4,3},{5,4},{6,5},{7,6},{8,15},{9,8},{10,9... | collective-permute-start | bytes 811016 | tf_op jit(solution)/shard_map/ppermute | solution.py:125
  112.5 4.8 %collective-permute-done.17 = bf16[176,768]{1,0:T(8,128)(2,1)S(1)} collective-permute-done((bf16[176,768]{1,0:T(8,128)(2,1)S(1)}, bf16[176,768]{1,0:T(8,128)(2,1)S(1)}, u32[]{:S(2)}, u32[]{:S(2)}) %collective-permute-start.17) | collective-permute-done | bytes 270368 | tf_op jit(solution)/shard_map/ppermute | solution.py:125
  117.5 10.3 %collective-permute-done.19 = bf16[176,768]{1,0:T(8,128)(2,1)S(1)} collective-permute-done((bf16[176,768]{1,0:T(8,128)(2,1)S(1)}, bf16[176,768]{1,0:T(8,128)(2,1)S(1)}, u32[]{:S(2)}, u32[]{:S(2)}) %collective-permute-start.19) | collective-permute-done | bytes 270368 | tf_op jit(solution)/shard_map/ppermute | solution.py:125
  128.7 10.3 %all-to-all-done.1 = bf16[16,64,1280]{2,1,0:T(8,128)(2,1)} async-done(((bf16[16,64,1280]{2,1,0:T(8,128)(2,1)}), bf16[16,64,1280]{2,1,0:T(8,128)(2,1)}, u32[]{:S(2)}, u32[]{:S(2)}) %all-to-all-start.1) | async-done | bytes 2621472 | tf_op jit(solution)/shard_map/all_to_all | solution.py:117
  140.4 4.4 %all-to-all-start.2 = ((f32[16,32,768]{2,1,0:T(8,128)}), f32[16,32,768]{2,1,0:T(8,128)}, u32[]{:S(2)}, u32[]{:S(2)}) async-start(f32[16,32,768]{2,1,0:T(8,128)} %broadcast_in_dim.56), calls=%async_computation.2 | async-start | bytes 3145728 | tf_op jit(solution)/shard_map/all_to_all | solution.py:117
  147.8 2.3 %convolution_add_fusion.a_ref = f32[512,512]{1,0:T(8,128)S(1)} fusion(f32[256,512]{1,0:T(8,128)S(1)} %bitcast.74, f32[256,512]{1,0:T(8,128)S(1)} %bitcast.73, bf16[1024,1280]{1,0:T(8,128)(2,1)} %bitcast.21), kind=kOutput, calls=%fused_computation.12 | convolution fusion | flops 537395200 | bytes 3145728 | tf_op jit(solution)/shard_map/dot_general | solution.py:144
  150.2 18.7 %inverse_factor.1 = f32[512,512]{1,0:T(8,128)S(1)} custom-call(f32[512,512]{1,0:T(8,128)S(1)} %convolution_add_fusion.a_ref), custom_call_target="tpu_custom_call" | custom-call | tf_op jit(solution)/shard_map/inverse_factor/pallas_call | solution.py:96
  169.0 2.3 %fusion.7 = f32[512,768]{1,0:T(8,128)S(1)} fusion(bf16[512,768]{1,0:T(8,128)(2,1)S(1)} %bitcast.70, bf16[512,768]{1,0:T(8,128)(2,1)S(1)} %bitcast.68, bf16[1024,1280]{1,0:T(8,128)(2,1)} %bitcast.21), kind=kOutput, calls=%fused_computation.17 | convolution fusion | flops 808452096 | bytes 4194304 | tf_op jit(solution)/shard_map/dot_general | solution.py:144
  174.0 4.7 %fusion.4 = f32[768,768]{1,0:T(8,128)} fusion(bf16[1024,1280]{1,0:T(8,128)(2,1)} %bitcast.21, bf16[512,768]{1,0:T(8,128)(2,1)} %bitcast.71, bf16[512,768]{1,0:T(8,128)(2,1)} %bitcast.69), kind=kOutput, calls=%fused_computation.10 | convolution fusion | flops 1211105280 | bytes 5505024 | tf_op jit(solution)/shard_map/dot_general | solution.py:144
  178.8 3.4 %bitcast_add_fusion = f32[512,768]{1,0:T(8,128)S(1)} fusion(f32[16,32,768]{2,1,0:T(8,128)} %all-to-all-done.2, bf16[1024,1280]{1,0:T(8,128)(2,1)} %bitcast.21), kind=kOutput, calls=%fused_computation.8 | convolution fusion | flops 805699584 | bytes 5767168 | tf_op jit(solution)/shard_map/dot_general | solution.py:144
  183.8 4.0 %add_subtract_fusion = f32[768,768]{1,0:T(8,128)} fusion(f32[768,768]{1,0:T(8,128)S(1)} %copy-done.2, f32[768,768]{1,0:T(8,128)S(1)} %copy-done.4, f32[512,768]{1,0:T(8,128)S(1)} %fusion, f32[512,768]{1,0:T(8,128)S(1)} %fusion.47), kind=kOutput, calls=%fused_computation | convolution fusion | flops 1813118976 | bytes 10223616 | tf_op jit(solution)/shard_map/dot_general | solution.py:250
  (111 shorter events, 41.7 us)
Async XLA Ops:
  2.2 16.3 %collective-permute-start.2 = (f32[4,32,768]{2,1,0:T(8,128)S(1)}, f32[4,32,768]{2,1,0:T(8,128)}, u32[]{:S(2)}, u32[]{:S(2)}) collective-permute-start(f32[4,32,768]{2,1,0:T(8,128)S(1)} %bitcast.77), channel_id=1, source_target_pairs={{0,32},{1,33},{2,34},{3,35},{4,36},{5,37},{6,38},{7,39},{128,160},... | collective-permute-start | bytes 1179656 | tf_op jit(solution)/shard_map/ppermute | solution.py:169
  7.0 15.4 %collective-permute-start.3 = (f32[4,32,768]{2,1,0:T(8,128)S(1)}, f32[4,32,768]{2,1,0:T(8,128)}, u32[]{:S(2)}, u32[]{:S(2)}) collective-permute-start(f32[4,32,768]{2,1,0:T(8,128)S(1)} %bitcast.76), channel_id=1, source_target_pairs={{0,64},{1,65},{2,66},{3,67},{4,68},{5,69},{6,70},{7,71},{128,192},... | collective-permute-start | bytes 1179656 | tf_op jit(solution)/shard_map/ppermute | solution.py:169
  10.0 12.4 %collective-permute-start.4 = (f32[4,32,768]{2,1,0:T(8,128)S(1)}, f32[4,32,768]{2,1,0:T(8,128)}, u32[]{:S(2)}, u32[]{:S(2)}) collective-permute-start(f32[4,32,768]{2,1,0:T(8,128)S(1)} %bitcast.75), channel_id=1, source_target_pairs={{0,96},{1,97},{2,98},{3,99},{4,100},{5,101},{6,102},{7,103},{128,2... | collective-permute-start | bytes 1179656 | tf_op jit(solution)/shard_map/ppermute | solution.py:169
  17.5 19.6 %collective-permute-start = (f32[4,128,256]{1,2,0:T(8,128)S(1)}, f32[4,128,256]{1,2,0:T(8,128)S(1)}, u32[]{:S(2)}, u32[]{:S(2)}) collective-permute-start(f32[4,128,256]{1,2,0:T(8,128)S(1)} %bitcast.72), channel_id=1, source_target_pairs={{0,128},{128,0},{1,129},{129,1},{2,130},{130,2},{3,131},{131,3},{4... | collective-permute-start | bytes 1572872 | tf_op jit(solution)/shard_map/ppermute | solution.py:186
  23.8 3.9 %collective-permute-start.6 = (f32[32,768]{1,0:T(8,128)S(1)}, f32[32,768]{1,0:T(8,128)S(1)}, u32[]{:S(2)}, u32[]{:S(2)}) collective-permute-start(f32[32,768]{1,0:T(8,128)S(1)} %get-tuple-element.38), channel_id=1, source_target_pairs={{0,16},{32,48},{64,80},{96,112},{1,17},{33,49},{65,81},{97,113},{2... | collective-permute-start | bytes 294920 | tf_op jit(solution)/shard_map/ppermute | solution.py:172
  26.4 3.0 %collective-permute-start.5 = (f32[32,768]{1,0:T(8,128)S(1)}, f32[32,768]{1,0:T(8,128)S(1)}, u32[]{:S(2)}, u32[]{:S(2)}) collective-permute-start(f32[32,768]{1,0:T(8,128)S(1)} %get-tuple-element.40), channel_id=1, source_target_pairs={{0,8},{32,40},{64,72},{96,104},{1,9},{33,41},{65,73},{97,105},{2,1... | collective-permute-start | bytes 294920 | tf_op jit(solution)/shard_map/ppermute | solution.py:172
  29.4 9.9 %collective-permute-start.8 = (f32[32,768]{1,0:T(8,128)S(1)}, f32[32,768]{1,0:T(8,128)S(1)}, u32[]{:S(2)}, u32[]{:S(2)}) collective-permute-start(f32[32,768]{1,0:T(8,128)S(1)} %fusion.26), channel_id=1, source_target_pairs={{0,0},{1,8},{2,16},{3,24},{4,32},{5,40},{6,48},{7,56},{128,64},{12... | collective-permute-start | bytes 294920 | tf_op jit(solution)/shard_map/ppermute | solution.py:206
  39.3 24.1 %collective-permute-start.11 = (f32[32,512]{1,0:T(8,128)S(1)}, f32[32,512]{1,0:T(8,128)S(1)}, u32[]{:S(2)}, u32[]{:S(2)}) collective-permute-start(f32[32,512]{1,0:T(8,128)S(1)} %slice.235), channel_id=1, source_target_pairs={{0,96},{1,97},{2,98},{3,99},{4,100},{5,101},{6,102},{7,103},{128,2... | collective-permute-start | bytes 196616 | tf_op jit(solution)/shard_map/ppermute | solution.py:209
  46.2 17.2 %collective-permute-start.10 = (f32[32,512]{1,0:T(8,128)S(1)}, f32[32,512]{1,0:T(8,128)S(1)}, u32[]{:S(2)}, u32[]{:S(2)}) collective-permute-start(f32[32,512]{1,0:T(8,128)S(1)} %slice.235), channel_id=1, source_target_pairs={{0,64},{1,65},{2,66},{3,67},{4,68},{5,69},{6,70},{7,71},{128,192},... | collective-permute-start | bytes 196616 | tf_op jit(solution)/shard_map/ppermute | solution.py:209
  47.5 15.9 %collective-permute-start.9 = (f32[32,512]{1,0:T(8,128)S(1)}, f32[32,512]{1,0:T(8,128)S(1)}, u32[]{:S(2)}, u32[]{:S(2)}) collective-permute-start(f32[32,512]{1,0:T(8,128)S(1)} %slice.235), channel_id=1, source_target_pairs={{0,32},{1,33},{2,34},{3,35},{4,36},{5,37},{6,38},{7,39},{128,160},... | collective-permute-start | bytes 196616 | tf_op jit(solution)/shard_map/ppermute | solution.py:209
  49.9 21.4 %all-to-all-start = ((bf16[16,4,1280]{2,1,0:T(4,128)(2,1)}), bf16[16,4,1280]{2,1,0:T(4,128)(2,1)S(1)}, u32[]{:S(2)}, u32[]{:S(2)}) async-start(bf16[16,4,1280]{2,1,0:T(4,128)(2,1)} %copy.25), calls=%async_computation | async-start | bytes 327680 | tf_op jit(solution)/shard_map/all_to_all | solution.py:198
  63.5 3.9 %collective-permute-start.14 = (f32[32,512]{1,0:T(8,128)S(1)}, f32[32,512]{1,0:T(8,128)S(1)}, u32[]{:S(2)}, u32[]{:S(2)}) collective-permute-start(f32[32,512]{1,0:T(8,128)S(1)} %add_select_fusion.2), channel_id=1, source_target_pairs={{0,24},{32,56},{64,88},{96,120},{1,25},{33,57},{65,89},{97,121},{2... | collective-permute-start | bytes 196616 | tf_op jit(solution)/shard_map/ppermute | solution.py:213
  71.3 7.4 %collective-permute-start.1 = (bf16[64,768]{1,0:T(8,128)(2,1)S(1)}, bf16[64,768]{1,0:T(8,128)(2,1)S(1)}, u32[]{:S(2)}, u32[]{:S(2)}) collective-permute-start(bf16[64,768]{1,0:T(8,128)(2,1)S(1)} %slice.230), channel_id=1, source_target_pairs={{0,0},{1,8},{2,16},{3,24},{4,32},{5,40},{6,48},{7,56},{128,64},{12... | collective-permute-start | bytes 294920 | tf_op jit(solution)/shard_map/ppermute | solution.py:224
  78.8 25.9 %collective-permute-start.16 = (bf16[176,768]{1,0:T(8,128)(2,1)S(1)}, bf16[176,768]{1,0:T(8,128)(2,1)S(1)}, u32[]{:S(2)}, u32[]{:S(2)}) collective-permute-start(bf16[176,768]{1,0:T(8,128)(2,1)S(1)} %fusion.22), channel_id=1, source_target_pairs={{0,6},{1,7},{2,0},{3,1},{4,2},{5,3},{6,4},{7,5},{8,14},{9,15},{10,... | collective-permute-start | bytes 811016 | tf_op jit(solution)/shard_map/ppermute | solution.py:125
  93.9 14.7 %collective-permute-start.15 = (bf16[176,768]{1,0:T(8,128)(2,1)S(1)}, bf16[176,768]{1,0:T(8,128)(2,1)S(1)}, u32[]{:S(2)}, u32[]{:S(2)}) collective-permute-start(bf16[176,768]{1,0:T(8,128)(2,1)S(1)} %fusion.22), channel_id=1, source_target_pairs={{0,2},{1,3},{2,4},{3,5},{4,6},{5,7},{6,0},{7,1},{8,10},{9,11},{10,... | collective-permute-start | bytes 811016 | tf_op jit(solution)/shard_map/ppermute | solution.py:125
  95.7 43.4 %all-to-all-start.1 = ((bf16[16,64,1280]{2,1,0:T(8,128)(2,1)}), bf16[16,64,1280]{2,1,0:T(8,128)(2,1)}, u32[]{:S(2)}, u32[]{:S(2)}) async-start(bf16[16,64,1280]{2,1,0:T(8,128)(2,1)} %broadcast_in_dim.55), calls=%async_computation.1 | async-start | bytes 5242880 | tf_op jit(solution)/shard_map/all_to_all | solution.py:117
  100.1 17.3 %collective-permute-start.17 = (bf16[176,768]{1,0:T(8,128)(2,1)S(1)}, bf16[176,768]{1,0:T(8,128)(2,1)S(1)}, u32[]{:S(2)}, u32[]{:S(2)}) collective-permute-start(bf16[176,768]{1,0:T(8,128)(2,1)S(1)} %fusion.22), channel_id=1, source_target_pairs={{0,1},{1,2},{2,3},{3,4},{4,5},{5,6},{6,7},{7,0},{8,9},{9,10},{10,1... | collective-permute-start | bytes 811016 | tf_op jit(solution)/shard_map/ppermute | solution.py:125
  102.0 15.4 %collective-permute-start.18 = (bf16[176,768]{1,0:T(8,128)(2,1)S(1)}, bf16[176,768]{1,0:T(8,128)(2,1)S(1)}, u32[]{:S(2)}, u32[]{:S(2)}) collective-permute-start(bf16[176,768]{1,0:T(8,128)(2,1)S(1)} %fusion.22), channel_id=1, source_target_pairs={{0,7},{1,0},{2,1},{3,2},{4,3},{5,4},{6,5},{7,6},{8,15},{9,8},{10,9... | collective-permute-start | bytes 811016 | tf_op jit(solution)/shard_map/ppermute | solution.py:125
  104.7 23.1 %collective-permute-start.22 = (bf16[88,768]{1,0:T(8,128)(2,1)S(1)}, bf16[88,768]{1,0:T(8,128)(2,1)S(1)}, u32[]{:S(2)}, u32[]{:S(2)}) collective-permute-start(bf16[88,768]{1,0:T(8,128)(2,1)S(1)} %slice.241), channel_id=1, source_target_pairs={{0,6},{1,7},{2,0},{3,1},{4,2},{5,3},{6,4},{7,5},{8,14},{9,15},{10,... | collective-permute-start | bytes 405512 | tf_op jit(solution)/shard_map/ppermute | solution.py:125
  108.6 19.2 %collective-permute-start.21 = (bf16[88,768]{1,0:T(8,128)(2,1)S(1)}, bf16[88,768]{1,0:T(8,128)(2,1)S(1)}, u32[]{:S(2)}, u32[]{:S(2)}) collective-permute-start(bf16[88,768]{1,0:T(8,128)(2,1)S(1)} %slice.240), channel_id=1, source_target_pairs={{0,2},{1,3},{2,4},{3,5},{4,6},{5,7},{6,0},{7,1},{8,10},{9,11},{10,... | collective-permute-start | bytes 405512 | tf_op jit(solution)/shard_map/ppermute | solution.py:125
  108.7 19.1 %collective-permute-start.20 = (bf16[176,768]{1,0:T(8,128)(2,1)S(1)}, bf16[176,768]{1,0:T(8,128)(2,1)S(1)}, u32[]{:S(2)}, u32[]{:S(2)}) collective-permute-start(bf16[176,768]{1,0:T(8,128)(2,1)S(1)} %collective-permute-done.16), channel_id=1, source_target_pairs={{0,7},{1,0},{2,1},{3,2},{4,3},{5,4},{6,5},{7,6},{8,15},{9,8},{10,9... | collective-permute-start | bytes 811016 | tf_op jit(solution)/shard_map/ppermute | solution.py:125
  117.4 10.3 %collective-permute-start.19 = (bf16[176,768]{1,0:T(8,128)(2,1)S(1)}, bf16[176,768]{1,0:T(8,128)(2,1)S(1)}, u32[]{:S(2)}, u32[]{:S(2)}) collective-permute-start(bf16[176,768]{1,0:T(8,128)(2,1)S(1)} %collective-permute-done.15), channel_id=1, source_target_pairs={{0,1},{1,2},{2,3},{3,4},{4,5},{5,6},{6,7},{7,0},{8,9},{9,10},{10,1... | collective-permute-start | bytes 811016 | tf_op jit(solution)/shard_map/ppermute | solution.py:125
  127.9 17.0 %collective-permute-start.23 = (bf16[8,176,768]{2,1,0:T(8,128)(2,1)S(1)}, bf16[8,176,768]{2,1,0:T(8,128)(2,1)}, u32[]{:S(2)}, u32[]{:S(2)}) collective-permute-start(bf16[8,176,768]{2,1,0:T(8,128)(2,1)S(1)} %fusion.23), channel_id=1, source_target_pairs={{0,128},{128,0},{1,129},{129,1},{2,130},{130,2},{3,131},{131,3},{4... | collective-permute-start | bytes 6488072 | tf_op jit(solution)/shard_map/ppermute | solution.py:229
  140.4 38.4 %all-to-all-start.2 = ((f32[16,32,768]{2,1,0:T(8,128)}), f32[16,32,768]{2,1,0:T(8,128)}, u32[]{:S(2)}, u32[]{:S(2)}) async-start(f32[16,32,768]{2,1,0:T(8,128)} %broadcast_in_dim.56), calls=%async_computation.2 | async-start | bytes 3145728 | tf_op jit(solution)/shard_map/all_to_all | solution.py:117
  (11 other events, 82.3 us)

commit v3 on v2

--- a/solution.py
+++ b/solution.py
@@ -85,7 +85,7 @@
         @pl.when(b < n // NB - 1)
         def _():
             u = jnp.where(lane >= o + NB, w[:, :n], 0.0)
-            s_ref[...] = s_ref[...] - dot3(u, w, ((0,), (0,)))
+            s_ref[NB:, NB:] = s_ref[NB:, NB:] - dot3(u[:, NB:], w[:, NB:], ((0,), (0,)))
 
         return carry
 
@@ -226,6 +226,8 @@
     mine = gather_ring(mine, "col")
     lead_col = gather(lead_piece, "row").reshape(-1, cols_blk)
 
+    gram_lead = gram(lead_feats, col_all)
+    mine, gram_lead = lax.optimization_barrier((mine, gram_lead))
     theirs = lax.ppermute(mine, "tp", swap)
     low, high = jnp.where(first, mine, theirs), jnp.where(first, theirs, mine)
     row_feats, lead_row, diag = [], [], []
@@ -241,9 +243,10 @@
         diag.append(d.reshape(-1, PANEL))
     row_feats, lead_row, diag = (jnp.concatenate(v) for v in (row_feats, lead_row, diag))
 
-    inv = inverse_factor(diag + gram(lead_feats, lead_feats))
+    inv = inverse_factor(diag + gram_lead[:, cols_blk:])
+    inv, lead_col = lax.optimization_barrier((inv, lead_col))
     panel_row = jnp.dot(inv, lead_row + gram(lead_feats, row_feats), precision=HIGH)
-    panel_col = jnp.dot(inv, lead_col + gram(lead_feats, col_feats), precision=HIGH)
+    panel_col = jnp.dot(inv, lead_col + gram_lead[:, :cols_blk], precision=HIGH)
     trailing = (
         curvature
         + gram(row_feats, col_feats)

time: 189 us -> 193 us (1.021)
  other arithmetic: 4.52 us -> 12.7 us
  local copies, waits for them, and re-layouts: 7.9 us -> 15.1 us
  starting transfers between devices: 86 us -> 80.8 us
  waiting for transfers between devices: 43.5 us -> 39.6 us
    ppermute x1, waiting for transfers between devices: 5.22 us -> 25.4 us  [per_device(): turned = lax.ppermute(got[:, :cols_blk], axes, turn)]
    ppermute x8, waiting for transfers between devices: 17.8 us -> 4.05 us  [shift(): return lax.ppermute(v, axis, [(i, (i + k) % n) for i in range(n)])]
    ppermute x8, starting transfers between devices: 24.5 us -> 12.6 us  [shift(): return lax.ppermute(v, axis, [(i, (i + k) % n) for i in range(n)])]
    all_to_all x2, waiting for transfers between devices: 10.3 us -> 0.01 us  [gather(): lax.all_to_all(jnp.broadcast_to(x[None], (n,) + x.shape), axis, 0, 0, til...]
    dot_general x4 -> x3, matrix products: 12.7 us -> 8.11 us  [gram(): lax.dot_general(a, b, (((0,), (0,)), ((), ())), preferred_element_type=f32)]
    dynamic_update_slice x6, local copies, waits for them, and re-layouts: 0.14 us -> 4.33 us  [put(): return lax.dynamic_update_index_in_dim(out, v, lax.rem(me + n - k, n), 0)]
    ppermute x1, starting transfers between devices: 2.2 us -> 5.89 us  [per_device(): turned = lax.ppermute(got[:, :cols_blk], axes, turn)]
    all_to_all x2, starting transfers between devices: 8.89 us -> 12 us  [gather(): lax.all_to_all(jnp.broadcast_to(x[None], (n,) + x.shape), axis, 0, 0, til...]
  transfers between devices with their start and end apart: 27 -> 27, of which waited for: 12 -> 11; matrix products, arithmetic and copies ran while one was open for 15% -> 16% of each run, Pallas kernels for 10% -> 9%
where the time goes in v3:
time: 193 us; the launch traced here: 192 us
  starting transfers between devices  80.8 us (42%)
  waiting for transfers between devices  39.6 us (21%)
  matrix products  25.1 us (13%)
  Pallas kernels  17.9 us (9%)
  local copies, waits for them, and re-layouts  15.1 us (8%)
  other arithmetic  12.7 us (7%)
    ppermute x1, waiting for transfers between devices, per_device(): turned = lax.ppermute(got[:, :cols_blk], axes, turn)  25.4 us
    pallas_call x1, Pallas kernels, inverse_factor(): pl.pallas_call(factor_kernel, out_shape=jax.ShapeDtypeStruct((PANEL, PANE...  17.9 us
    all_to_all x1, starting transfers between devices, per_device(): got = lax.all_to_all(out, ('tp', 'col'), 0, 0, tiled=True)  14.2 us
    ppermute x8, starting transfers between devices, shift(): return lax.ppermute(v, axis, [(i, (i + k) % n) for i in range(n)])  12.6 us
    all_to_all x2, starting transfers between devices, gather(): lax.all_to_all(jnp.broadcast_to(x[None], (n,) + x.shape), axis, 0, 0, til...  12 us
    ppermute x3, starting transfers between devices, per_device(): lax.ppermute(lead[k], 'row', [(0, side * k)])  9.85 us
    ppermute x3, starting transfers between devices, per_device(): lax.ppermute(diag, 'row', [(0, side * k)])  9.69 us
    dot_general x3, matrix products, gram(): lax.dot_general(a, b, (((0,), (0,)), ((), ())), preferred_element_type=f32)  8.11 us
  transfers between devices with their start and end apart: 27, of which 11 were waited for; matrix products, arithmetic and copies ran while one was open for 16% of the time, Pallas kernels for 9%

profile of v3, /device:TPU:1, one launch (start us, length us, event | category | flops | bytes accessed | tf_op | source)
XLA Modules:
  0.0 192.3 jit_solution(1994493958820950564)
XLA Ops:
  2.2 4.8 %collective-permute-start.2 = (f32[4,32,768]{2,1,0:T(8,128)S(1)}, f32[4,32,768]{2,1,0:T(8,128)}, u32[]{:S(2)}, u32[]{:S(2)}) collective-permute-start(f32[4,32,768]{2,1,0:T(8,128)S(1)} %bitcast.80), channel_id=1, source_target_pairs={{0,32},{1,33},{2,34},{3,35},{4,36},{5,37},{6,38},{7,39},{128,160},... | collective-permute-start | bytes 1179656 | tf_op jit(solution)/shard_map/ppermute | solution.py:169
  7.0 3.0 %collective-permute-start.3 = (f32[4,32,768]{2,1,0:T(8,128)S(1)}, f32[4,32,768]{2,1,0:T(8,128)}, u32[]{:S(2)}, u32[]{:S(2)}) collective-permute-start(f32[4,32,768]{2,1,0:T(8,128)S(1)} %bitcast.79), channel_id=1, source_target_pairs={{0,64},{1,65},{2,66},{3,67},{4,68},{5,69},{6,70},{7,71},{128,192},... | collective-permute-start | bytes 1179656 | tf_op jit(solution)/shard_map/ppermute | solution.py:169
  12.1 3.9 %fusion.47 = f32[1024,192]{0,1:T(8,128)S(1)} fusion(bf16[1024,2048]{1,0:T(8,128)(2,1)} %bitcast.82, bf16[2048,192]{0,1:T(8,128)(2,1)S(1)} %copy-done), kind=kOutput, calls=%fused_computation.99 | convolution fusion | flops 805306368 | bytes 5767168 | tf_op jit(solution)/shard_map/dot_general | solution.py:179
  18.6 3.9 %collective-permute-done.3 = f32[4,32,768]{2,1,0:T(8,128)} collective-permute-done((f32[4,32,768]{2,1,0:T(8,128)S(1)}, f32[4,32,768]{2,1,0:T(8,128)}, u32[]{:S(2)}, u32[]{:S(2)}) %collective-permute-start.3) | collective-permute-done | bytes 393248 | tf_op jit(solution)/shard_map/ppermute | solution.py:169
  29.3 7.7 %collective-permute-start.8 = (f32[32,768]{1,0:T(8,128)S(1)}, f32[32,768]{1,0:T(8,128)S(1)}, u32[]{:S(2)}, u32[]{:S(2)}) collective-permute-start(f32[32,768]{1,0:T(8,128)S(1)} %fusion.28), channel_id=1, source_target_pairs={{0,0},{1,8},{2,16},{3,24},{4,32},{5,40},{6,48},{7,56},{128,64},{12... | collective-permute-start | bytes 294920 | tf_op jit(solution)/shard_map/ppermute | solution.py:206
  40.6 6.2 %collective-permute-start.11 = (f32[32,512]{1,0:T(8,128)S(1)}, f32[32,512]{1,0:T(8,128)S(1)}, u32[]{:S(2)}, u32[]{:S(2)}) collective-permute-start(f32[32,512]{1,0:T(8,128)S(1)} %slice.243), channel_id=1, source_target_pairs={{0,96},{1,97},{2,98},{3,99},{4,100},{5,101},{6,102},{7,103},{128,2... | collective-permute-start | bytes 196616 | tf_op jit(solution)/shard_map/ppermute | solution.py:209
  46.8 2.2 %collective-permute-start.9 = (f32[32,512]{1,0:T(8,128)S(1)}, f32[32,512]{1,0:T(8,128)S(1)}, u32[]{:S(2)}, u32[]{:S(2)}) collective-permute-start(f32[32,512]{1,0:T(8,128)S(1)} %slice.243), channel_id=1, source_target_pairs={{0,32},{1,33},{2,34},{3,35},{4,36},{5,37},{6,38},{7,39},{128,160},... | collective-permute-start | bytes 196616 | tf_op jit(solution)/shard_map/ppermute | solution.py:209
  49.8 14.2 %all-to-all-start = ((bf16[16,4,1280]{2,1,0:T(4,128)(2,1)}), bf16[16,4,1280]{2,1,0:T(4,128)(2,1)S(1)}, u32[]{:S(2)}, u32[]{:S(2)}) async-start(bf16[16,4,1280]{2,1,0:T(4,128)(2,1)} %copy.25), calls=%async_computation | async-start | bytes 327680 | tf_op jit(solution)/shard_map/all_to_all | solution.py:198
  69.6 2.3 %all-to-all-done = bf16[16,4,1280]{2,1,0:T(4,128)(2,1)S(1)} async-done(((bf16[16,4,1280]{2,1,0:T(4,128)(2,1)}), bf16[16,4,1280]{2,1,0:T(4,128)(2,1)S(1)}, u32[]{:S(2)}, u32[]{:S(2)}) %all-to-all-start) | async-done | bytes 163872 | tf_op jit(solution)/shard_map/all_to_all | solution.py:198
  73.7 3.7 %all-to-all-start.1 = ((bf16[16,64,1280]{2,1,0:T(8,128)(2,1)}), bf16[16,64,1280]{2,1,0:T(8,128)(2,1)S(1)}, u32[]{:S(2)}, u32[]{:S(2)}) async-start(bf16[16,64,1280]{2,1,0:T(8,128)(2,1)} %broadcast_in_dim.55), calls=%async_computation.1 | async-start | bytes 5242880 | tf_op jit(solution)/shard_map/all_to_all | solution.py:117
  77.5 5.9 %collective-permute-start.1 = (bf16[64,768]{1,0:T(8,128)(2,1)S(1)}, bf16[64,768]{1,0:T(8,128)(2,1)S(1)}, u32[]{:S(2)}, u32[]{:S(2)}) collective-permute-start(bf16[64,768]{1,0:T(8,128)(2,1)S(1)} %slice.238), channel_id=1, source_target_pairs={{0,0},{1,8},{2,16},{3,24},{4,32},{5,40},{6,48},{7,56},{128,64},{12... | collective-permute-start | bytes 294920 | tf_op jit(solution)/shard_map/ppermute | solution.py:224
  83.4 25.4 %collective-permute-done.1 = bf16[64,768]{1,0:T(8,128)(2,1)S(1)} collective-permute-done((bf16[64,768]{1,0:T(8,128)(2,1)S(1)}, bf16[64,768]{1,0:T(8,128)(2,1)S(1)}, u32[]{:S(2)}, u32[]{:S(2)}) %collective-permute-start.1) | collective-permute-done | bytes 98336 | tf_op jit(solution)/shard_map/ppermute | solution.py:224
  109.5 3.6 %collective-permute-start.16 = (bf16[176,768]{1,0:T(8,128)(2,1)}, bf16[176,768]{1,0:T(8,128)(2,1)S(1)}, u32[]{:S(2)}, u32[]{:S(2)}) collective-permute-start(bf16[176,768]{1,0:T(8,128)(2,1)} %fusion.24), channel_id=1, source_target_pairs={{0,6},{1,7},{2,0},{3,1},{4,2},{5,3},{6,4},{7,5},{8,14},{9,15},{10,... | collective-permute-start | bytes 811016 | tf_op jit(solution)/shard_map/ppermute | solution.py:125
  113.1 2.7 %collective-permute-start.18 = (bf16[176,768]{1,0:T(8,128)(2,1)}, bf16[176,768]{1,0:T(8,128)(2,1)S(1)}, u32[]{:S(2)}, u32[]{:S(2)}) collective-permute-start(bf16[176,768]{1,0:T(8,128)(2,1)} %fusion.24), channel_id=1, source_target_pairs={{0,7},{1,0},{2,1},{3,2},{4,3},{5,4},{6,5},{7,6},{8,15},{9,8},{10,9... | collective-permute-start | bytes 811016 | tf_op jit(solution)/shard_map/ppermute | solution.py:125
  118.0 2.8 %collective-permute-done.15 = bf16[176,768]{1,0:T(8,128)(2,1)S(1)} collective-permute-done((bf16[176,768]{1,0:T(8,128)(2,1)}, bf16[176,768]{1,0:T(8,128)(2,1)S(1)}, u32[]{:S(2)}, u32[]{:S(2)}) %collective-permute-start.15) | collective-permute-done | bytes 270368 | tf_op jit(solution)/shard_map/ppermute | solution.py:125
  120.9 3.6 %collective-permute-start.22 = (bf16[88,768]{1,0:T(8,128)(2,1)S(1)}, bf16[88,768]{1,0:T(8,128)(2,1)S(1)}, u32[]{:S(2)}, u32[]{:S(2)}) collective-permute-start(bf16[88,768]{1,0:T(8,128)(2,1)S(1)} %slice.249), channel_id=1, source_target_pairs={{0,6},{1,7},{2,0},{3,1},{4,2},{5,3},{6,4},{7,5},{8,14},{9,15},{10,... | collective-permute-start | bytes 405512 | tf_op jit(solution)/shard_map/ppermute | solution.py:125
  126.0 2.7 %collective-permute-start.20 = (bf16[176,768]{1,0:T(8,128)(2,1)S(1)}, bf16[176,768]{1,0:T(8,128)(2,1)S(1)}, u32[]{:S(2)}, u32[]{:S(2)}) collective-permute-start(bf16[176,768]{1,0:T(8,128)(2,1)S(1)} %collective-permute-done.16), channel_id=1, source_target_pairs={{0,7},{1,0},{2,1},{3,2},{4,3},{5,4},{6,5},{7,6},{8,15},{9,8},{10,9... | collective-permute-start | bytes 811016 | tf_op jit(solution)/shard_map/ppermute | solution.py:125
  133.5 3.1 %fusion.11 = f32[512,1280]{1,0:T(8,128)} fusion(bf16[1024,1280]{1,0:T(8,128)(2,1)S(1)} %bitcast.63), kind=kOutput, calls=%fused_computation.20 | convolution fusion | flops 1342177280 | bytes 6291456 | tf_op jit(solution)/shard_map/dot_general | solution.py:144
  137.9 8.3 %all-to-all-start.2 = ((f32[16,32,768]{2,1,0:T(8,128)}), f32[16,32,768]{2,1,0:T(8,128)S(1)}, u32[]{:S(2)}, u32[]{:S(2)}) async-start(f32[16,32,768]{2,1,0:T(8,128)} %broadcast_in_dim.56), calls=%async_computation.2 | async-start | bytes 3145728 | tf_op jit(solution)/shard_map/all_to_all | solution.py:117
  146.3 2.5 %broadcast_select_fusion.1 = (bf16[8,176,768]{2,1,0:T(8,128)(2,1)S(1)}, bf16[8,176,768]{2,1,0:T(8,128)(2,1)S(1)}) fusion(bf16[8,176,768]{2,1,0:T(8,128)(2,1)} %fusion.25, bf16[8,176,768]{2,1,0:T(8,128)(2,1)} %collective-permute-done.23, pred[]{:T(512)S(6)} %eq.11), kind=kLoop, calls=%fused_computation.2 | loop fusion | flops 2162688 | bytes 8650753 | tf_op jit(solution)/shard_map/jit(_where)/select_n | solution.py:232
  150.9 17.9 %inverse_factor.1 = f32[512,512]{1,0:T(8,128)S(1)} custom-call(f32[512,512]{1,0:T(8,128)S(1)} %maximum_add_fusion.2.a_ref), custom_call_target="tpu_custom_call" | custom-call | tf_op jit(solution)/shard_map/inverse_factor/pallas_call | solution.py:96
  174.7 2.9 %fusion.6 = f32[768,768]{1,0:T(8,128)} fusion(bf16[1024,1280]{1,0:T(8,128)(2,1)S(1)} %bitcast.65, bf16[512,768]{1,0:T(8,128)(2,1)S(1)} %bitcast.76, bf16[512,768]{1,0:T(8,128)(2,1)S(1)} %bitcast.74), kind=kOutput, calls=%fused_computation.11 | convolution fusion | flops 1211105280 | bytes 5505024 | tf_op jit(solution)/shard_map/dot_general | solution.py:144
  180.2 2.7 %fusion.3 = f32[512,768]{1,0:T(8,128)} fusion(f32[512,512]{1,0:T(8,128)S(1)} %inverse_factor.1, f32[512,768]{1,0:T(8,128)S(1)} %bitcast.67, f32[512,1280]{1,0:T(8,128)S(1)} %copy-done.4), kind=kOutput, calls=%fused_computation.8 | convolution fusion | flops 1208352768 | bytes 5767168 | tf_op jit(solution)/shard_map/dot_general | solution.py:249
  185.6 6.7 %add_subtract_fusion = f32[768,768]{1,0:T(8,128)} fusion(f32[768,768]{1,0:T(8,128)} %param.9, f32[768,768]{1,0:T(8,128)} %fusion.6, f32[512,768]{1,0:T(8,128)S(1)} %fusion, f32[512,768]{1,0:T(8,128)} %fusion.3), kind=kOutput, calls=%fused_computation | convolution fusion | flops 1813118976 | bytes 10223616 | tf_op jit(solution)/shard_map/dot_general | solution.py:253
  (117 shorter events, 48.7 us)
Async XLA Ops:
  2.2 16.4 %collective-permute-start.2 = (f32[4,32,768]{2,1,0:T(8,128)S(1)}, f32[4,32,768]{2,1,0:T(8,128)}, u32[]{:S(2)}, u32[]{:S(2)}) collective-permute-start(f32[4,32,768]{2,1,0:T(8,128)S(1)} %bitcast.80), channel_id=1, source_target_pairs={{0,32},{1,33},{2,34},{3,35},{4,36},{5,37},{6,38},{7,39},{128,160},... | collective-permute-start | bytes 1179656 | tf_op jit(solution)/shard_map/ppermute | solution.py:169
  7.0 15.4 %collective-permute-start.3 = (f32[4,32,768]{2,1,0:T(8,128)S(1)}, f32[4,32,768]{2,1,0:T(8,128)}, u32[]{:S(2)}, u32[]{:S(2)}) collective-permute-start(f32[4,32,768]{2,1,0:T(8,128)S(1)} %bitcast.79), channel_id=1, source_target_pairs={{0,64},{1,65},{2,66},{3,67},{4,68},{5,69},{6,70},{7,71},{128,192},... | collective-permute-start | bytes 1179656 | tf_op jit(solution)/shard_map/ppermute | solution.py:169
  10.0 12.4 %collective-permute-start.4 = (f32[4,32,768]{2,1,0:T(8,128)S(1)}, f32[4,32,768]{2,1,0:T(8,128)}, u32[]{:S(2)}, u32[]{:S(2)}) collective-permute-start(f32[4,32,768]{2,1,0:T(8,128)S(1)} %bitcast.78), channel_id=1, source_target_pairs={{0,96},{1,97},{2,98},{3,99},{4,100},{5,101},{6,102},{7,103},{128,2... | collective-permute-start | bytes 1179656 | tf_op jit(solution)/shard_map/ppermute | solution.py:169
  17.5 19.5 %collective-permute-start = (f32[4,128,256]{1,2,0:T(8,128)S(1)}, f32[4,128,256]{1,2,0:T(8,128)S(1)}, u32[]{:S(2)}, u32[]{:S(2)}) collective-permute-start(f32[4,128,256]{1,2,0:T(8,128)S(1)} %bitcast.77), channel_id=1, source_target_pairs={{0,128},{128,0},{1,129},{129,1},{2,130},{130,2},{3,131},{131,3},{4... | collective-permute-start | bytes 1572872 | tf_op jit(solution)/shard_map/ppermute | solution.py:186
  23.8 3.9 %collective-permute-start.5 = (f32[32,768]{1,0:T(8,128)S(1)}, f32[32,768]{1,0:T(8,128)S(1)}, u32[]{:S(2)}, u32[]{:S(2)}) collective-permute-start(f32[32,768]{1,0:T(8,128)S(1)} %get-tuple-element.48), channel_id=1, source_target_pairs={{0,8},{32,40},{64,72},{96,104},{1,9},{33,41},{65,73},{97,105},{2,1... | collective-permute-start | bytes 294920 | tf_op jit(solution)/shard_map/ppermute | solution.py:172
  25.1 3.5 %collective-permute-start.6 = (f32[32,768]{1,0:T(8,128)S(1)}, f32[32,768]{1,0:T(8,128)S(1)}, u32[]{:S(2)}, u32[]{:S(2)}) collective-permute-start(f32[32,768]{1,0:T(8,128)S(1)} %get-tuple-element.46), channel_id=1, source_target_pairs={{0,16},{32,48},{64,80},{96,112},{1,17},{33,49},{65,81},{97,113},{2... | collective-permute-start | bytes 294920 | tf_op jit(solution)/shard_map/ppermute | solution.py:172
  29.3 10.0 %collective-permute-start.8 = (f32[32,768]{1,0:T(8,128)S(1)}, f32[32,768]{1,0:T(8,128)S(1)}, u32[]{:S(2)}, u32[]{:S(2)}) collective-permute-start(f32[32,768]{1,0:T(8,128)S(1)} %fusion.28), channel_id=1, source_target_pairs={{0,0},{1,8},{2,16},{3,24},{4,32},{5,40},{6,48},{7,56},{128,64},{12... | collective-permute-start | bytes 294920 | tf_op jit(solution)/shard_map/ppermute | solution.py:206
  39.3 24.7 %collective-permute-start.10 = (f32[32,512]{1,0:T(8,128)S(1)}, f32[32,512]{1,0:T(8,128)S(1)}, u32[]{:S(2)}, u32[]{:S(2)}) collective-permute-start(f32[32,512]{1,0:T(8,128)S(1)} %slice.243), channel_id=1, source_target_pairs={{0,64},{1,65},{2,66},{3,67},{4,68},{5,69},{6,70},{7,71},{128,192},... | collective-permute-start | bytes 196616 | tf_op jit(solution)/shard_map/ppermute | solution.py:209
  40.6 23.4 %collective-permute-start.11 = (f32[32,512]{1,0:T(8,128)S(1)}, f32[32,512]{1,0:T(8,128)S(1)}, u32[]{:S(2)}, u32[]{:S(2)}) collective-permute-start(f32[32,512]{1,0:T(8,128)S(1)} %slice.243), channel_id=1, source_target_pairs={{0,96},{1,97},{2,98},{3,99},{4,100},{5,101},{6,102},{7,103},{128,2... | collective-permute-start | bytes 196616 | tf_op jit(solution)/shard_map/ppermute | solution.py:209
  46.8 17.2 %collective-permute-start.9 = (f32[32,512]{1,0:T(8,128)S(1)}, f32[32,512]{1,0:T(8,128)S(1)}, u32[]{:S(2)}, u32[]{:S(2)}) collective-permute-start(f32[32,512]{1,0:T(8,128)S(1)} %slice.243), channel_id=1, source_target_pairs={{0,32},{1,33},{2,34},{3,35},{4,36},{5,37},{6,38},{7,39},{128,160},... | collective-permute-start | bytes 196616 | tf_op jit(solution)/shard_map/ppermute | solution.py:209
  49.8 22.1 %all-to-all-start = ((bf16[16,4,1280]{2,1,0:T(4,128)(2,1)}), bf16[16,4,1280]{2,1,0:T(4,128)(2,1)S(1)}, u32[]{:S(2)}, u32[]{:S(2)}) async-start(bf16[16,4,1280]{2,1,0:T(4,128)(2,1)} %copy.25), calls=%async_computation | async-start | bytes 327680 | tf_op jit(solution)/shard_map/all_to_all | solution.py:198
  64.1 3.9 %collective-permute-start.12 = (f32[32,512]{1,0:T(8,128)S(1)}, f32[32,512]{1,0:T(8,128)S(1)}, u32[]{:S(2)}, u32[]{:S(2)}) collective-permute-start(f32[32,512]{1,0:T(8,128)S(1)} %add_select_fusion.2), channel_id=1, source_target_pairs={{0,8},{32,40},{64,72},{96,104},{1,9},{33,41},{65,73},{97,105},{2,1... | collective-permute-start | bytes 196616 | tf_op jit(solution)/shard_map/ppermute | solution.py:213
  73.7 59.8 %all-to-all-start.1 = ((bf16[16,64,1280]{2,1,0:T(8,128)(2,1)}), bf16[16,64,1280]{2,1,0:T(8,128)(2,1)S(1)}, u32[]{:S(2)}, u32[]{:S(2)}) async-start(bf16[16,64,1280]{2,1,0:T(8,128)(2,1)} %broadcast_in_dim.55), calls=%async_computation.1 | async-start | bytes 5242880 | tf_op jit(solution)/shard_map/all_to_all | solution.py:117
  77.5 31.3 %collective-permute-start.1 = (bf16[64,768]{1,0:T(8,128)(2,1)S(1)}, bf16[64,768]{1,0:T(8,128)(2,1)S(1)}, u32[]{:S(2)}, u32[]{:S(2)}) collective-permute-start(bf16[64,768]{1,0:T(8,128)(2,1)S(1)} %slice.238), channel_id=1, source_target_pairs={{0,0},{1,8},{2,16},{3,24},{4,32},{5,40},{6,48},{7,56},{128,64},{12... | collective-permute-start | bytes 294920 | tf_op jit(solution)/shard_map/ppermute | solution.py:224
  109.5 11.3 %collective-permute-start.15 = (bf16[176,768]{1,0:T(8,128)(2,1)}, bf16[176,768]{1,0:T(8,128)(2,1)S(1)}, u32[]{:S(2)}, u32[]{:S(2)}) collective-permute-start(bf16[176,768]{1,0:T(8,128)(2,1)} %fusion.24), channel_id=1, source_target_pairs={{0,2},{1,3},{2,4},{3,5},{4,6},{5,7},{6,0},{7,1},{8,10},{9,11},{10,... | collective-permute-start | bytes 811016 | tf_op jit(solution)/shard_map/ppermute | solution.py:125
  109.5 11.4 %collective-permute-start.16 = (bf16[176,768]{1,0:T(8,128)(2,1)}, bf16[176,768]{1,0:T(8,128)(2,1)S(1)}, u32[]{:S(2)}, u32[]{:S(2)}) collective-permute-start(bf16[176,768]{1,0:T(8,128)(2,1)} %fusion.24), channel_id=1, source_target_pairs={{0,6},{1,7},{2,0},{3,1},{4,2},{5,3},{6,4},{7,5},{8,14},{9,15},{10,... | collective-permute-start | bytes 811016 | tf_op jit(solution)/shard_map/ppermute | solution.py:125
  113.1 12.9 %collective-permute-start.17 = (bf16[176,768]{1,0:T(8,128)(2,1)}, bf16[176,768]{1,0:T(8,128)(2,1)S(1)}, u32[]{:S(2)}, u32[]{:S(2)}) collective-permute-start(bf16[176,768]{1,0:T(8,128)(2,1)} %fusion.24), channel_id=1, source_target_pairs={{0,1},{1,2},{2,3},{3,4},{4,5},{5,6},{6,7},{7,0},{8,9},{9,10},{10,1... | collective-permute-start | bytes 811016 | tf_op jit(solution)/shard_map/ppermute | solution.py:125
  113.1 16.3 %collective-permute-start.18 = (bf16[176,768]{1,0:T(8,128)(2,1)}, bf16[176,768]{1,0:T(8,128)(2,1)S(1)}, u32[]{:S(2)}, u32[]{:S(2)}) collective-permute-start(bf16[176,768]{1,0:T(8,128)(2,1)} %fusion.24), channel_id=1, source_target_pairs={{0,7},{1,0},{2,1},{3,2},{4,3},{5,4},{6,5},{7,6},{8,15},{9,8},{10,9... | collective-permute-start | bytes 811016 | tf_op jit(solution)/shard_map/ppermute | solution.py:125
  120.8 12.0 %collective-permute-start.21 = (bf16[88,768]{1,0:T(8,128)(2,1)S(1)}, bf16[88,768]{1,0:T(8,128)(2,1)S(1)}, u32[]{:S(2)}, u32[]{:S(2)}) collective-permute-start(bf16[88,768]{1,0:T(8,128)(2,1)S(1)} %slice.248), channel_id=1, source_target_pairs={{0,2},{1,3},{2,4},{3,5},{4,6},{5,7},{6,0},{7,1},{8,10},{9,11},{10,... | collective-permute-start | bytes 405512 | tf_op jit(solution)/shard_map/ppermute | solution.py:125
  120.9 11.9 %collective-permute-start.22 = (bf16[88,768]{1,0:T(8,128)(2,1)S(1)}, bf16[88,768]{1,0:T(8,128)(2,1)S(1)}, u32[]{:S(2)}, u32[]{:S(2)}) collective-permute-start(bf16[88,768]{1,0:T(8,128)(2,1)S(1)} %slice.249), channel_id=1, source_target_pairs={{0,6},{1,7},{2,0},{3,1},{4,2},{5,3},{6,4},{7,5},{8,14},{9,15},{10,... | collective-permute-start | bytes 405512 | tf_op jit(solution)/shard_map/ppermute | solution.py:125
  124.6 6.5 %collective-permute-start.19 = (bf16[176,768]{1,0:T(8,128)(2,1)S(1)}, bf16[176,768]{1,0:T(8,128)(2,1)S(1)}, u32[]{:S(2)}, u32[]{:S(2)}) collective-permute-start(bf16[176,768]{1,0:T(8,128)(2,1)S(1)} %collective-permute-done.15), channel_id=1, source_target_pairs={{0,1},{1,2},{2,3},{3,4},{4,5},{5,6},{6,7},{7,0},{8,9},{9,10},{10,1... | collective-permute-start | bytes 811016 | tf_op jit(solution)/shard_map/ppermute | solution.py:125
  126.0 6.1 %collective-permute-start.20 = (bf16[176,768]{1,0:T(8,128)(2,1)S(1)}, bf16[176,768]{1,0:T(8,128)(2,1)S(1)}, u32[]{:S(2)}, u32[]{:S(2)}) collective-permute-start(bf16[176,768]{1,0:T(8,128)(2,1)S(1)} %collective-permute-done.16), channel_id=1, source_target_pairs={{0,7},{1,0},{2,1},{3,2},{4,3},{5,4},{6,5},{7,6},{8,15},{9,8},{10,9... | collective-permute-start | bytes 811016 | tf_op jit(solution)/shard_map/ppermute | solution.py:125
  136.6 9.6 %collective-permute-start.23 = (bf16[8,176,768]{2,1,0:T(8,128)(2,1)}, bf16[8,176,768]{2,1,0:T(8,128)(2,1)}, u32[]{:S(2)}, u32[]{:S(2)}) collective-permute-start(bf16[8,176,768]{2,1,0:T(8,128)(2,1)} %fusion.25), channel_id=1, source_target_pairs={{0,128},{128,0},{1,129},{129,1},{2,130},{130,2},{3,131},{131,3},{4... | collective-permute-start | bytes 6488072 | tf_op jit(solution)/shard_map/ppermute | solution.py:231
  137.9 39.6 %all-to-all-start.2 = ((f32[16,32,768]{2,1,0:T(8,128)}), f32[16,32,768]{2,1,0:T(8,128)S(1)}, u32[]{:S(2)}, u32[]{:S(2)}) async-start(f32[16,32,768]{2,1,0:T(8,128)} %broadcast_in_dim.56), calls=%async_computation.2 | async-start | bytes 3145728 | tf_op jit(solution)/shard_map/all_to_all | solution.py:117
  (14 other events, 52.3 us)

commit v4 on v2

--- a/solution.py
+++ b/solution.py
@@ -85,7 +85,7 @@
         @pl.when(b < n // NB - 1)
         def _():
             u = jnp.where(lane >= o + NB, w[:, :n], 0.0)
-            s_ref[...] = s_ref[...] - dot3(u, w, ((0,), (0,)))
+            s_ref[NB:, NB:] = s_ref[NB:, NB:] - dot3(u[:, NB:], w[:, NB:], ((0,), (0,)))
 
         return carry
 
@@ -203,8 +203,9 @@
     col_all, lead_piece = lax.optimization_barrier((col_all, piece_col))
     col_feats, lead_feats = col_all[:, :cols_blk], col_all[:, cols_blk:]
 
-    piece_row = lax.ppermute(piece_col, axes, turn)
-    diag = piece_row[:, :PANEL]
+    both = jnp.concatenate([got[:, :cols_blk], *wire_halves(piece_col)], axis=0)
+    both = lax.ppermute(both, axes, turn)
+    diag = both[n_ex:, :PANEL]
     got_diag = sum(
         lax.ppermute(diag, "row", [(0, side * k)]) for k in range(1, side)
     )
@@ -214,15 +215,8 @@
         for k in range(1, side)
     )
     diag = jnp.where(lax.rem(row, side) == 0, diag, got_diag)
-    cut = rows_blk // 3
-    packed = [v[:, i : i + cut] for v in wire_halves(diag) for i in range(0, PANEL, cut)]
-    packed = jnp.concatenate(packed, axis=0)
-    group = 16 * (-(-packed.shape[0] // 48))
-    packed = jnp.pad(packed, ((0, 3 * group - packed.shape[0]), (0, 0)))
-    packed = jnp.concatenate([packed[i * group : (i + 1) * group] for i in range(3)], axis=1)
-
-    turned = lax.ppermute(got[:, :cols_blk], axes, turn)
-    mine = jnp.concatenate([turned, *wire_halves(piece_row), packed], axis=0)
+    diag = jnp.pad(diag, ((0, 0), (0, rows_blk - PANEL)))
+    mine = lax.optimization_barrier(jnp.concatenate([both, diag], axis=0))
     mine = gather_ring(mine, "col")
     lead_col = gather(lead_piece, "row").reshape(-1, cols_blk)
 
@@ -233,12 +227,8 @@
         row_feats.append(x[:, :n_ex].reshape(-1, rows_blk))
         c = x[:, n_ex : n_ex + 2 * piece].astype(f32)
         lead_row.append((c[:, :piece] + c[:, piece:]).reshape(-1, rows_blk))
-        d = x[:, n_ex + 2 * piece :]
-        d = jnp.concatenate([d[:, :, i * cut : (i + 1) * cut] for i in range(3)], axis=1)
-        d = d[:, : 2 * piece * PANEL // cut].astype(f32)
-        d = d[:, : d.shape[1] // 2] + d[:, d.shape[1] // 2 :]
-        d = jnp.concatenate([d[:, i : i + piece] for i in range(0, d.shape[1], piece)], axis=2)
-        diag.append(d.reshape(-1, PANEL))
+        d = x[:, n_ex + 2 * piece :, :PANEL].astype(f32)
+        diag.append((d[:, :piece] + d[:, piece:]).reshape(-1, PANEL))
     row_feats, lead_row, diag = (jnp.concatenate(v) for v in (row_feats, lead_row, diag))
 
     inv = inverse_factor(diag + gram(lead_feats, lead_feats))

time: 189 us -> 186 us (0.984)
  starting transfers between devices: 86 us -> 76.3 us
  local copies, waits for them, and re-layouts: 7.9 us -> 14.3 us
    ppermute x3, starting transfers between devices: 3.88 us -> 15.5 us  [per_device(): lax.ppermute(diag, 'row', [(side * j, side * j + k) for j in range(side)])]
    ppermute x8, starting transfers between devices: 24.5 us -> 13.5 us  [shift(): return lax.ppermute(v, axis, [(i, (i + k) % n) for i in range(n)])]
    all_to_all x1, waiting for transfers between devices: 2.19 us -> 7.76 us  [per_device(): got = lax.all_to_all(out, ('tp', 'col'), 0, 0, tiled=True)]
    ppermute x8, waiting for transfers between devices: 17.8 us -> 12.5 us  [shift(): return lax.ppermute(v, axis, [(i, (i + k) % n) for i in range(n)])]
    ppermute x3, starting transfers between devices: 9.73 us -> 5.63 us  [per_device(): lax.ppermute(diag, 'row', [(0, side * k)])]
    all_to_all x1, starting transfers between devices: 13.5 us -> 10 us  [per_device(): got = lax.all_to_all(out, ('tp', 'col'), 0, 0, tiled=True)]
    ppermute x2 -> x1, starting transfers between devices: 9.83 us -> 6.63 us  [per_device(): both = lax.ppermute(both, axes, turn)]
    dynamic_update_slice x6 -> x7, local copies, waits for them, and re-layouts: 0.14 us -> 2.1 us  [put(): return lax.dynamic_update_index_in_dim(out, v, lax.rem(me + n - k, n), 0)]
  transfers between devices with their start and end apart: 27 -> 26, of which waited for: 12 -> 7; matrix products, arithmetic and copies ran while one was open for 15% -> 18% of each run, Pallas kernels for 10% -> 10%
where the time goes in v4:
time: 186 us; the launch traced here: 185 us
  starting transfers between devices  76.3 us (41%)
  waiting for transfers between devices  44.1 us (24%)
  matrix products  26.3 us (14%)
  Pallas kernels  17.9 us (10%)
  local copies, waits for them, and re-layouts  14.3 us (8%)
  other arithmetic  4.56 us (2%)
    pallas_call x1, Pallas kernels, inverse_factor(): pl.pallas_call(factor_kernel, out_shape=jax.ShapeDtypeStruct((PANEL, PANE...  17.9 us
    ppermute x3, starting transfers between devices, per_device(): lax.ppermute(diag, 'row', [(side * j, side * j + k) for j in range(side)])  15.5 us
    ppermute x8, starting transfers between devices, shift(): return lax.ppermute(v, axis, [(i, (i + k) % n) for i in range(n)])  13.5 us
    dot_general x4, matrix products, gram(): lax.dot_general(a, b, (((0,), (0,)), ((), ())), preferred_element_type=f32)  13 us
    ppermute x8, waiting for transfers between devices, shift(): return lax.ppermute(v, axis, [(i, (i + k) % n) for i in range(n)])  12.5 us
    all_to_all x2, waiting for transfers between devices, gather(): lax.all_to_all(jnp.broadcast_to(x[None], (n,) + x.shape), axis, 0, 0, til...  11.9 us
    all_to_all x1, starting transfers between devices, per_device(): got = lax.all_to_all(out, ('tp', 'col'), 0, 0, tiled=True)  10 us
    ppermute x3, starting transfers between devices, per_device(): lax.ppermute(lead[k], 'row', [(0, side * k)])  9.83 us
  transfers between devices with their start and end apart: 26, of which 7 were waited for; matrix products, arithmetic and copies ran while one was open for 18% of the time, Pallas kernels for 10%

profile of v4, /device:TPU:1, one launch (start us, length us, event | category | flops | bytes accessed | tf_op | source)
XLA Modules:
  0.0 184.7 jit_solution(6000003074711912963)
XLA Ops:
  3.0 4.8 %collective-permute-start.1 = (f32[4,32,768]{2,1,0:T(8,128)}, f32[4,32,768]{2,1,0:T(8,128)}, u32[]{:S(2)}, u32[]{:S(2)}) collective-permute-start(f32[4,32,768]{2,1,0:T(8,128)} %bitcast.4), channel_id=1, source_target_pairs={{0,32},{1,33},{2,34},{3,35},{4,36},{5,37},{6,38},{7,39},{128,160},... | collective-permute-start | bytes 1179656 | tf_op jit(solution)/shard_map/ppermute | solution.py:169
  7.7 3.0 %collective-permute-start.2 = (f32[4,32,768]{2,1,0:T(8,128)S(1)}, f32[4,32,768]{2,1,0:T(8,128)}, u32[]{:S(2)}, u32[]{:S(2)}) collective-permute-start(f32[4,32,768]{2,1,0:T(8,128)S(1)} %bitcast.77), channel_id=1, source_target_pairs={{0,64},{1,65},{2,66},{3,67},{4,68},{5,69},{6,70},{7,71},{128,192},... | collective-permute-start | bytes 1179656 | tf_op jit(solution)/shard_map/ppermute | solution.py:169
  12.8 3.9 %fusion.24 = f32[1024,192]{0,1:T(8,128)S(1)} fusion(bf16[1024,2048]{1,0:T(8,128)(2,1)} %bitcast.79, bf16[2048,192]{0,1:T(8,128)(2,1)S(1)} %copy-done), kind=kOutput, calls=%fused_computation.67 | convolution fusion | flops 805306368 | bytes 5767168 | tf_op jit(solution)/shard_map/dot_general | solution.py:179
  19.3 4.1 %collective-permute-done.2 = f32[4,32,768]{2,1,0:T(8,128)} collective-permute-done((f32[4,32,768]{2,1,0:T(8,128)S(1)}, f32[4,32,768]{2,1,0:T(8,128)}, u32[]{:S(2)}, u32[]{:S(2)}) %collective-permute-start.2) | collective-permute-done | bytes 393248 | tf_op jit(solution)/shard_map/ppermute | solution.py:169
  30.9 10.0 %all-to-all-start = ((bf16[16,4,1280]{2,1,0:T(4,128)(2,1)}), bf16[16,4,1280]{2,1,0:T(4,128)(2,1)S(1)}, u32[]{:S(2)}, u32[]{:S(2)}) async-start(bf16[16,4,1280]{2,1,0:T(4,128)(2,1)} %copy.25), calls=%async_computation | async-start | bytes 327680 | tf_op jit(solution)/shard_map/all_to_all | solution.py:198
  41.0 7.8 %all-to-all-done = bf16[16,4,1280]{2,1,0:T(4,128)(2,1)S(1)} async-done(((bf16[16,4,1280]{2,1,0:T(4,128)(2,1)}), bf16[16,4,1280]{2,1,0:T(4,128)(2,1)S(1)}, u32[]{:S(2)}, u32[]{:S(2)}) %all-to-all-start) | async-done | bytes 163872 | tf_op jit(solution)/shard_map/all_to_all | solution.py:198
  48.9 6.6 %collective-permute-start.7 = (bf16[128,768]{1,0:T(8,128)(2,1)S(1)}, bf16[128,768]{1,0:T(8,128)(2,1)S(1)}, u32[]{:S(2)}, u32[]{:S(2)}) collective-permute-start(bf16[128,768]{1,0:T(8,128)(2,1)S(1)} %pad_maximum_fusion.4), channel_id=1, source_target_pairs={{0,0},{1,8},{2,16},{3,24},{4,32},{5,40},{6,48},{7,56},{128,64},{12... | collective-permute-start | bytes 589832 | tf_op jit(solution)/shard_map/ppermute | solution.py:207
  55.5 5.1 %collective-permute-done.7 = bf16[128,768]{1,0:T(8,128)(2,1)S(1)} collective-permute-done((bf16[128,768]{1,0:T(8,128)(2,1)S(1)}, bf16[128,768]{1,0:T(8,128)(2,1)S(1)}, u32[]{:S(2)}, u32[]{:S(2)}) %collective-permute-start.7) | collective-permute-done | bytes 196640 | tf_op jit(solution)/shard_map/ppermute | solution.py:207
  60.6 3.0 %collective-permute-start.10 = (bf16[64,512]{1,0:T(8,128)(2,1)S(1)}, bf16[64,512]{1,0:T(8,128)(2,1)S(1)}, u32[]{:S(2)}, u32[]{:S(2)}) collective-permute-start(bf16[64,512]{1,0:T(8,128)(2,1)S(1)} %slice.155), channel_id=1, source_target_pairs={{0,96},{1,97},{2,98},{3,99},{4,100},{5,101},{6,102},{7,103},{128,2... | collective-permute-start | bytes 196616 | tf_op jit(solution)/shard_map/ppermute | solution.py:210
  69.1 7.4 %collective-permute-start.12 = (bf16[64,512]{1,0:T(8,128)(2,1)S(1)}, bf16[64,512]{1,0:T(8,128)(2,1)S(1)}, u32[]{:S(2)}, u32[]{:S(2)}) collective-permute-start(bf16[64,512]{1,0:T(8,128)(2,1)S(1)} %add_select_fusion.2), channel_id=1, source_target_pairs={{0,16},{32,48},{64,80},{96,112},{1,17},{33,49},{65,81},{97,113},{2... | collective-permute-start | bytes 196616 | tf_op jit(solution)/shard_map/ppermute | solution.py:214
  76.5 6.8 %collective-permute-start.11 = (bf16[64,512]{1,0:T(8,128)(2,1)S(1)}, bf16[64,512]{1,0:T(8,128)(2,1)S(1)}, u32[]{:S(2)}, u32[]{:S(2)}) collective-permute-start(bf16[64,512]{1,0:T(8,128)(2,1)S(1)} %add_select_fusion.2), channel_id=1, source_target_pairs={{0,8},{32,40},{64,72},{96,104},{1,9},{33,41},{65,73},{97,105},{2,1... | collective-permute-start | bytes 196616 | tf_op jit(solution)/shard_map/ppermute | solution.py:214
  84.8 2.4 %collective-permute-start.14 = (bf16[192,768]{1,0:T(8,128)(2,1)S(1)}, bf16[192,768]{1,0:T(8,128)(2,1)}, u32[]{:S(2)}, u32[]{:S(2)}) collective-permute-start(bf16[192,768]{1,0:T(8,128)(2,1)S(1)} %fusion.14), channel_id=1, source_target_pairs={{0,2},{1,3},{2,4},{3,5},{4,6},{5,7},{6,0},{7,1},{8,10},{9,11},{10,... | collective-permute-start | bytes 884744 | tf_op jit(solution)/shard_map/ppermute | solution.py:125
  88.9 4.5 %all-to-all-start.1 = ((bf16[16,64,1280]{2,1,0:T(8,128)(2,1)}), bf16[16,64,1280]{2,1,0:T(8,128)(2,1)}, u32[]{:S(2)}, u32[]{:S(2)}) async-start(bf16[16,64,1280]{2,1,0:T(8,128)(2,1)} %broadcast_in_dim.55), calls=%async_computation.1 | async-start | bytes 5242880 | tf_op jit(solution)/shard_map/all_to_all | solution.py:117
  93.3 4.4 %collective-permute-start.17 = (bf16[192,768]{1,0:T(8,128)(2,1)S(1)}, bf16[192,768]{1,0:T(8,128)(2,1)S(1)}, u32[]{:S(2)}, u32[]{:S(2)}) collective-permute-start(bf16[192,768]{1,0:T(8,128)(2,1)S(1)} %fusion.14), channel_id=1, source_target_pairs={{0,7},{1,0},{2,1},{3,2},{4,3},{5,4},{6,5},{7,6},{8,15},{9,8},{10,9... | collective-permute-start | bytes 884744 | tf_op jit(solution)/shard_map/ppermute | solution.py:125
  98.9 3.9 %collective-permute-start.21 = (bf16[96,768]{1,0:T(8,128)(2,1)S(1)}, bf16[96,768]{1,0:T(8,128)(2,1)S(1)}, u32[]{:S(2)}, u32[]{:S(2)}) collective-permute-start(bf16[96,768]{1,0:T(8,128)(2,1)S(1)} %slice.157), channel_id=1, source_target_pairs={{0,6},{1,7},{2,0},{3,1},{4,2},{5,3},{6,4},{7,5},{8,14},{9,15},{10,... | collective-permute-start | bytes 442376 | tf_op jit(solution)/shard_map/ppermute | solution.py:125
  103.8 2.4 %collective-permute-start.19 = (bf16[192,768]{1,0:T(8,128)(2,1)}, bf16[192,768]{1,0:T(8,128)(2,1)S(1)}, u32[]{:S(2)}, u32[]{:S(2)}) collective-permute-start(bf16[192,768]{1,0:T(8,128)(2,1)} %collective-permute-done.15), channel_id=1, source_target_pairs={{0,7},{1,0},{2,1},{3,2},{4,3},{5,4},{6,5},{7,6},{8,15},{9,8},{10,9... | collective-permute-start | bytes 884744 | tf_op jit(solution)/shard_map/ppermute | solution.py:125
  108.6 12.4 %collective-permute-done.18 = bf16[192,768]{1,0:T(8,128)(2,1)S(1)} collective-permute-done((bf16[192,768]{1,0:T(8,128)(2,1)}, bf16[192,768]{1,0:T(8,128)(2,1)S(1)}, u32[]{:S(2)}, u32[]{:S(2)}) %collective-permute-start.18) | collective-permute-done | bytes 294944 | tf_op jit(solution)/shard_map/ppermute | solution.py:125
  122.6 11.9 %all-to-all-done.1 = bf16[16,64,1280]{2,1,0:T(8,128)(2,1)} async-done(((bf16[16,64,1280]{2,1,0:T(8,128)(2,1)}), bf16[16,64,1280]{2,1,0:T(8,128)(2,1)}, u32[]{:S(2)}, u32[]{:S(2)}) %all-to-all-start.1) | async-done | bytes 2621472 | tf_op jit(solution)/shard_map/all_to_all | solution.py:117
  135.8 4.4 %all-to-all-start.2 = ((f32[16,32,768]{2,1,0:T(8,128)}), f32[16,32,768]{2,1,0:T(8,128)}, u32[]{:S(2)}, u32[]{:S(2)}) async-start(f32[16,32,768]{2,1,0:T(8,128)} %broadcast_in_dim.56), calls=%async_computation.2 | async-start | bytes 3145728 | tf_op jit(solution)/shard_map/all_to_all | solution.py:117
  143.1 2.7 %convolution_add_fusion.a_ref = f32[512,512]{1,0:T(8,128)S(1)} fusion(f32[256,512]{1,0:T(8,128)S(1)} %bitcast.73, f32[256,512]{1,0:T(8,128)S(1)} %bitcast.74, bf16[1024,1280]{1,0:T(8,128)(2,1)} %bitcast.21), kind=kOutput, calls=%fused_computation.12 | convolution fusion | flops 537395200 | bytes 3145728 | tf_op jit(solution)/shard_map/dot_general | solution.py:144
  145.8 17.9 %inverse_factor.1 = f32[512,512]{1,0:T(8,128)S(1)} custom-call(f32[512,512]{1,0:T(8,128)S(1)} %convolution_add_fusion.a_ref), custom_call_target="tpu_custom_call" | custom-call | tf_op jit(solution)/shard_map/inverse_factor/pallas_call | solution.py:96
  170.8 4.7 %fusion.4 = f32[768,768]{1,0:T(8,128)} fusion(bf16[1024,1280]{1,0:T(8,128)(2,1)} %bitcast.21, bf16[512,768]{1,0:T(8,128)(2,1)} %bitcast.70, bf16[512,768]{1,0:T(8,128)(2,1)} %bitcast.72), kind=kOutput, calls=%fused_computation.10 | convolution fusion | flops 1211105280 | bytes 5505024 | tf_op jit(solution)/shard_map/dot_general | solution.py:144
  175.6 3.4 %bitcast_add_fusion = f32[512,768]{1,0:T(8,128)S(1)} fusion(f32[16,32,768]{2,1,0:T(8,128)} %all-to-all-done.2, bf16[1024,1280]{1,0:T(8,128)(2,1)} %bitcast.21), kind=kOutput, calls=%fused_computation.8 | convolution fusion | flops 805699584 | bytes 5767168 | tf_op jit(solution)/shard_map/dot_general | solution.py:144
  180.6 4.0 %add_subtract_fusion = f32[768,768]{1,0:T(8,128)} fusion(f32[768,768]{1,0:T(8,128)S(1)} %copy-done.1, f32[768,768]{1,0:T(8,128)S(1)} %copy-done.3, f32[512,768]{1,0:T(8,128)S(1)} %fusion, f32[512,768]{1,0:T(8,128)S(1)} %fusion.26), kind=kOutput, calls=%fused_computation | convolution fusion | flops 1813118976 | bytes 10223616 | tf_op jit(solution)/shard_map/dot_general | solution.py:240
  (97 shorter events, 41.9 us)
Async XLA Ops:
  3.0 16.3 %collective-permute-start.1 = (f32[4,32,768]{2,1,0:T(8,128)}, f32[4,32,768]{2,1,0:T(8,128)}, u32[]{:S(2)}, u32[]{:S(2)}) collective-permute-start(f32[4,32,768]{2,1,0:T(8,128)} %bitcast.4), channel_id=1, source_target_pairs={{0,32},{1,33},{2,34},{3,35},{4,36},{5,37},{6,38},{7,39},{128,160},... | collective-permute-start | bytes 1179656 | tf_op jit(solution)/shard_map/ppermute | solution.py:169
  7.7 15.7 %collective-permute-start.2 = (f32[4,32,768]{2,1,0:T(8,128)S(1)}, f32[4,32,768]{2,1,0:T(8,128)}, u32[]{:S(2)}, u32[]{:S(2)}) collective-permute-start(f32[4,32,768]{2,1,0:T(8,128)S(1)} %bitcast.77), channel_id=1, source_target_pairs={{0,64},{1,65},{2,66},{3,67},{4,68},{5,69},{6,70},{7,71},{128,192},... | collective-permute-start | bytes 1179656 | tf_op jit(solution)/shard_map/ppermute | solution.py:169
  10.8 12.6 %collective-permute-start.3 = (f32[4,32,768]{2,1,0:T(8,128)S(1)}, f32[4,32,768]{2,1,0:T(8,128)}, u32[]{:S(2)}, u32[]{:S(2)}) collective-permute-start(f32[4,32,768]{2,1,0:T(8,128)S(1)} %bitcast.76), channel_id=1, source_target_pairs={{0,96},{1,97},{2,98},{3,99},{4,100},{5,101},{6,102},{7,103},{128,2... | collective-permute-start | bytes 1179656 | tf_op jit(solution)/shard_map/ppermute | solution.py:169
  18.2 10.4 %collective-permute-start = (f32[4,128,256]{1,2,0:T(8,128)S(1)}, f32[4,128,256]{1,2,0:T(8,128)S(1)}, u32[]{:S(2)}, u32[]{:S(2)}) collective-permute-start(f32[4,128,256]{1,2,0:T(8,128)S(1)} %bitcast.75), channel_id=1, source_target_pairs={{0,128},{128,0},{1,129},{129,1},{2,130},{130,2},{3,131},{131,3},{4... | collective-permute-start | bytes 1572872 | tf_op jit(solution)/shard_map/ppermute | solution.py:186
  24.7 16.2 %collective-permute-start.5 = (f32[32,768]{1,0:T(8,128)S(1)}, f32[32,768]{1,0:T(8,128)S(1)}, u32[]{:S(2)}, u32[]{:S(2)}) collective-permute-start(f32[32,768]{1,0:T(8,128)S(1)} %get-tuple-element.28), channel_id=1, source_target_pairs={{0,16},{32,48},{64,80},{96,112},{1,17},{33,49},{65,81},{97,113},{2... | collective-permute-start | bytes 294920 | tf_op jit(solution)/shard_map/ppermute | solution.py:172
  26.0 14.9 %collective-permute-start.6 = (f32[32,768]{1,0:T(8,128)S(1)}, f32[32,768]{1,0:T(8,128)S(1)}, u32[]{:S(2)}, u32[]{:S(2)}) collective-permute-start(f32[32,768]{1,0:T(8,128)S(1)} %get-tuple-element.29), channel_id=1, source_target_pairs={{0,24},{32,56},{64,88},{96,120},{1,25},{33,57},{65,89},{97,121},{2... | collective-permute-start | bytes 294920 | tf_op jit(solution)/shard_map/ppermute | solution.py:172
  27.4 13.6 %collective-permute-start.4 = (f32[32,768]{1,0:T(8,128)S(1)}, f32[32,768]{1,0:T(8,128)S(1)}, u32[]{:S(2)}, u32[]{:S(2)}) collective-permute-start(f32[32,768]{1,0:T(8,128)S(1)} %get-tuple-element.30), channel_id=1, source_target_pairs={{0,8},{32,40},{64,72},{96,104},{1,9},{33,41},{65,73},{97,105},{2,1... | collective-permute-start | bytes 294920 | tf_op jit(solution)/shard_map/ppermute | solution.py:172
  30.9 17.8 %all-to-all-start = ((bf16[16,4,1280]{2,1,0:T(4,128)(2,1)}), bf16[16,4,1280]{2,1,0:T(4,128)(2,1)S(1)}, u32[]{:S(2)}, u32[]{:S(2)}) async-start(bf16[16,4,1280]{2,1,0:T(4,128)(2,1)} %copy.25), calls=%async_computation | async-start | bytes 327680 | tf_op jit(solution)/shard_map/all_to_all | solution.py:198
  48.9 11.7 %collective-permute-start.7 = (bf16[128,768]{1,0:T(8,128)(2,1)S(1)}, bf16[128,768]{1,0:T(8,128)(2,1)S(1)}, u32[]{:S(2)}, u32[]{:S(2)}) collective-permute-start(bf16[128,768]{1,0:T(8,128)(2,1)S(1)} %pad_maximum_fusion.4), channel_id=1, source_target_pairs={{0,0},{1,8},{2,16},{3,24},{4,32},{5,40},{6,48},{7,56},{128,64},{12... | collective-permute-start | bytes 589832 | tf_op jit(solution)/shard_map/ppermute | solution.py:207
  60.6 5.7 %collective-permute-start.10 = (bf16[64,512]{1,0:T(8,128)(2,1)S(1)}, bf16[64,512]{1,0:T(8,128)(2,1)S(1)}, u32[]{:S(2)}, u32[]{:S(2)}) collective-permute-start(bf16[64,512]{1,0:T(8,128)(2,1)S(1)} %slice.155), channel_id=1, source_target_pairs={{0,96},{1,97},{2,98},{3,99},{4,100},{5,101},{6,102},{7,103},{128,2... | collective-permute-start | bytes 196616 | tf_op jit(solution)/shard_map/ppermute | solution.py:210
  67.8 15.6 %collective-permute-start.13 = (bf16[64,512]{1,0:T(8,128)(2,1)S(1)}, bf16[64,512]{1,0:T(8,128)(2,1)S(1)}, u32[]{:S(2)}, u32[]{:S(2)}) collective-permute-start(bf16[64,512]{1,0:T(8,128)(2,1)S(1)} %add_select_fusion.2), channel_id=1, source_target_pairs={{0,24},{32,56},{64,88},{96,120},{1,25},{33,57},{65,89},{97,121},{2... | collective-permute-start | bytes 196616 | tf_op jit(solution)/shard_map/ppermute | solution.py:214
  69.1 14.3 %collective-permute-start.12 = (bf16[64,512]{1,0:T(8,128)(2,1)S(1)}, bf16[64,512]{1,0:T(8,128)(2,1)S(1)}, u32[]{:S(2)}, u32[]{:S(2)}) collective-permute-start(bf16[64,512]{1,0:T(8,128)(2,1)S(1)} %add_select_fusion.2), channel_id=1, source_target_pairs={{0,16},{32,48},{64,80},{96,112},{1,17},{33,49},{65,81},{97,113},{2... | collective-permute-start | bytes 196616 | tf_op jit(solution)/shard_map/ppermute | solution.py:214
  76.5 8.2 %collective-permute-start.11 = (bf16[64,512]{1,0:T(8,128)(2,1)S(1)}, bf16[64,512]{1,0:T(8,128)(2,1)S(1)}, u32[]{:S(2)}, u32[]{:S(2)}) collective-permute-start(bf16[64,512]{1,0:T(8,128)(2,1)S(1)} %add_select_fusion.2), channel_id=1, source_target_pairs={{0,8},{32,40},{64,72},{96,104},{1,9},{33,41},{65,73},{97,105},{2,1... | collective-permute-start | bytes 196616 | tf_op jit(solution)/shard_map/ppermute | solution.py:214
  84.7 13.3 %collective-permute-start.15 = (bf16[192,768]{1,0:T(8,128)(2,1)S(1)}, bf16[192,768]{1,0:T(8,128)(2,1)}, u32[]{:S(2)}, u32[]{:S(2)}) collective-permute-start(bf16[192,768]{1,0:T(8,128)(2,1)S(1)} %fusion.14), channel_id=1, source_target_pairs={{0,6},{1,7},{2,0},{3,1},{4,2},{5,3},{6,4},{7,5},{8,14},{9,15},{10,... | collective-permute-start | bytes 884744 | tf_op jit(solution)/shard_map/ppermute | solution.py:125
  84.8 18.0 %collective-permute-start.14 = (bf16[192,768]{1,0:T(8,128)(2,1)S(1)}, bf16[192,768]{1,0:T(8,128)(2,1)}, u32[]{:S(2)}, u32[]{:S(2)}) collective-permute-start(bf16[192,768]{1,0:T(8,128)(2,1)S(1)} %fusion.14), channel_id=1, source_target_pairs={{0,2},{1,3},{2,4},{3,5},{4,6},{5,7},{6,0},{7,1},{8,10},{9,11},{10,... | collective-permute-start | bytes 884744 | tf_op jit(solution)/shard_map/ppermute | solution.py:125
  88.9 45.6 %all-to-all-start.1 = ((bf16[16,64,1280]{2,1,0:T(8,128)(2,1)}), bf16[16,64,1280]{2,1,0:T(8,128)(2,1)}, u32[]{:S(2)}, u32[]{:S(2)}) async-start(bf16[16,64,1280]{2,1,0:T(8,128)(2,1)} %broadcast_in_dim.55), calls=%async_computation.1 | async-start | bytes 5242880 | tf_op jit(solution)/shard_map/all_to_all | solution.py:117
  93.3 15.2 %collective-permute-start.17 = (bf16[192,768]{1,0:T(8,128)(2,1)S(1)}, bf16[192,768]{1,0:T(8,128)(2,1)S(1)}, u32[]{:S(2)}, u32[]{:S(2)}) collective-permute-start(bf16[192,768]{1,0:T(8,128)(2,1)S(1)} %fusion.14), channel_id=1, source_target_pairs={{0,7},{1,0},{2,1},{3,2},{4,3},{5,4},{6,5},{7,6},{8,15},{9,8},{10,9... | collective-permute-start | bytes 884744 | tf_op jit(solution)/shard_map/ppermute | solution.py:125
  97.8 10.4 %collective-permute-start.16 = (bf16[192,768]{1,0:T(8,128)(2,1)S(1)}, bf16[192,768]{1,0:T(8,128)(2,1)S(1)}, u32[]{:S(2)}, u32[]{:S(2)}) collective-permute-start(bf16[192,768]{1,0:T(8,128)(2,1)S(1)} %fusion.14), channel_id=1, source_target_pairs={{0,1},{1,2},{2,3},{3,4},{4,5},{5,6},{6,7},{7,0},{8,9},{9,10},{10,1... | collective-permute-start | bytes 884744 | tf_op jit(solution)/shard_map/ppermute | solution.py:125
  98.9 22.2 %collective-permute-start.21 = (bf16[96,768]{1,0:T(8,128)(2,1)S(1)}, bf16[96,768]{1,0:T(8,128)(2,1)S(1)}, u32[]{:S(2)}, u32[]{:S(2)}) collective-permute-start(bf16[96,768]{1,0:T(8,128)(2,1)S(1)} %slice.157), channel_id=1, source_target_pairs={{0,6},{1,7},{2,0},{3,1},{4,2},{5,3},{6,4},{7,5},{8,14},{9,15},{10,... | collective-permute-start | bytes 442376 | tf_op jit(solution)/shard_map/ppermute | solution.py:125
  103.7 17.4 %collective-permute-start.20 = (bf16[96,768]{1,0:T(8,128)(2,1)S(1)}, bf16[96,768]{1,0:T(8,128)(2,1)S(1)}, u32[]{:S(2)}, u32[]{:S(2)}) collective-permute-start(bf16[96,768]{1,0:T(8,128)(2,1)S(1)} %slice.156), channel_id=1, source_target_pairs={{0,2},{1,3},{2,4},{3,5},{4,6},{5,7},{6,0},{7,1},{8,10},{9,11},{10,... | collective-permute-start | bytes 442376 | tf_op jit(solution)/shard_map/ppermute | solution.py:125
  103.8 17.2 %collective-permute-start.19 = (bf16[192,768]{1,0:T(8,128)(2,1)}, bf16[192,768]{1,0:T(8,128)(2,1)S(1)}, u32[]{:S(2)}, u32[]{:S(2)}) collective-permute-start(bf16[192,768]{1,0:T(8,128)(2,1)} %collective-permute-done.15), channel_id=1, source_target_pairs={{0,7},{1,0},{2,1},{3,2},{4,3},{5,4},{6,5},{7,6},{8,15},{9,8},{10,9... | collective-permute-start | bytes 884744 | tf_op jit(solution)/shard_map/ppermute | solution.py:125
  108.2 12.8 %collective-permute-start.18 = (bf16[192,768]{1,0:T(8,128)(2,1)}, bf16[192,768]{1,0:T(8,128)(2,1)S(1)}, u32[]{:S(2)}, u32[]{:S(2)}) collective-permute-start(bf16[192,768]{1,0:T(8,128)(2,1)} %collective-permute-done.14), channel_id=1, source_target_pairs={{0,1},{1,2},{2,3},{3,4},{4,5},{5,6},{6,7},{7,0},{8,9},{9,10},{10,1... | collective-permute-start | bytes 884744 | tf_op jit(solution)/shard_map/ppermute | solution.py:125
  121.1 19.1 %collective-permute-start.22 = (bf16[8,192,768]{2,1,0:T(8,128)(2,1)S(1)}, bf16[8,192,768]{2,1,0:T(8,128)(2,1)}, u32[]{:S(2)}, u32[]{:S(2)}) collective-permute-start(bf16[8,192,768]{2,1,0:T(8,128)(2,1)S(1)} %fusion.15), channel_id=1, source_target_pairs={{0,128},{128,0},{1,129},{129,1},{2,130},{130,2},{3,131},{131,3},{4... | collective-permute-start | bytes 7077896 | tf_op jit(solution)/shard_map/ppermute | solution.py:223
  135.8 39.7 %all-to-all-start.2 = ((f32[16,32,768]{2,1,0:T(8,128)}), f32[16,32,768]{2,1,0:T(8,128)}, u32[]{:S(2)}, u32[]{:S(2)}) async-start(f32[16,32,768]{2,1,0:T(8,128)} %broadcast_in_dim.56), calls=%async_computation.2 | async-start | bytes 3145728 | tf_op jit(solution)/shard_map/all_to_all | solution.py:117
  (9 other events, 73.9 us)

commit v5 on v4

--- a/solution.py
+++ b/solution.py
@@ -203,9 +203,10 @@
     col_all, lead_piece = lax.optimization_barrier((col_all, piece_col))
     col_feats, lead_feats = col_all[:, :cols_blk], col_all[:, cols_blk:]
 
-    both = jnp.concatenate([got[:, :cols_blk], *wire_halves(piece_col)], axis=0)
+    halved = jnp.concatenate(wire_halves(piece_col), axis=0)
+    both = jnp.concatenate([got[:, :cols_blk], halved], axis=1)
     both = lax.ppermute(both, axes, turn)
-    diag = both[n_ex:, :PANEL]
+    diag = both[:, cols_blk : cols_blk + PANEL]
     got_diag = sum(
         lax.ppermute(diag, "row", [(0, side * k)]) for k in range(1, side)
     )
@@ -215,25 +216,27 @@
         for k in range(1, side)
     )
     diag = jnp.where(lax.rem(row, side) == 0, diag, got_diag)
-    diag = jnp.pad(diag, ((0, 0), (0, rows_blk - PANEL)))
-    mine = lax.optimization_barrier(jnp.concatenate([both, diag], axis=0))
+    mine = lax.optimization_barrier(jnp.concatenate([both, diag], axis=1))
     mine = gather_ring(mine, "col")
     lead_col = gather(lead_piece, "row").reshape(-1, cols_blk)
 
+    gram_lead = gram(lead_feats, col_all)
+    mine, gram_lead = lax.optimization_barrier((mine, gram_lead))
     theirs = lax.ppermute(mine, "tp", swap)
     low, high = jnp.where(first, mine, theirs), jnp.where(first, theirs, mine)
     row_feats, lead_row, diag = [], [], []
     for x in (low, high):
-        row_feats.append(x[:, :n_ex].reshape(-1, rows_blk))
-        c = x[:, n_ex : n_ex + 2 * piece].astype(f32)
-        lead_row.append((c[:, :piece] + c[:, piece:]).reshape(-1, rows_blk))
-        d = x[:, n_ex + 2 * piece :, :PANEL].astype(f32)
-        diag.append((d[:, :piece] + d[:, piece:]).reshape(-1, PANEL))
+        row_feats.append(x[:, :, :rows_blk].reshape(-1, rows_blk))
+        x = x[:, :, rows_blk:].astype(f32)
+        x = x[:, :piece] + x[:, piece:]
+        lead_row.append(x[:, :, :rows_blk].reshape(-1, rows_blk))
+        diag.append(x[:, :, rows_blk:].reshape(-1, PANEL))
     row_feats, lead_row, diag = (jnp.concatenate(v) for v in (row_feats, lead_row, diag))
 
-    inv = inverse_factor(diag + gram(lead_feats, lead_feats))
+    inv = inverse_factor(diag + gram_lead[:, cols_blk:])
+    inv, lead_col = lax.optimization_barrier((inv, lead_col))
     panel_row = jnp.dot(inv, lead_row + gram(lead_feats, row_feats), precision=HIGH)
-    panel_col = jnp.dot(inv, lead_col + gram(lead_feats, col_feats), precision=HIGH)
+    panel_col = jnp.dot(inv, lead_col + gram_lead[:, :cols_blk], precision=HIGH)
     trailing = (
         curvature
         + gram(row_feats, col_feats)

time: 186 us -> 179 us (0.962)
  waiting for transfers between devices: 44.1 us -> 31.4 us
  other arithmetic: 4.56 us -> 7.23 us
    all_to_all x2, waiting for transfers between devices: 11.9 us -> 1.71 us  [gather(): lax.all_to_all(jnp.broadcast_to(x[None], (n,) + x.shape), axis, 0, 0, til...]
    dot_general x4 -> x3, matrix products: 13 us -> 8.07 us  [gram(): lax.dot_general(a, b, (((0,), (0,)), ((), ())), preferred_element_type=f32)]
    dynamic_update_slice x7, local copies, waits for them, and re-layouts: 2.1 us -> 5.03 us  [put(): return lax.dynamic_update_index_in_dim(out, v, lax.rem(me + n - k, n), 0)]
    dot_general x1, matrix products: 1.54 us -> 4.24 us  [per_device(): panel_col = jnp.dot(inv, lead_col + gram_lead[:, :cols_blk], precision=HIGH)]
    dot_general x1, matrix products: 4.02 us -> 6.68 us  [per_device(): lax.dot_general(panel_row, panel_col, (((0,), (0,)), ((), ())), precision...]
  transfers between devices with their start and end apart: 26 -> 26, of which waited for: 7 -> 8; matrix products, arithmetic and copies ran while one was open for 18% -> 17% of each run, Pallas kernels for 10% -> 10%
where the time goes in v5:
time: 179 us; the launch traced here: 178 us
  starting transfers between devices  78.1 us (44%)
  waiting for transfers between devices  31.4 us (18%)
  matrix products  26.6 us (15%)
  Pallas kernels  17.9 us (10%)
  local copies, waits for them, and re-layouts  16.1 us (9%)
  other arithmetic  7.23 us (4%)
    pallas_call x1, Pallas kernels, inverse_factor(): pl.pallas_call(factor_kernel, out_shape=jax.ShapeDtypeStruct((PANEL, PANE...  17.9 us
    ppermute x3, starting transfers between devices, per_device(): lax.ppermute(diag, 'row', [(side * j, side * j + k) for j in range(side)])  15.9 us
    ppermute x8, starting transfers between devices, shift(): return lax.ppermute(v, axis, [(i, (i + k) % n) for i in range(n)])  13.5 us
    ppermute x8, waiting for transfers between devices, shift(): return lax.ppermute(v, axis, [(i, (i + k) % n) for i in range(n)])  11.7 us
    all_to_all x2, starting transfers between devices, gather(): lax.all_to_all(jnp.broadcast_to(x[None], (n,) + x.shape), axis, 0, 0, til...  10.7 us
    all_to_all x1, starting transfers between devices, per_device(): got = lax.all_to_all(out, ('tp', 'col'), 0, 0, tiled=True)  10 us
    ppermute x3, starting transfers between devices, per_device(): lax.ppermute(lead[k], 'row', [(0, side * k)])  9.85 us
    dot_general x3, matrix products, gram(): lax.dot_general(a, b, (((0,), (0,)), ((), ())), preferred_element_type=f32)  8.07 us
  transfers between devices with their start and end apart: 26, of which 8 were waited for; matrix products, arithmetic and copies ran while one was open for 17% of the time, Pallas kernels for 10%

profile of v5, /device:TPU:1, one launch (start us, length us, event | category | flops | bytes accessed | tf_op | source)
XLA Modules:
  0.0 178.5 jit_solution(2000401391995120650)
XLA Ops:
  2.2 4.8 %collective-permute-start.1 = (f32[4,32,768]{2,1,0:T(8,128)S(1)}, f32[4,32,768]{2,1,0:T(8,128)}, u32[]{:S(2)}, u32[]{:S(2)}) collective-permute-start(f32[4,32,768]{2,1,0:T(8,128)S(1)} %bitcast.81), channel_id=1, source_target_pairs={{0,32},{1,33},{2,34},{3,35},{4,36},{5,37},{6,38},{7,39},{128,160},... | collective-permute-start | bytes 1179656 | tf_op jit(solution)/shard_map/ppermute | solution.py:169
  7.0 3.0 %collective-permute-start.2 = (f32[4,32,768]{2,1,0:T(8,128)S(1)}, f32[4,32,768]{2,1,0:T(8,128)}, u32[]{:S(2)}, u32[]{:S(2)}) collective-permute-start(f32[4,32,768]{2,1,0:T(8,128)S(1)} %bitcast.80), channel_id=1, source_target_pairs={{0,64},{1,65},{2,66},{3,67},{4,68},{5,69},{6,70},{7,71},{128,192},... | collective-permute-start | bytes 1179656 | tf_op jit(solution)/shard_map/ppermute | solution.py:169
  12.1 3.9 %fusion.24 = f32[1024,192]{0,1:T(8,128)S(1)} fusion(bf16[1024,2048]{1,0:T(8,128)(2,1)} %bitcast.83, bf16[2048,192]{0,1:T(8,128)(2,1)S(1)} %copy-done), kind=kOutput, calls=%fused_computation.62 | convolution fusion | flops 805306368 | bytes 5767168 | tf_op jit(solution)/shard_map/dot_general | solution.py:179
  18.6 3.9 %collective-permute-done.2 = f32[4,32,768]{2,1,0:T(8,128)} collective-permute-done((f32[4,32,768]{2,1,0:T(8,128)S(1)}, f32[4,32,768]{2,1,0:T(8,128)}, u32[]{:S(2)}, u32[]{:S(2)}) %collective-permute-start.2) | collective-permute-done | bytes 393248 | tf_op jit(solution)/shard_map/ppermute | solution.py:169
  30.0 10.0 %all-to-all-start = ((bf16[16,4,1280]{2,1,0:T(4,128)(2,1)}), bf16[16,4,1280]{2,1,0:T(4,128)(2,1)S(1)}, u32[]{:S(2)}, u32[]{:S(2)}) async-start(bf16[16,4,1280]{2,1,0:T(4,128)(2,1)} %copy.25), calls=%async_computation | async-start | bytes 327680 | tf_op jit(solution)/shard_map/all_to_all | solution.py:198
  40.1 7.8 %all-to-all-done = bf16[16,4,1280]{2,1,0:T(4,128)(2,1)S(1)} async-done(((bf16[16,4,1280]{2,1,0:T(4,128)(2,1)}), bf16[16,4,1280]{2,1,0:T(4,128)(2,1)S(1)}, u32[]{:S(2)}, u32[]{:S(2)}) %all-to-all-start) | async-done | bytes 163872 | tf_op jit(solution)/shard_map/all_to_all | solution.py:198
  47.9 6.6 %collective-permute-start.7 = (bf16[64,1536]{1,0:T(8,128)(2,1)S(1)}, bf16[64,1536]{1,0:T(8,128)(2,1)S(1)}, u32[]{:S(2)}, u32[]{:S(2)}) collective-permute-start(bf16[64,1536]{1,0:T(8,128)(2,1)S(1)} %maximum_maximum_fusion), channel_id=1, source_target_pairs={{0,0},{1,8},{2,16},{3,24},{4,32},{5,40},{6,48},{7,56},{128,64},{12... | collective-permute-start | bytes 589832 | tf_op jit(solution)/shard_map/ppermute | solution.py:208
  54.5 4.6 %collective-permute-done.7 = bf16[64,1536]{1,0:T(8,128)(2,1)S(1)} collective-permute-done((bf16[64,1536]{1,0:T(8,128)(2,1)S(1)}, bf16[64,1536]{1,0:T(8,128)(2,1)S(1)}, u32[]{:S(2)}, u32[]{:S(2)}) %collective-permute-start.7) | collective-permute-done | bytes 196640 | tf_op jit(solution)/shard_map/ppermute | solution.py:208
  59.2 3.9 %collective-permute-start.10 = (bf16[64,512]{1,0:T(8,128)(2,1)S(1)}, bf16[64,512]{1,0:T(8,128)(2,1)S(1)}, u32[]{:S(2)}, u32[]{:S(2)}) collective-permute-start(bf16[64,512]{1,0:T(8,128)(2,1)S(1)} %slice.155), channel_id=1, source_target_pairs={{0,96},{1,97},{2,98},{3,99},{4,100},{5,101},{6,102},{7,103},{128,2... | collective-permute-start | bytes 196616 | tf_op jit(solution)/shard_map/ppermute | solution.py:211
  67.3 13.3 %collective-permute-start.11 = (bf16[64,512]{1,0:T(8,128)(2,1)S(1)}, bf16[64,512]{1,0:T(8,128)(2,1)S(1)}, u32[]{:S(2)}, u32[]{:S(2)}) collective-permute-start(bf16[64,512]{1,0:T(8,128)(2,1)S(1)} %add_select_fusion.2), channel_id=1, source_target_pairs={{0,8},{32,40},{64,72},{96,104},{1,9},{33,41},{65,73},{97,105},{2,1... | collective-permute-start | bytes 196616 | tf_op jit(solution)/shard_map/ppermute | solution.py:215
  85.1 3.7 %all-to-all-start.1 = ((bf16[16,64,1280]{2,1,0:T(8,128)(2,1)}), bf16[16,64,1280]{2,1,0:T(8,128)(2,1)S(1)}, u32[]{:S(2)}, u32[]{:S(2)}) async-start(bf16[16,64,1280]{2,1,0:T(8,128)(2,1)} %broadcast_in_dim.55), calls=%async_computation.1 | async-start | bytes 5242880 | tf_op jit(solution)/shard_map/all_to_all | solution.py:117
  89.0 3.6 %collective-permute-start.15 = (bf16[64,2048]{1,0:T(8,128)(2,1)S(1)}, bf16[64,2048]{1,0:T(8,128)(2,1)S(1)}, u32[]{:S(2)}, u32[]{:S(2)}) collective-permute-start(bf16[64,2048]{1,0:T(8,128)(2,1)S(1)} %pad_maximum_fusion.4), channel_id=1, source_target_pairs={{0,6},{1,7},{2,0},{3,1},{4,2},{5,3},{6,4},{7,5},{8,14},{9,15},{10,... | collective-permute-start | bytes 786440 | tf_op jit(solution)/shard_map/ppermute | solution.py:125
  97.5 5.9 %collective-permute-done.14 = bf16[64,2048]{1,0:T(8,128)(2,1)S(1)} collective-permute-done((bf16[64,2048]{1,0:T(8,128)(2,1)S(1)}, bf16[64,2048]{1,0:T(8,128)(2,1)S(1)}, u32[]{:S(2)}, u32[]{:S(2)}) %collective-permute-start.14) | collective-permute-done | bytes 262176 | tf_op jit(solution)/shard_map/ppermute | solution.py:125
  103.6 3.6 %collective-permute-start.21 = (bf16[32,2048]{1,0:T(8,128)(2,1)S(1)}, bf16[32,2048]{1,0:T(8,128)(2,1)S(1)}, u32[]{:S(2)}, u32[]{:S(2)}) collective-permute-start(bf16[32,2048]{1,0:T(8,128)(2,1)S(1)} %slice.157), channel_id=1, source_target_pairs={{0,6},{1,7},{2,0},{3,1},{4,2},{5,3},{6,4},{7,5},{8,14},{9,15},{10,... | collective-permute-start | bytes 393224 | tf_op jit(solution)/shard_map/ppermute | solution.py:125
  109.1 3.1 %collective-permute-start.19 = (bf16[64,2048]{1,0:T(8,128)(2,1)S(1)}, bf16[64,2048]{1,0:T(8,128)(2,1)S(1)}, u32[]{:S(2)}, u32[]{:S(2)}) collective-permute-start(bf16[64,2048]{1,0:T(8,128)(2,1)S(1)} %collective-permute-done.15), channel_id=1, source_target_pairs={{0,7},{1,0},{2,1},{3,2},{4,3},{5,4},{6,5},{7,6},{8,15},{9,8},{10,9... | collective-permute-start | bytes 786440 | tf_op jit(solution)/shard_map/ppermute | solution.py:125
  113.6 5.6 %collective-permute-done.18 = bf16[64,2048]{1,0:T(8,128)(2,1)S(1)} collective-permute-done((bf16[64,2048]{1,0:T(8,128)(2,1)S(1)}, bf16[64,2048]{1,0:T(8,128)(2,1)S(1)}, u32[]{:S(2)}, u32[]{:S(2)}) %collective-permute-start.18) | collective-permute-done | bytes 262176 | tf_op jit(solution)/shard_map/ppermute | solution.py:125
  123.3 3.0 %fusion.11 = f32[512,1280]{1,0:T(8,128)} fusion(bf16[1024,1280]{1,0:T(8,128)(2,1)S(1)} %bitcast.64), kind=kOutput, calls=%fused_computation.24 | convolution fusion | flops 1342177280 | bytes 6291456 | tf_op jit(solution)/shard_map/dot_general | solution.py:144
  127.7 7.0 %all-to-all-start.2 = ((f32[16,32,768]{2,1,0:T(8,128)}), f32[16,32,768]{2,1,0:T(8,128)S(1)}, u32[]{:S(2)}, u32[]{:S(2)}) async-start(f32[16,32,768]{2,1,0:T(8,128)} %broadcast_in_dim.56), calls=%async_computation.2 | async-start | bytes 3145728 | tf_op jit(solution)/shard_map/all_to_all | solution.py:117
  134.7 2.5 %broadcast_select_fusion.1 = (bf16[8,64,2048]{2,1,0:T(8,128)(2,1)S(1)}, bf16[8,64,2048]{2,1,0:T(8,128)(2,1)S(1)}) fusion(bf16[8,64,2048]{2,1,0:T(8,128)(2,1)} %fusion.15, bf16[8,64,2048]{2,1,0:T(8,128)(2,1)} %collective-permute-done.22, pred[]{:T(512)S(6)} %eq.11), kind=kLoop, calls=%fused_computation.2 | loop fusion | flops 2097152 | bytes 8388609 | tf_op jit(solution)/shard_map/jit(_where)/select_n | solution.py:226
  141.9 17.9 %inverse_factor.1 = f32[512,512]{1,0:T(8,128)S(1)} custom-call(f32[512,512]{1,0:T(8,128)S(1)} %maximum_add_fusion.2.a_ref), custom_call_target="tpu_custom_call" | custom-call | tf_op jit(solution)/shard_map/inverse_factor/pallas_call | solution.py:96
  159.8 2.2 %fusion.9 = f32[512,768]{1,0:T(8,128)} fusion(bf16[512,768]{1,0:T(8,128)(2,1)S(1)} %bitcast.76, bf16[512,768]{1,0:T(8,128)(2,1)S(1)} %bitcast.74, bf16[1024,1280]{1,0:T(8,128)(2,1)S(1)} %bitcast.65), kind=kOutput, calls=%fused_computation.22 | convolution fusion | flops 808452096 | bytes 4194304 | tf_op jit(solution)/shard_map/dot_general | solution.py:144
  162.0 2.8 %fusion.6 = f32[768,768]{1,0:T(8,128)} fusion(bf16[1024,1280]{1,0:T(8,128)(2,1)S(1)} %bitcast.66, bf16[512,768]{1,0:T(8,128)(2,1)S(1)} %bitcast.77, bf16[512,768]{1,0:T(8,128)(2,1)S(1)} %bitcast.75), kind=kOutput, calls=%fused_computation.11 | convolution fusion | flops 1211105280 | bytes 5505024 | tf_op jit(solution)/shard_map/dot_general | solution.py:144
  164.8 4.2 %fusion.3 = f32[512,768]{1,0:T(8,128)} fusion(f32[512,512]{1,0:T(8,128)S(1)} %inverse_factor.1, f32[512,768]{1,0:T(8,128)S(1)} %bitcast.68, f32[512,1280]{1,0:T(8,128)} %fusion.11), kind=kOutput, calls=%fused_computation.8 | convolution fusion | flops 1208352768 | bytes 5767168 | tf_op jit(solution)/shard_map/dot_general | solution.py:239
  171.8 6.7 %add_subtract_fusion = f32[768,768]{1,0:T(8,128)} fusion(f32[768,768]{1,0:T(8,128)} %param.9, f32[768,768]{1,0:T(8,128)} %fusion.6, f32[512,768]{1,0:T(8,128)S(1)} %fusion, f32[512,768]{1,0:T(8,128)} %fusion.3), kind=kOutput, calls=%fused_computation | convolution fusion | flops 1813118976 | bytes 10223616 | tf_op jit(solution)/shard_map/dot_general | solution.py:243
  (106 shorter events, 43.7 us)
Async XLA Ops:
  2.2 16.4 %collective-permute-start.1 = (f32[4,32,768]{2,1,0:T(8,128)S(1)}, f32[4,32,768]{2,1,0:T(8,128)}, u32[]{:S(2)}, u32[]{:S(2)}) collective-permute-start(f32[4,32,768]{2,1,0:T(8,128)S(1)} %bitcast.81), channel_id=1, source_target_pairs={{0,32},{1,33},{2,34},{3,35},{4,36},{5,37},{6,38},{7,39},{128,160},... | collective-permute-start | bytes 1179656 | tf_op jit(solution)/shard_map/ppermute | solution.py:169
  7.0 15.4 %collective-permute-start.2 = (f32[4,32,768]{2,1,0:T(8,128)S(1)}, f32[4,32,768]{2,1,0:T(8,128)}, u32[]{:S(2)}, u32[]{:S(2)}) collective-permute-start(f32[4,32,768]{2,1,0:T(8,128)S(1)} %bitcast.80), channel_id=1, source_target_pairs={{0,64},{1,65},{2,66},{3,67},{4,68},{5,69},{6,70},{7,71},{128,192},... | collective-permute-start | bytes 1179656 | tf_op jit(solution)/shard_map/ppermute | solution.py:169
  10.0 12.4 %collective-permute-start.3 = (f32[4,32,768]{2,1,0:T(8,128)S(1)}, f32[4,32,768]{2,1,0:T(8,128)}, u32[]{:S(2)}, u32[]{:S(2)}) collective-permute-start(f32[4,32,768]{2,1,0:T(8,128)S(1)} %bitcast.79), channel_id=1, source_target_pairs={{0,96},{1,97},{2,98},{3,99},{4,100},{5,101},{6,102},{7,103},{128,2... | collective-permute-start | bytes 1179656 | tf_op jit(solution)/shard_map/ppermute | solution.py:169
  17.5 10.2 %collective-permute-start = (f32[4,128,256]{1,2,0:T(8,128)S(1)}, f32[4,128,256]{1,2,0:T(8,128)S(1)}, u32[]{:S(2)}, u32[]{:S(2)}) collective-permute-start(f32[4,128,256]{1,2,0:T(8,128)S(1)} %bitcast.78), channel_id=1, source_target_pairs={{0,128},{128,0},{1,129},{129,1},{2,130},{130,2},{3,131},{131,3},{4... | collective-permute-start | bytes 1572872 | tf_op jit(solution)/shard_map/ppermute | solution.py:186
  23.8 16.2 %collective-permute-start.4 = (f32[32,768]{1,0:T(8,128)S(1)}, f32[32,768]{1,0:T(8,128)S(1)}, u32[]{:S(2)}, u32[]{:S(2)}) collective-permute-start(f32[32,768]{1,0:T(8,128)S(1)} %get-tuple-element.34), channel_id=1, source_target_pairs={{0,8},{32,40},{64,72},{96,104},{1,9},{33,41},{65,73},{97,105},{2,1... | collective-permute-start | bytes 294920 | tf_op jit(solution)/shard_map/ppermute | solution.py:172
  25.1 14.9 %collective-permute-start.5 = (f32[32,768]{1,0:T(8,128)S(1)}, f32[32,768]{1,0:T(8,128)S(1)}, u32[]{:S(2)}, u32[]{:S(2)}) collective-permute-start(f32[32,768]{1,0:T(8,128)S(1)} %get-tuple-element.32), channel_id=1, source_target_pairs={{0,16},{32,48},{64,80},{96,112},{1,17},{33,49},{65,81},{97,113},{2... | collective-permute-start | bytes 294920 | tf_op jit(solution)/shard_map/ppermute | solution.py:172
  26.4 13.6 %collective-permute-start.6 = (f32[32,768]{1,0:T(8,128)S(1)}, f32[32,768]{1,0:T(8,128)S(1)}, u32[]{:S(2)}, u32[]{:S(2)}) collective-permute-start(f32[32,768]{1,0:T(8,128)S(1)} %get-tuple-element.33), channel_id=1, source_target_pairs={{0,24},{32,56},{64,88},{96,120},{1,25},{33,57},{65,89},{97,121},{2... | collective-permute-start | bytes 294920 | tf_op jit(solution)/shard_map/ppermute | solution.py:172
  30.0 17.8 %all-to-all-start = ((bf16[16,4,1280]{2,1,0:T(4,128)(2,1)}), bf16[16,4,1280]{2,1,0:T(4,128)(2,1)S(1)}, u32[]{:S(2)}, u32[]{:S(2)}) async-start(bf16[16,4,1280]{2,1,0:T(4,128)(2,1)} %copy.25), calls=%async_computation | async-start | bytes 327680 | tf_op jit(solution)/shard_map/all_to_all | solution.py:198
  47.9 11.3 %collective-permute-start.7 = (bf16[64,1536]{1,0:T(8,128)(2,1)S(1)}, bf16[64,1536]{1,0:T(8,128)(2,1)S(1)}, u32[]{:S(2)}, u32[]{:S(2)}) collective-permute-start(bf16[64,1536]{1,0:T(8,128)(2,1)S(1)} %maximum_maximum_fusion), channel_id=1, source_target_pairs={{0,0},{1,8},{2,16},{3,24},{4,32},{5,40},{6,48},{7,56},{128,64},{12... | collective-permute-start | bytes 589832 | tf_op jit(solution)/shard_map/ppermute | solution.py:208
  59.2 6.5 %collective-permute-start.10 = (bf16[64,512]{1,0:T(8,128)(2,1)S(1)}, bf16[64,512]{1,0:T(8,128)(2,1)S(1)}, u32[]{:S(2)}, u32[]{:S(2)}) collective-permute-start(bf16[64,512]{1,0:T(8,128)(2,1)S(1)} %slice.155), channel_id=1, source_target_pairs={{0,96},{1,97},{2,98},{3,99},{4,100},{5,101},{6,102},{7,103},{128,2... | collective-permute-start | bytes 196616 | tf_op jit(solution)/shard_map/ppermute | solution.py:211
  67.3 21.5 %collective-permute-start.11 = (bf16[64,512]{1,0:T(8,128)(2,1)S(1)}, bf16[64,512]{1,0:T(8,128)(2,1)S(1)}, u32[]{:S(2)}, u32[]{:S(2)}) collective-permute-start(bf16[64,512]{1,0:T(8,128)(2,1)S(1)} %add_select_fusion.2), channel_id=1, source_target_pairs={{0,8},{32,40},{64,72},{96,104},{1,9},{33,41},{65,73},{97,105},{2,1... | collective-permute-start | bytes 196616 | tf_op jit(solution)/shard_map/ppermute | solution.py:215
  80.7 8.1 %collective-permute-start.12 = (bf16[64,512]{1,0:T(8,128)(2,1)S(1)}, bf16[64,512]{1,0:T(8,128)(2,1)S(1)}, u32[]{:S(2)}, u32[]{:S(2)}) collective-permute-start(bf16[64,512]{1,0:T(8,128)(2,1)S(1)} %add_select_fusion.2), channel_id=1, source_target_pairs={{0,16},{32,48},{64,80},{96,112},{1,17},{33,49},{65,81},{97,113},{2... | collective-permute-start | bytes 196616 | tf_op jit(solution)/shard_map/ppermute | solution.py:215
  82.0 6.9 %collective-permute-start.13 = (bf16[64,512]{1,0:T(8,128)(2,1)S(1)}, bf16[64,512]{1,0:T(8,128)(2,1)S(1)}, u32[]{:S(2)}, u32[]{:S(2)}) collective-permute-start(bf16[64,512]{1,0:T(8,128)(2,1)S(1)} %add_select_fusion.2), channel_id=1, source_target_pairs={{0,24},{32,56},{64,88},{96,120},{1,25},{33,57},{65,89},{97,121},{2... | collective-permute-start | bytes 196616 | tf_op jit(solution)/shard_map/ppermute | solution.py:215
  85.1 38.2 %all-to-all-start.1 = ((bf16[16,64,1280]{2,1,0:T(8,128)(2,1)}), bf16[16,64,1280]{2,1,0:T(8,128)(2,1)S(1)}, u32[]{:S(2)}, u32[]{:S(2)}) async-start(bf16[16,64,1280]{2,1,0:T(8,128)(2,1)} %broadcast_in_dim.55), calls=%async_computation.1 | async-start | bytes 5242880 | tf_op jit(solution)/shard_map/all_to_all | solution.py:117
  88.9 14.5 %collective-permute-start.14 = (bf16[64,2048]{1,0:T(8,128)(2,1)S(1)}, bf16[64,2048]{1,0:T(8,128)(2,1)S(1)}, u32[]{:S(2)}, u32[]{:S(2)}) collective-permute-start(bf16[64,2048]{1,0:T(8,128)(2,1)S(1)} %pad_maximum_fusion.4), channel_id=1, source_target_pairs={{0,2},{1,3},{2,4},{3,5},{4,6},{5,7},{6,0},{7,1},{8,10},{9,11},{10,... | collective-permute-start | bytes 786440 | tf_op jit(solution)/shard_map/ppermute | solution.py:125
  89.0 14.6 %collective-permute-start.15 = (bf16[64,2048]{1,0:T(8,128)(2,1)S(1)}, bf16[64,2048]{1,0:T(8,128)(2,1)S(1)}, u32[]{:S(2)}, u32[]{:S(2)}) collective-permute-start(bf16[64,2048]{1,0:T(8,128)(2,1)S(1)} %pad_maximum_fusion.4), channel_id=1, source_target_pairs={{0,6},{1,7},{2,0},{3,1},{4,2},{5,3},{6,4},{7,5},{8,14},{9,15},{10,... | collective-permute-start | bytes 786440 | tf_op jit(solution)/shard_map/ppermute | solution.py:125
  92.6 16.5 %collective-permute-start.16 = (bf16[64,2048]{1,0:T(8,128)(2,1)S(1)}, bf16[64,2048]{1,0:T(8,128)(2,1)S(1)}, u32[]{:S(2)}, u32[]{:S(2)}) collective-permute-start(bf16[64,2048]{1,0:T(8,128)(2,1)S(1)} %pad_maximum_fusion.4), channel_id=1, source_target_pairs={{0,1},{1,2},{2,3},{3,4},{4,5},{5,6},{6,7},{7,0},{8,9},{9,10},{10,1... | collective-permute-start | bytes 786440 | tf_op jit(solution)/shard_map/ppermute | solution.py:125
  93.9 19.0 %collective-permute-start.17 = (bf16[64,2048]{1,0:T(8,128)(2,1)S(1)}, bf16[64,2048]{1,0:T(8,128)(2,1)S(1)}, u32[]{:S(2)}, u32[]{:S(2)}) collective-permute-start(bf16[64,2048]{1,0:T(8,128)(2,1)S(1)} %pad_maximum_fusion.4), channel_id=1, source_target_pairs={{0,7},{1,0},{2,1},{3,2},{4,3},{5,4},{6,5},{7,6},{8,15},{9,8},{10,9... | collective-permute-start | bytes 786440 | tf_op jit(solution)/shard_map/ppermute | solution.py:125
  103.5 17.4 %collective-permute-start.20 = (bf16[32,2048]{1,0:T(8,128)(2,1)S(1)}, bf16[32,2048]{1,0:T(8,128)(2,1)S(1)}, u32[]{:S(2)}, u32[]{:S(2)}) collective-permute-start(bf16[32,2048]{1,0:T(8,128)(2,1)S(1)} %slice.156), channel_id=1, source_target_pairs={{0,2},{1,3},{2,4},{3,5},{4,6},{5,7},{6,0},{7,1},{8,10},{9,11},{10,... | collective-permute-start | bytes 393224 | tf_op jit(solution)/shard_map/ppermute | solution.py:125
  103.6 17.3 %collective-permute-start.21 = (bf16[32,2048]{1,0:T(8,128)(2,1)S(1)}, bf16[32,2048]{1,0:T(8,128)(2,1)S(1)}, u32[]{:S(2)}, u32[]{:S(2)}) collective-permute-start(bf16[32,2048]{1,0:T(8,128)(2,1)S(1)} %slice.157), channel_id=1, source_target_pairs={{0,6},{1,7},{2,0},{3,1},{4,2},{5,3},{6,4},{7,5},{8,14},{9,15},{10,... | collective-permute-start | bytes 393224 | tf_op jit(solution)/shard_map/ppermute | solution.py:125
  107.2 12.0 %collective-permute-start.18 = (bf16[64,2048]{1,0:T(8,128)(2,1)S(1)}, bf16[64,2048]{1,0:T(8,128)(2,1)S(1)}, u32[]{:S(2)}, u32[]{:S(2)}) collective-permute-start(bf16[64,2048]{1,0:T(8,128)(2,1)S(1)} %collective-permute-done.14), channel_id=1, source_target_pairs={{0,1},{1,2},{2,3},{3,4},{4,5},{5,6},{6,7},{7,0},{8,9},{9,10},{10,1... | collective-permute-start | bytes 786440 | tf_op jit(solution)/shard_map/ppermute | solution.py:125
  109.1 11.1 %collective-permute-start.19 = (bf16[64,2048]{1,0:T(8,128)(2,1)S(1)}, bf16[64,2048]{1,0:T(8,128)(2,1)S(1)}, u32[]{:S(2)}, u32[]{:S(2)}) collective-permute-start(bf16[64,2048]{1,0:T(8,128)(2,1)S(1)} %collective-permute-done.15), channel_id=1, source_target_pairs={{0,7},{1,0},{2,1},{3,2},{4,3},{5,4},{6,5},{7,6},{8,15},{9,8},{10,9... | collective-permute-start | bytes 786440 | tf_op jit(solution)/shard_map/ppermute | solution.py:125
  126.3 8.4 %collective-permute-start.22 = (bf16[8,64,2048]{2,1,0:T(8,128)(2,1)}, bf16[8,64,2048]{2,1,0:T(8,128)(2,1)}, u32[]{:S(2)}, u32[]{:S(2)}) collective-permute-start(bf16[8,64,2048]{2,1,0:T(8,128)(2,1)} %fusion.15), channel_id=1, source_target_pairs={{0,128},{128,0},{1,129},{129,1},{2,130},{130,2},{3,131},{131,3},{4... | collective-permute-start | bytes 6291464 | tf_op jit(solution)/shard_map/ppermute | solution.py:225
  127.7 37.1 %all-to-all-start.2 = ((f32[16,32,768]{2,1,0:T(8,128)}), f32[16,32,768]{2,1,0:T(8,128)S(1)}, u32[]{:S(2)}, u32[]{:S(2)}) async-start(f32[16,32,768]{2,1,0:T(8,128)} %broadcast_in_dim.56), calls=%async_computation.2 | async-start | bytes 3145728 | tf_op jit(solution)/shard_map/all_to_all | solution.py:117
  (13 other events, 68.9 us)

commit v6 on v5

--- a/solution.py
+++ b/solution.py
@@ -220,8 +220,6 @@
     mine = gather_ring(mine, "col")
     lead_col = gather(lead_piece, "row").reshape(-1, cols_blk)
 
-    gram_lead = gram(lead_feats, col_all)
-    mine, gram_lead = lax.optimization_barrier((mine, gram_lead))
     theirs = lax.ppermute(mine, "tp", swap)
     low, high = jnp.where(first, mine, theirs), jnp.where(first, theirs, mine)
     row_feats, lead_row, diag = [], [], []
@@ -233,10 +231,9 @@
         diag.append(x[:, :, rows_blk:].reshape(-1, PANEL))
     row_feats, lead_row, diag = (jnp.concatenate(v) for v in (row_feats, lead_row, diag))
 
-    inv = inverse_factor(diag + gram_lead[:, cols_blk:])
-    inv, lead_col = lax.optimization_barrier((inv, lead_col))
+    inv = inverse_factor(diag + gram(lead_feats, lead_feats))
     panel_row = jnp.dot(inv, lead_row + gram(lead_feats, row_feats), precision=HIGH)
-    panel_col = jnp.dot(inv, lead_col + gram_lead[:, :cols_blk], precision=HIGH)
+    panel_col = jnp.dot(inv, lead_col + gram(lead_feats, col_feats), precision=HIGH)
     trailing = (
         curvature
         + gram(row_feats, col_feats)

time: 179 us -> 179 us (level)
  waiting for transfers between devices: 31.4 us -> 43.4 us
  local copies, waits for them, and re-layouts: 16.1 us -> 10.1 us
  starting transfers between devices: 78.1 us -> 74.6 us
  other arithmetic: 7.23 us -> 4.32 us
    ppermute x8, waiting for transfers between devices: 11.7 us -> 25.5 us  [shift(): return lax.ppermute(v, axis, [(i, (i + k) % n) for i in range(n)])]
    dynamic_update_slice x7, local copies, waits for them, and re-layouts: 5.03 us -> 0.16 us  [put(): return lax.dynamic_update_index_in_dim(out, v, lax.rem(me + n - k, n), 0)]
    dot_general x3 -> x4, matrix products: 8.07 us -> 12.8 us  [gram(): lax.dot_general(a, b, (((0,), (0,)), ((), ())), preferred_element_type=f32)]
    ppermute x8, starting transfers between devices: 13.5 us -> 9.22 us  [shift(): return lax.ppermute(v, axis, [(i, (i + k) % n) for i in range(n)])]
    dot_general x1, matrix products: 4.24 us -> 1.54 us  [per_device(): jnp.dot(inv, lead_col + gram(lead_feats, col_feats), precision=HIGH)]
    dot_general x1, matrix products: 6.68 us -> 4.02 us  [per_device(): lax.dot_general(panel_row, panel_col, (((0,), (0,)), ((), ())), precision...]
    ppermute x1, starting transfers between devices: 0.01 us -> 2.3 us  [per_device(): theirs = lax.ppermute(mine, 'tp', swap)]
  transfers between devices with their start and end apart: 26 -> 26, of which waited for: 8 -> 6; matrix products, arithmetic and copies ran while one was open for 17% -> 16% of each run, Pallas kernels for 10% -> 10%
where the time goes in v6:
time: 179 us; the launch traced here: 178 us
  starting transfers between devices  74.6 us (42%)
  waiting for transfers between devices  43.4 us (24%)
  matrix products  26 us (15%)
  Pallas kernels  17.9 us (10%)
  local copies, waits for them, and re-layouts  10.1 us (6%)
  other arithmetic  4.32 us (2%)
    ppermute x8, waiting for transfers between devices, shift(): return lax.ppermute(v, axis, [(i, (i + k) % n) for i in range(n)])  25.5 us
    pallas_call x1, Pallas kernels, inverse_factor(): pl.pallas_call(factor_kernel, out_shape=jax.ShapeDtypeStruct((PANEL, PANE...  17.9 us
    ppermute x3, starting transfers between devices, per_device(): lax.ppermute(diag, 'row', [(side * j, side * j + k) for j in range(side)])  14.7 us
    dot_general x4, matrix products, gram(): lax.dot_general(a, b, (((0,), (0,)), ((), ())), preferred_element_type=f32)  12.8 us
    all_to_all x2, starting transfers between devices, gather(): lax.all_to_all(jnp.broadcast_to(x[None], (n,) + x.shape), axis, 0, 0, til...  10.4 us
    all_to_all x1, starting transfers between devices, per_device(): got = lax.all_to_all(out, ('tp', 'col'), 0, 0, tiled=True)  10 us
    ppermute x3, starting transfers between devices, per_device(): lax.ppermute(lead[k], 'row', [(0, side * k)])  9.85 us
    ppermute x8, starting transfers between devices, shift(): return lax.ppermute(v, axis, [(i, (i + k) % n) for i in range(n)])  9.22 us
  transfers between devices with their start and end apart: 26, of which 6 were waited for; matrix products, arithmetic and copies ran while one was open for 16% of the time, Pallas kernels for 10%

profile of v6, /device:TPU:1, one launch (start us, length us, event | category | flops | bytes accessed | tf_op | source)
XLA Modules:
  0.0 177.7 jit_solution(12123723207866269584)
XLA Ops:
  2.2 4.8 %collective-permute-start.1 = (f32[4,32,768]{2,1,0:T(8,128)S(1)}, f32[4,32,768]{2,1,0:T(8,128)}, u32[]{:S(2)}, u32[]{:S(2)}) collective-permute-start(f32[4,32,768]{2,1,0:T(8,128)S(1)} %bitcast.78), channel_id=1, source_target_pairs={{0,32},{1,33},{2,34},{3,35},{4,36},{5,37},{6,38},{7,39},{128,160},... | collective-permute-start | bytes 1179656 | tf_op jit(solution)/shard_map/ppermute | solution.py:169
  7.0 3.0 %collective-permute-start.2 = (f32[4,32,768]{2,1,0:T(8,128)S(1)}, f32[4,32,768]{2,1,0:T(8,128)}, u32[]{:S(2)}, u32[]{:S(2)}) collective-permute-start(f32[4,32,768]{2,1,0:T(8,128)S(1)} %bitcast.77), channel_id=1, source_target_pairs={{0,64},{1,65},{2,66},{3,67},{4,68},{5,69},{6,70},{7,71},{128,192},... | collective-permute-start | bytes 1179656 | tf_op jit(solution)/shard_map/ppermute | solution.py:169
  12.1 3.9 %fusion.22 = f32[1024,192]{0,1:T(8,128)S(1)} fusion(bf16[1024,2048]{1,0:T(8,128)(2,1)} %bitcast.80, bf16[2048,192]{0,1:T(8,128)(2,1)S(1)} %copy-done), kind=kOutput, calls=%fused_computation.61 | convolution fusion | flops 805306368 | bytes 5767168 | tf_op jit(solution)/shard_map/dot_general | solution.py:179
  18.6 3.9 %collective-permute-done.2 = f32[4,32,768]{2,1,0:T(8,128)} collective-permute-done((f32[4,32,768]{2,1,0:T(8,128)S(1)}, f32[4,32,768]{2,1,0:T(8,128)}, u32[]{:S(2)}, u32[]{:S(2)}) %collective-permute-start.2) | collective-permute-done | bytes 393248 | tf_op jit(solution)/shard_map/ppermute | solution.py:169
  30.0 10.0 %all-to-all-start = ((bf16[16,4,1280]{2,1,0:T(4,128)(2,1)}), bf16[16,4,1280]{2,1,0:T(4,128)(2,1)S(1)}, u32[]{:S(2)}, u32[]{:S(2)}) async-start(bf16[16,4,1280]{2,1,0:T(4,128)(2,1)} %copy.25), calls=%async_computation | async-start | bytes 327680 | tf_op jit(solution)/shard_map/all_to_all | solution.py:198
  40.1 7.8 %all-to-all-done = bf16[16,4,1280]{2,1,0:T(4,128)(2,1)S(1)} async-done(((bf16[16,4,1280]{2,1,0:T(4,128)(2,1)}), bf16[16,4,1280]{2,1,0:T(4,128)(2,1)S(1)}, u32[]{:S(2)}, u32[]{:S(2)}) %all-to-all-start) | async-done | bytes 163872 | tf_op jit(solution)/shard_map/all_to_all | solution.py:198
  47.9 6.6 %collective-permute-start.7 = (bf16[64,1536]{1,0:T(8,128)(2,1)S(1)}, bf16[64,1536]{1,0:T(8,128)(2,1)S(1)}, u32[]{:S(2)}, u32[]{:S(2)}) collective-permute-start(bf16[64,1536]{1,0:T(8,128)(2,1)S(1)} %maximum_maximum_fusion), channel_id=1, source_target_pairs={{0,0},{1,8},{2,16},{3,24},{4,32},{5,40},{6,48},{7,56},{128,64},{12... | collective-permute-start | bytes 589832 | tf_op jit(solution)/shard_map/ppermute | solution.py:208
  54.5 4.6 %collective-permute-done.7 = bf16[64,1536]{1,0:T(8,128)(2,1)S(1)} collective-permute-done((bf16[64,1536]{1,0:T(8,128)(2,1)S(1)}, bf16[64,1536]{1,0:T(8,128)(2,1)S(1)}, u32[]{:S(2)}, u32[]{:S(2)}) %collective-permute-start.7) | collective-permute-done | bytes 196640 | tf_op jit(solution)/shard_map/ppermute | solution.py:208
  59.2 4.0 %collective-permute-start.10 = (bf16[64,512]{1,0:T(8,128)(2,1)S(1)}, bf16[64,512]{1,0:T(8,128)(2,1)S(1)}, u32[]{:S(2)}, u32[]{:S(2)}) collective-permute-start(bf16[64,512]{1,0:T(8,128)(2,1)S(1)} %slice.147), channel_id=1, source_target_pairs={{0,96},{1,97},{2,98},{3,99},{4,100},{5,101},{6,102},{7,103},{128,2... | collective-permute-start | bytes 196616 | tf_op jit(solution)/shard_map/ppermute | solution.py:211
  68.7 6.4 %collective-permute-start.12 = (bf16[64,512]{1,0:T(8,128)(2,1)S(1)}, bf16[64,512]{1,0:T(8,128)(2,1)S(1)}, u32[]{:S(2)}, u32[]{:S(2)}) collective-permute-start(bf16[64,512]{1,0:T(8,128)(2,1)S(1)} %add_select_fusion.2), channel_id=1, source_target_pairs={{0,16},{32,48},{64,80},{96,112},{1,17},{33,49},{65,81},{97,113},{2... | collective-permute-start | bytes 196616 | tf_op jit(solution)/shard_map/ppermute | solution.py:215
  75.1 7.0 %collective-permute-start.11 = (bf16[64,512]{1,0:T(8,128)(2,1)S(1)}, bf16[64,512]{1,0:T(8,128)(2,1)S(1)}, u32[]{:S(2)}, u32[]{:S(2)}) collective-permute-start(bf16[64,512]{1,0:T(8,128)(2,1)S(1)} %add_select_fusion.2), channel_id=1, source_target_pairs={{0,8},{32,40},{64,72},{96,104},{1,9},{33,41},{65,73},{97,105},{2,1... | collective-permute-start | bytes 196616 | tf_op jit(solution)/shard_map/ppermute | solution.py:215
  84.0 4.5 %all-to-all-start.1 = ((bf16[16,64,1280]{2,1,0:T(8,128)(2,1)}), bf16[16,64,1280]{2,1,0:T(8,128)(2,1)}, u32[]{:S(2)}, u32[]{:S(2)}) async-start(bf16[16,64,1280]{2,1,0:T(8,128)(2,1)} %broadcast_in_dim.55), calls=%async_computation.1 | async-start | bytes 5242880 | tf_op jit(solution)/shard_map/all_to_all | solution.py:117
  88.6 2.5 %collective-permute-start.16 = (bf16[64,2048]{1,0:T(8,128)(2,1)S(1)}, bf16[64,2048]{1,0:T(8,128)(2,1)S(1)}, u32[]{:S(2)}, u32[]{:S(2)}) collective-permute-start(bf16[64,2048]{1,0:T(8,128)(2,1)S(1)} %pad_maximum_fusion.4), channel_id=1, source_target_pairs={{0,1},{1,2},{2,3},{3,4},{4,5},{5,6},{6,7},{7,0},{8,9},{9,10},{10,1... | collective-permute-start | bytes 786440 | tf_op jit(solution)/shard_map/ppermute | solution.py:125
  91.1 2.4 %collective-permute-start.14 = (bf16[64,2048]{1,0:T(8,128)(2,1)S(1)}, bf16[64,2048]{1,0:T(8,128)(2,1)S(1)}, u32[]{:S(2)}, u32[]{:S(2)}) collective-permute-start(bf16[64,2048]{1,0:T(8,128)(2,1)S(1)} %pad_maximum_fusion.4), channel_id=1, source_target_pairs={{0,2},{1,3},{2,4},{3,5},{4,6},{5,7},{6,0},{7,1},{8,10},{9,11},{10,... | collective-permute-start | bytes 786440 | tf_op jit(solution)/shard_map/ppermute | solution.py:125
  93.8 17.9 %collective-permute-done.15 = bf16[64,2048]{1,0:T(8,128)(2,1)S(1)} collective-permute-done((bf16[64,2048]{1,0:T(8,128)(2,1)S(1)}, bf16[64,2048]{1,0:T(8,128)(2,1)S(1)}, u32[]{:S(2)}, u32[]{:S(2)}) %collective-permute-start.15) | collective-permute-done | bytes 262176 | tf_op jit(solution)/shard_map/ppermute | solution.py:125
  111.8 2.4 %collective-permute-start.20 = (bf16[32,2048]{1,0:T(8,128)(2,1)S(1)}, bf16[32,2048]{1,0:T(8,128)(2,1)S(1)}, u32[]{:S(2)}, u32[]{:S(2)}) collective-permute-start(bf16[32,2048]{1,0:T(8,128)(2,1)S(1)} %slice.148), channel_id=1, source_target_pairs={{0,2},{1,3},{2,4},{3,5},{4,6},{5,7},{6,0},{7,1},{8,10},{9,11},{10,... | collective-permute-start | bytes 393224 | tf_op jit(solution)/shard_map/ppermute | solution.py:125
  116.1 7.6 %collective-permute-done.18 = bf16[64,2048]{1,0:T(8,128)(2,1)S(1)} collective-permute-done((bf16[64,2048]{1,0:T(8,128)(2,1)S(1)}, bf16[64,2048]{1,0:T(8,128)(2,1)S(1)}, u32[]{:S(2)}, u32[]{:S(2)}) %collective-permute-start.18) | collective-permute-done | bytes 262176 | tf_op jit(solution)/shard_map/ppermute | solution.py:125
  123.8 2.3 %collective-permute-start.22 = (bf16[8,64,2048]{2,1,0:T(8,128)(2,1)S(1)}, bf16[8,64,2048]{2,1,0:T(8,128)(2,1)}, u32[]{:S(2)}, u32[]{:S(2)}) collective-permute-start(bf16[8,64,2048]{2,1,0:T(8,128)(2,1)S(1)} %fusion.13), channel_id=1, source_target_pairs={{0,128},{128,0},{1,129},{129,1},{2,130},{130,2},{3,131},{131,3},{4... | collective-permute-start | bytes 6291464 | tf_op jit(solution)/shard_map/ppermute | solution.py:223
  127.5 5.9 %all-to-all-start.2 = ((f32[16,32,768]{2,1,0:T(8,128)}), f32[16,32,768]{2,1,0:T(8,128)}, u32[]{:S(2)}, u32[]{:S(2)}) async-start(f32[16,32,768]{2,1,0:T(8,128)} %broadcast_in_dim.56), calls=%async_computation.2 | async-start | bytes 3145728 | tf_op jit(solution)/shard_map/all_to_all | solution.py:117
  140.8 17.9 %inverse_factor.1 = f32[512,512]{1,0:T(8,128)S(1)} custom-call(f32[512,512]{1,0:T(8,128)S(1)} %convolution_add_fusion.a_ref), custom_call_target="tpu_custom_call" | custom-call | tf_op jit(solution)/shard_map/inverse_factor/pallas_call | solution.py:96
  158.7 2.4 %fusion.7 = f32[512,768]{1,0:T(8,128)S(1)} fusion(bf16[512,768]{1,0:T(8,128)(2,1)S(1)} %bitcast.72, bf16[512,768]{1,0:T(8,128)(2,1)S(1)} %bitcast.70, bf16[1024,1280]{1,0:T(8,128)(2,1)} %bitcast.21), kind=kOutput, calls=%fused_computation.21 | convolution fusion | flops 808452096 | bytes 4194304 | tf_op jit(solution)/shard_map/dot_general | solution.py:144
  163.8 4.7 %fusion.4 = f32[768,768]{1,0:T(8,128)} fusion(bf16[1024,1280]{1,0:T(8,128)(2,1)} %bitcast.21, bf16[512,768]{1,0:T(8,128)(2,1)} %bitcast.73, bf16[512,768]{1,0:T(8,128)(2,1)} %bitcast.71), kind=kOutput, calls=%fused_computation.10 | convolution fusion | flops 1211105280 | bytes 5505024 | tf_op jit(solution)/shard_map/dot_general | solution.py:144
  168.6 3.4 %bitcast_add_fusion = f32[512,768]{1,0:T(8,128)S(1)} fusion(f32[16,32,768]{2,1,0:T(8,128)} %all-to-all-done.2, bf16[1024,1280]{1,0:T(8,128)(2,1)} %bitcast.21), kind=kOutput, calls=%fused_computation.8 | convolution fusion | flops 805699584 | bytes 5767168 | tf_op jit(solution)/shard_map/dot_general | solution.py:144
  173.7 4.0 %add_subtract_fusion = f32[768,768]{1,0:T(8,128)} fusion(f32[768,768]{1,0:T(8,128)S(1)} %copy-done.2, f32[768,768]{1,0:T(8,128)S(1)} %copy-done.6, f32[512,768]{1,0:T(8,128)S(1)} %fusion, f32[512,768]{1,0:T(8,128)S(1)} %fusion.24), kind=kOutput, calls=%fused_computation | convolution fusion | flops 1813118976 | bytes 10223616 | tf_op jit(solution)/shard_map/dot_general | solution.py:240
  (109 shorter events, 36.5 us)
Async XLA Ops:
  2.2 16.4 %collective-permute-start.1 = (f32[4,32,768]{2,1,0:T(8,128)S(1)}, f32[4,32,768]{2,1,0:T(8,128)}, u32[]{:S(2)}, u32[]{:S(2)}) collective-permute-start(f32[4,32,768]{2,1,0:T(8,128)S(1)} %bitcast.78), channel_id=1, source_target_pairs={{0,32},{1,33},{2,34},{3,35},{4,36},{5,37},{6,38},{7,39},{128,160},... | collective-permute-start | bytes 1179656 | tf_op jit(solution)/shard_map/ppermute | solution.py:169
  7.0 15.4 %collective-permute-start.2 = (f32[4,32,768]{2,1,0:T(8,128)S(1)}, f32[4,32,768]{2,1,0:T(8,128)}, u32[]{:S(2)}, u32[]{:S(2)}) collective-permute-start(f32[4,32,768]{2,1,0:T(8,128)S(1)} %bitcast.77), channel_id=1, source_target_pairs={{0,64},{1,65},{2,66},{3,67},{4,68},{5,69},{6,70},{7,71},{128,192},... | collective-permute-start | bytes 1179656 | tf_op jit(solution)/shard_map/ppermute | solution.py:169
  10.0 12.4 %collective-permute-start.3 = (f32[4,32,768]{2,1,0:T(8,128)S(1)}, f32[4,32,768]{2,1,0:T(8,128)}, u32[]{:S(2)}, u32[]{:S(2)}) collective-permute-start(f32[4,32,768]{2,1,0:T(8,128)S(1)} %bitcast.76), channel_id=1, source_target_pairs={{0,96},{1,97},{2,98},{3,99},{4,100},{5,101},{6,102},{7,103},{128,2... | collective-permute-start | bytes 1179656 | tf_op jit(solution)/shard_map/ppermute | solution.py:169
  17.5 10.2 %collective-permute-start = (f32[4,128,256]{1,2,0:T(8,128)S(1)}, f32[4,128,256]{1,2,0:T(8,128)S(1)}, u32[]{:S(2)}, u32[]{:S(2)}) collective-permute-start(f32[4,128,256]{1,2,0:T(8,128)S(1)} %bitcast.74), channel_id=1, source_target_pairs={{0,128},{128,0},{1,129},{129,1},{2,130},{130,2},{3,131},{131,3},{4... | collective-permute-start | bytes 1572872 | tf_op jit(solution)/shard_map/ppermute | solution.py:186
  23.8 16.2 %collective-permute-start.5 = (f32[32,768]{1,0:T(8,128)S(1)}, f32[32,768]{1,0:T(8,128)S(1)}, u32[]{:S(2)}, u32[]{:S(2)}) collective-permute-start(f32[32,768]{1,0:T(8,128)S(1)} %get-tuple-element.24), channel_id=1, source_target_pairs={{0,16},{32,48},{64,80},{96,112},{1,17},{33,49},{65,81},{97,113},{2... | collective-permute-start | bytes 294920 | tf_op jit(solution)/shard_map/ppermute | solution.py:172
  25.1 14.9 %collective-permute-start.6 = (f32[32,768]{1,0:T(8,128)S(1)}, f32[32,768]{1,0:T(8,128)S(1)}, u32[]{:S(2)}, u32[]{:S(2)}) collective-permute-start(f32[32,768]{1,0:T(8,128)S(1)} %get-tuple-element.25), channel_id=1, source_target_pairs={{0,24},{32,56},{64,88},{96,120},{1,25},{33,57},{65,89},{97,121},{2... | collective-permute-start | bytes 294920 | tf_op jit(solution)/shard_map/ppermute | solution.py:172
  26.4 13.6 %collective-permute-start.4 = (f32[32,768]{1,0:T(8,128)S(1)}, f32[32,768]{1,0:T(8,128)S(1)}, u32[]{:S(2)}, u32[]{:S(2)}) collective-permute-start(f32[32,768]{1,0:T(8,128)S(1)} %get-tuple-element.26), channel_id=1, source_target_pairs={{0,8},{32,40},{64,72},{96,104},{1,9},{33,41},{65,73},{97,105},{2,1... | collective-permute-start | bytes 294920 | tf_op jit(solution)/shard_map/ppermute | solution.py:172
  30.0 17.8 %all-to-all-start = ((bf16[16,4,1280]{2,1,0:T(4,128)(2,1)}), bf16[16,4,1280]{2,1,0:T(4,128)(2,1)S(1)}, u32[]{:S(2)}, u32[]{:S(2)}) async-start(bf16[16,4,1280]{2,1,0:T(4,128)(2,1)} %copy.25), calls=%async_computation | async-start | bytes 327680 | tf_op jit(solution)/shard_map/all_to_all | solution.py:198
  47.9 11.2 %collective-permute-start.7 = (bf16[64,1536]{1,0:T(8,128)(2,1)S(1)}, bf16[64,1536]{1,0:T(8,128)(2,1)S(1)}, u32[]{:S(2)}, u32[]{:S(2)}) collective-permute-start(bf16[64,1536]{1,0:T(8,128)(2,1)S(1)} %maximum_maximum_fusion), channel_id=1, source_target_pairs={{0,0},{1,8},{2,16},{3,24},{4,32},{5,40},{6,48},{7,56},{128,64},{12... | collective-permute-start | bytes 589832 | tf_op jit(solution)/shard_map/ppermute | solution.py:208
  59.2 6.6 %collective-permute-start.10 = (bf16[64,512]{1,0:T(8,128)(2,1)S(1)}, bf16[64,512]{1,0:T(8,128)(2,1)S(1)}, u32[]{:S(2)}, u32[]{:S(2)}) collective-permute-start(bf16[64,512]{1,0:T(8,128)(2,1)S(1)} %slice.147), channel_id=1, source_target_pairs={{0,96},{1,97},{2,98},{3,99},{4,100},{5,101},{6,102},{7,103},{128,2... | collective-permute-start | bytes 196616 | tf_op jit(solution)/shard_map/ppermute | solution.py:211
  67.4 21.0 %collective-permute-start.13 = (bf16[64,512]{1,0:T(8,128)(2,1)S(1)}, bf16[64,512]{1,0:T(8,128)(2,1)S(1)}, u32[]{:S(2)}, u32[]{:S(2)}) collective-permute-start(bf16[64,512]{1,0:T(8,128)(2,1)S(1)} %add_select_fusion.2), channel_id=1, source_target_pairs={{0,24},{32,56},{64,88},{96,120},{1,25},{33,57},{65,89},{97,121},{2... | collective-permute-start | bytes 196616 | tf_op jit(solution)/shard_map/ppermute | solution.py:215
  68.7 19.7 %collective-permute-start.12 = (bf16[64,512]{1,0:T(8,128)(2,1)S(1)}, bf16[64,512]{1,0:T(8,128)(2,1)S(1)}, u32[]{:S(2)}, u32[]{:S(2)}) collective-permute-start(bf16[64,512]{1,0:T(8,128)(2,1)S(1)} %add_select_fusion.2), channel_id=1, source_target_pairs={{0,16},{32,48},{64,80},{96,112},{1,17},{33,49},{65,81},{97,113},{2... | collective-permute-start | bytes 196616 | tf_op jit(solution)/shard_map/ppermute | solution.py:215
  75.1 13.3 %collective-permute-start.11 = (bf16[64,512]{1,0:T(8,128)(2,1)S(1)}, bf16[64,512]{1,0:T(8,128)(2,1)S(1)}, u32[]{:S(2)}, u32[]{:S(2)}) collective-permute-start(bf16[64,512]{1,0:T(8,128)(2,1)S(1)} %add_select_fusion.2), channel_id=1, source_target_pairs={{0,8},{32,40},{64,72},{96,104},{1,9},{33,41},{65,73},{97,105},{2,1... | collective-permute-start | bytes 196616 | tf_op jit(solution)/shard_map/ppermute | solution.py:215
  84.0 42.1 %all-to-all-start.1 = ((bf16[16,64,1280]{2,1,0:T(8,128)(2,1)}), bf16[16,64,1280]{2,1,0:T(8,128)(2,1)}, u32[]{:S(2)}, u32[]{:S(2)}) async-start(bf16[16,64,1280]{2,1,0:T(8,128)(2,1)} %broadcast_in_dim.55), calls=%async_computation.1 | async-start | bytes 5242880 | tf_op jit(solution)/shard_map/all_to_all | solution.py:117
  88.5 27.5 %collective-permute-start.17 = (bf16[64,2048]{1,0:T(8,128)(2,1)S(1)}, bf16[64,2048]{1,0:T(8,128)(2,1)S(1)}, u32[]{:S(2)}, u32[]{:S(2)}) collective-permute-start(bf16[64,2048]{1,0:T(8,128)(2,1)S(1)} %pad_maximum_fusion.4), channel_id=1, source_target_pairs={{0,7},{1,0},{2,1},{3,2},{4,3},{5,4},{6,5},{7,6},{8,15},{9,8},{10,9... | collective-permute-start | bytes 786440 | tf_op jit(solution)/shard_map/ppermute | solution.py:125
  88.6 25.7 %collective-permute-start.16 = (bf16[64,2048]{1,0:T(8,128)(2,1)S(1)}, bf16[64,2048]{1,0:T(8,128)(2,1)S(1)}, u32[]{:S(2)}, u32[]{:S(2)}) collective-permute-start(bf16[64,2048]{1,0:T(8,128)(2,1)S(1)} %pad_maximum_fusion.4), channel_id=1, source_target_pairs={{0,1},{1,2},{2,3},{3,4},{4,5},{5,6},{6,7},{7,0},{8,9},{9,10},{10,1... | collective-permute-start | bytes 786440 | tf_op jit(solution)/shard_map/ppermute | solution.py:125
  91.1 20.5 %collective-permute-start.15 = (bf16[64,2048]{1,0:T(8,128)(2,1)S(1)}, bf16[64,2048]{1,0:T(8,128)(2,1)S(1)}, u32[]{:S(2)}, u32[]{:S(2)}) collective-permute-start(bf16[64,2048]{1,0:T(8,128)(2,1)S(1)} %pad_maximum_fusion.4), channel_id=1, source_target_pairs={{0,6},{1,7},{2,0},{3,1},{4,2},{5,3},{6,4},{7,5},{8,14},{9,15},{10,... | collective-permute-start | bytes 786440 | tf_op jit(solution)/shard_map/ppermute | solution.py:125
  91.1 20.6 %collective-permute-start.14 = (bf16[64,2048]{1,0:T(8,128)(2,1)S(1)}, bf16[64,2048]{1,0:T(8,128)(2,1)S(1)}, u32[]{:S(2)}, u32[]{:S(2)}) collective-permute-start(bf16[64,2048]{1,0:T(8,128)(2,1)S(1)} %pad_maximum_fusion.4), channel_id=1, source_target_pairs={{0,2},{1,3},{2,4},{3,5},{4,6},{5,7},{6,0},{7,1},{8,10},{9,11},{10,... | collective-permute-start | bytes 786440 | tf_op jit(solution)/shard_map/ppermute | solution.py:125
  111.7 12.1 %collective-permute-start.21 = (bf16[32,2048]{1,0:T(8,128)(2,1)S(1)}, bf16[32,2048]{1,0:T(8,128)(2,1)S(1)}, u32[]{:S(2)}, u32[]{:S(2)}) collective-permute-start(bf16[32,2048]{1,0:T(8,128)(2,1)S(1)} %slice.149), channel_id=1, source_target_pairs={{0,6},{1,7},{2,0},{3,1},{4,2},{5,3},{6,4},{7,5},{8,14},{9,15},{10,... | collective-permute-start | bytes 393224 | tf_op jit(solution)/shard_map/ppermute | solution.py:125
  111.8 11.9 %collective-permute-start.20 = (bf16[32,2048]{1,0:T(8,128)(2,1)S(1)}, bf16[32,2048]{1,0:T(8,128)(2,1)S(1)}, u32[]{:S(2)}, u32[]{:S(2)}) collective-permute-start(bf16[32,2048]{1,0:T(8,128)(2,1)S(1)} %slice.148), channel_id=1, source_target_pairs={{0,2},{1,3},{2,4},{3,5},{4,6},{5,7},{6,0},{7,1},{8,10},{9,11},{10,... | collective-permute-start | bytes 393224 | tf_op jit(solution)/shard_map/ppermute | solution.py:125
  114.2 9.5 %collective-permute-start.19 = (bf16[64,2048]{1,0:T(8,128)(2,1)S(1)}, bf16[64,2048]{1,0:T(8,128)(2,1)S(1)}, u32[]{:S(2)}, u32[]{:S(2)}) collective-permute-start(bf16[64,2048]{1,0:T(8,128)(2,1)S(1)} %collective-permute-done.15), channel_id=1, source_target_pairs={{0,7},{1,0},{2,1},{3,2},{4,3},{5,4},{6,5},{7,6},{8,15},{9,8},{10,9... | collective-permute-start | bytes 786440 | tf_op jit(solution)/shard_map/ppermute | solution.py:125
  114.3 9.4 %collective-permute-start.18 = (bf16[64,2048]{1,0:T(8,128)(2,1)S(1)}, bf16[64,2048]{1,0:T(8,128)(2,1)S(1)}, u32[]{:S(2)}, u32[]{:S(2)}) collective-permute-start(bf16[64,2048]{1,0:T(8,128)(2,1)S(1)} %collective-permute-done.14), channel_id=1, source_target_pairs={{0,1},{1,2},{2,3},{3,4},{4,5},{5,6},{6,7},{7,0},{8,9},{9,10},{10,1... | collective-permute-start | bytes 786440 | tf_op jit(solution)/shard_map/ppermute | solution.py:125
  123.8 9.6 %collective-permute-start.22 = (bf16[8,64,2048]{2,1,0:T(8,128)(2,1)S(1)}, bf16[8,64,2048]{2,1,0:T(8,128)(2,1)}, u32[]{:S(2)}, u32[]{:S(2)}) collective-permute-start(bf16[8,64,2048]{2,1,0:T(8,128)(2,1)S(1)} %fusion.13), channel_id=1, source_target_pairs={{0,128},{128,0},{1,129},{129,1},{2,130},{130,2},{3,131},{131,3},{4... | collective-permute-start | bytes 6291464 | tf_op jit(solution)/shard_map/ppermute | solution.py:223
  127.5 41.1 %all-to-all-start.2 = ((f32[16,32,768]{2,1,0:T(8,128)}), f32[16,32,768]{2,1,0:T(8,128)}, u32[]{:S(2)}, u32[]{:S(2)}) async-start(f32[16,32,768]{2,1,0:T(8,128)} %broadcast_in_dim.56), calls=%async_computation.2 | async-start | bytes 3145728 | tf_op jit(solution)/shard_map/all_to_all | solution.py:117
  (15 other events, 88.8 us)

commit v7 on v6

--- a/solution.py
+++ b/solution.py
@@ -203,10 +203,8 @@
     col_all, lead_piece = lax.optimization_barrier((col_all, piece_col))
     col_feats, lead_feats = col_all[:, :cols_blk], col_all[:, cols_blk:]
 
-    halved = jnp.concatenate(wire_halves(piece_col), axis=0)
-    both = jnp.concatenate([got[:, :cols_blk], halved], axis=1)
-    both = lax.ppermute(both, axes, turn)
-    diag = both[:, cols_blk : cols_blk + PANEL]
+    piece_row = lax.ppermute(piece_col, axes, turn)
+    diag = piece_row[:, :PANEL]
     got_diag = sum(
         lax.ppermute(diag, "row", [(0, side * k)]) for k in range(1, side)
     )
@@ -216,7 +214,9 @@
         for k in range(1, side)
     )
     diag = jnp.where(lax.rem(row, side) == 0, diag, got_diag)
-    mine = lax.optimization_barrier(jnp.concatenate([both, diag], axis=1))
+    turned = lax.ppermute(got[:, :cols_blk], axes, turn)
+    mine = [turned] + [jnp.concatenate(wire_halves(v), axis=0) for v in (piece_row, diag)]
+    mine = lax.optimization_barrier(jnp.concatenate(mine, axis=1))
     mine = gather_ring(mine, "col")
     lead_col = gather(lead_piece, "row").reshape(-1, cols_blk)
 

time: 179 us -> 179 us (level)
  starting transfers between devices: 74.6 us -> 82.8 us
  waiting for transfers between devices: 43.4 us -> 35.3 us
    ppermute x3, starting transfers between devices: 14.7 us -> 3.88 us  [per_device(): lax.ppermute(diag, 'row', [(side * j, side * j + k) for j in range(side)])]
    ppermute x8, starting transfers between devices: 9.22 us -> 18.7 us  [shift(): return lax.ppermute(v, axis, [(i, (i + k) % n) for i in range(n)])]
    all_to_all x1, waiting for transfers between devices: 7.76 us -> 2.22 us  [per_device(): got = lax.all_to_all(out, ('tp', 'col'), 0, 0, tiled=True)]
    ppermute x1 -> x2, waiting for transfers between devices: 4.61 us -> 0.79 us  [the longest x1 0.79 us: per_device(): piece_row = lax.ppermute(piece_col, axes, turn)]
    all_to_all x1, starting transfers between devices: 10 us -> 13.5 us  [per_device(): got = lax.all_to_all(out, ('tp', 'col'), 0, 0, tiled=True)]
    ppermute x3, starting transfers between devices: 6.55 us -> 9.73 us  [per_device(): lax.ppermute(diag, 'row', [(0, side * k)])]
    ppermute x1 -> x2, starting transfers between devices: 6.63 us -> 9.8 us  [the longest x1 7.63 us: per_device(): piece_row = lax.ppermute(piece_col, axes, turn)]
  transfers between devices with their start and end apart: 26 -> 27, of which waited for: 6 -> 9; matrix products, arithmetic and copies ran while one was open for 16% -> 16% of each run, Pallas kernels for 10% -> 10%
where the time goes in v7:
time: 179 us; the launch traced here: 178 us
  starting transfers between devices  82.8 us (46%)
  waiting for transfers between devices  35.3 us (20%)
  matrix products  26.1 us (15%)
  Pallas kernels  17.9 us (10%)
  local copies, waits for them, and re-layouts  10.1 us (6%)
  other arithmetic  4.32 us (2%)
    ppermute x8, waiting for transfers between devices, shift(): return lax.ppermute(v, axis, [(i, (i + k) % n) for i in range(n)])  25.2 us
    ppermute x8, starting transfers between devices, shift(): return lax.ppermute(v, axis, [(i, (i + k) % n) for i in range(n)])  18.7 us
    pallas_call x1, Pallas kernels, inverse_factor(): pl.pallas_call(factor_kernel, out_shape=jax.ShapeDtypeStruct((PANEL, PANE...  17.9 us
    all_to_all x1, starting transfers between devices, per_device(): got = lax.all_to_all(out, ('tp', 'col'), 0, 0, tiled=True)  13.5 us
    dot_general x4, matrix products, gram(): lax.dot_general(a, b, (((0,), (0,)), ((), ())), preferred_element_type=f32)  12.9 us
    all_to_all x2, starting transfers between devices, gather(): lax.all_to_all(jnp.broadcast_to(x[None], (n,) + x.shape), axis, 0, 0, til...  11.3 us
    ppermute x3, starting transfers between devices, per_device(): lax.ppermute(lead[k], 'row', [(0, side * k)])  9.86 us
    ppermute x3, starting transfers between devices, per_device(): lax.ppermute(diag, 'row', [(0, side * k)])  9.73 us
  transfers between devices with their start and end apart: 27, of which 9 were waited for; matrix products, arithmetic and copies ran while one was open for 16% of the time, Pallas kernels for 10%

profile of v7, /device:TPU:1, one launch (start us, length us, event | category | flops | bytes accessed | tf_op | source)
XLA Modules:
  0.0 178.0 jit_solution(296960541641160317)
XLA Ops:
  2.2 4.8 %collective-permute-start.2 = (f32[4,32,768]{2,1,0:T(8,128)S(1)}, f32[4,32,768]{2,1,0:T(8,128)}, u32[]{:S(2)}, u32[]{:S(2)}) collective-permute-start(f32[4,32,768]{2,1,0:T(8,128)S(1)} %bitcast.77), channel_id=1, source_target_pairs={{0,32},{1,33},{2,34},{3,35},{4,36},{5,37},{6,38},{7,39},{128,160},... | collective-permute-start | bytes 1179656 | tf_op jit(solution)/shard_map/ppermute | solution.py:169
  7.0 3.0 %collective-permute-start.3 = (f32[4,32,768]{2,1,0:T(8,128)S(1)}, f32[4,32,768]{2,1,0:T(8,128)}, u32[]{:S(2)}, u32[]{:S(2)}) collective-permute-start(f32[4,32,768]{2,1,0:T(8,128)S(1)} %bitcast.76), channel_id=1, source_target_pairs={{0,64},{1,65},{2,66},{3,67},{4,68},{5,69},{6,70},{7,71},{128,192},... | collective-permute-start | bytes 1179656 | tf_op jit(solution)/shard_map/ppermute | solution.py:169
  10.0 2.0 %collective-permute-start.4 = (f32[4,32,768]{2,1,0:T(8,128)S(1)}, f32[4,32,768]{2,1,0:T(8,128)}, u32[]{:S(2)}, u32[]{:S(2)}) collective-permute-start(f32[4,32,768]{2,1,0:T(8,128)S(1)} %bitcast.75), channel_id=1, source_target_pairs={{0,96},{1,97},{2,98},{3,99},{4,100},{5,101},{6,102},{7,103},{128,2... | collective-permute-start | bytes 1179656 | tf_op jit(solution)/shard_map/ppermute | solution.py:169
  12.1 3.9 %fusion.22 = f32[1024,192]{0,1:T(8,128)S(1)} fusion(bf16[1024,2048]{1,0:T(8,128)(2,1)} %bitcast.79, bf16[2048,192]{0,1:T(8,128)(2,1)S(1)} %copy-done), kind=kOutput, calls=%fused_computation.63 | convolution fusion | flops 805306368 | bytes 5767168 | tf_op jit(solution)/shard_map/dot_general | solution.py:179
  18.6 3.9 %collective-permute-done.3 = f32[4,32,768]{2,1,0:T(8,128)} collective-permute-done((f32[4,32,768]{2,1,0:T(8,128)S(1)}, f32[4,32,768]{2,1,0:T(8,128)}, u32[]{:S(2)}, u32[]{:S(2)}) %collective-permute-start.3) | collective-permute-done | bytes 393248 | tf_op jit(solution)/shard_map/ppermute | solution.py:169
  29.4 7.6 %collective-permute-start.8 = (f32[32,768]{1,0:T(8,128)S(1)}, f32[32,768]{1,0:T(8,128)S(1)}, u32[]{:S(2)}, u32[]{:S(2)}) collective-permute-start(f32[32,768]{1,0:T(8,128)S(1)} %fusion.16), channel_id=1, source_target_pairs={{0,0},{1,8},{2,16},{3,24},{4,32},{5,40},{6,48},{7,56},{128,64},{12... | collective-permute-start | bytes 294920 | tf_op jit(solution)/shard_map/ppermute | solution.py:206
  39.3 6.9 %collective-permute-start.11 = (f32[32,512]{1,0:T(8,128)S(1)}, f32[32,512]{1,0:T(8,128)S(1)}, u32[]{:S(2)}, u32[]{:S(2)}) collective-permute-start(f32[32,512]{1,0:T(8,128)S(1)} %slice.147), channel_id=1, source_target_pairs={{0,96},{1,97},{2,98},{3,99},{4,100},{5,101},{6,102},{7,103},{128,2... | collective-permute-start | bytes 196616 | tf_op jit(solution)/shard_map/ppermute | solution.py:209
  49.9 13.5 %all-to-all-start = ((bf16[16,4,1280]{2,1,0:T(4,128)(2,1)}), bf16[16,4,1280]{2,1,0:T(4,128)(2,1)S(1)}, u32[]{:S(2)}, u32[]{:S(2)}) async-start(bf16[16,4,1280]{2,1,0:T(4,128)(2,1)} %copy.25), calls=%async_computation | async-start | bytes 327680 | tf_op jit(solution)/shard_map/all_to_all | solution.py:198
  69.0 2.2 %all-to-all-done = bf16[16,4,1280]{2,1,0:T(4,128)(2,1)S(1)} async-done(((bf16[16,4,1280]{2,1,0:T(4,128)(2,1)}), bf16[16,4,1280]{2,1,0:T(4,128)(2,1)S(1)}, u32[]{:S(2)}, u32[]{:S(2)}) %all-to-all-start) | async-done | bytes 163872 | tf_op jit(solution)/shard_map/all_to_all | solution.py:198
  71.3 2.2 %collective-permute-start.1 = (bf16[64,768]{1,0:T(8,128)(2,1)S(1)}, bf16[64,768]{1,0:T(8,128)(2,1)S(1)}, u32[]{:S(2)}, u32[]{:S(2)}) collective-permute-start(bf16[64,768]{1,0:T(8,128)(2,1)S(1)} %slice.142), channel_id=1, source_target_pairs={{0,0},{1,8},{2,16},{3,24},{4,32},{5,40},{6,48},{7,56},{128,64},{12... | collective-permute-start | bytes 294920 | tf_op jit(solution)/shard_map/ppermute | solution.py:217
  73.5 1.8 %broadcast_in_dim.55 = bf16[16,64,1280]{2,1,0:T(8,128)(2,1)} broadcast(bf16[64,1280]{1,0:T(8,128)(2,1)S(1)} %reshape.64), dimensions={1,2} | broadcast | bytes 2785280 | tf_op jit(solution)/shard_map/broadcast_in_dim | solution.py:117
  75.3 6.9 %all-to-all-start.1 = ((bf16[16,64,1280]{2,1,0:T(8,128)(2,1)}), bf16[16,64,1280]{2,1,0:T(8,128)(2,1)}, u32[]{:S(2)}, u32[]{:S(2)}) async-start(bf16[16,64,1280]{2,1,0:T(8,128)(2,1)} %broadcast_in_dim.55), calls=%async_computation.1 | async-start | bytes 5242880 | tf_op jit(solution)/shard_map/all_to_all | solution.py:117
  82.2 8.6 %collective-permute-start.18 = (bf16[64,2048]{1,0:T(8,128)(2,1)S(1)}, bf16[64,2048]{1,0:T(8,128)(2,1)S(1)}, u32[]{:S(2)}, u32[]{:S(2)}) collective-permute-start(bf16[64,2048]{1,0:T(8,128)(2,1)S(1)} %maximum_maximum_fusion), channel_id=1, source_target_pairs={{0,7},{1,0},{2,1},{3,2},{4,3},{5,4},{6,5},{7,6},{8,15},{9,8},{10,9... | collective-permute-start | bytes 786440 | tf_op jit(solution)/shard_map/ppermute | solution.py:125
  93.5 13.8 %collective-permute-done.16 = bf16[64,2048]{1,0:T(8,128)(2,1)S(1)} collective-permute-done((bf16[64,2048]{1,0:T(8,128)(2,1)S(1)}, bf16[64,2048]{1,0:T(8,128)(2,1)S(1)}, u32[]{:S(2)}, u32[]{:S(2)}) %collective-permute-start.16) | collective-permute-done | bytes 262176 | tf_op jit(solution)/shard_map/ppermute | solution.py:125
  107.3 5.8 %collective-permute-start.22 = (bf16[32,2048]{1,0:T(8,128)(2,1)S(1)}, bf16[32,2048]{1,0:T(8,128)(2,1)S(1)}, u32[]{:S(2)}, u32[]{:S(2)}) collective-permute-start(bf16[32,2048]{1,0:T(8,128)(2,1)S(1)} %slice.149), channel_id=1, source_target_pairs={{0,6},{1,7},{2,0},{3,1},{4,2},{5,3},{6,4},{7,5},{8,14},{9,15},{10,... | collective-permute-start | bytes 393224 | tf_op jit(solution)/shard_map/ppermute | solution.py:125
  115.1 11.4 %collective-permute-done.19 = bf16[64,2048]{1,0:T(8,128)(2,1)S(1)} collective-permute-done((bf16[64,2048]{1,0:T(8,128)(2,1)S(1)}, bf16[64,2048]{1,0:T(8,128)(2,1)S(1)}, u32[]{:S(2)}, u32[]{:S(2)}) %collective-permute-start.19) | collective-permute-done | bytes 262176 | tf_op jit(solution)/shard_map/ppermute | solution.py:125
  129.2 4.4 %all-to-all-start.2 = ((f32[16,32,768]{2,1,0:T(8,128)}), f32[16,32,768]{2,1,0:T(8,128)}, u32[]{:S(2)}, u32[]{:S(2)}) async-start(f32[16,32,768]{2,1,0:T(8,128)} %broadcast_in_dim.56), calls=%async_computation.2 | async-start | bytes 3145728 | tf_op jit(solution)/shard_map/all_to_all | solution.py:117
  133.6 1.9 %broadcast_select_fusion.1 = (bf16[8,64,2048]{2,1,0:T(8,128)(2,1)S(1)}, bf16[8,64,2048]{2,1,0:T(8,128)(2,1)S(1)}) fusion(bf16[8,64,2048]{2,1,0:T(8,128)(2,1)S(1)} %fusion.13, bf16[8,64,2048]{2,1,0:T(8,128)(2,1)} %collective-permute-done.23, pred[]{:T(512)S(6)} %eq.11), kind=kLoop, calls=%fused_computation.2 | loop fusion | flops 2097152 | bytes 8388609 | tf_op jit(solution)/shard_map/jit(_where)/select_n | solution.py:224
  138.6 2.4 %convolution_add_fusion.a_ref = f32[512,512]{1,0:T(8,128)S(1)} fusion(f32[256,512]{1,0:T(8,128)S(1)} %bitcast.65, f32[256,512]{1,0:T(8,128)S(1)} %bitcast.74, bf16[1024,1280]{1,0:T(8,128)(2,1)} %bitcast.21), kind=kOutput, calls=%fused_computation.12 | convolution fusion | flops 537395200 | bytes 3145728 | tf_op jit(solution)/shard_map/dot_general | solution.py:144
  141.1 17.9 %inverse_factor.1 = f32[512,512]{1,0:T(8,128)S(1)} custom-call(f32[512,512]{1,0:T(8,128)S(1)} %convolution_add_fusion.a_ref), custom_call_target="tpu_custom_call" | custom-call | tf_op jit(solution)/shard_map/inverse_factor/pallas_call | solution.py:96
  159.0 2.4 %fusion.7 = f32[512,768]{1,0:T(8,128)S(1)} fusion(bf16[512,768]{1,0:T(8,128)(2,1)S(1)} %bitcast.71, bf16[512,768]{1,0:T(8,128)(2,1)S(1)} %bitcast.69, bf16[1024,1280]{1,0:T(8,128)(2,1)} %bitcast.21), kind=kOutput, calls=%fused_computation.21 | convolution fusion | flops 808452096 | bytes 4194304 | tf_op jit(solution)/shard_map/dot_general | solution.py:144
  164.1 4.7 %fusion.4 = f32[768,768]{1,0:T(8,128)} fusion(bf16[1024,1280]{1,0:T(8,128)(2,1)} %bitcast.21, bf16[512,768]{1,0:T(8,128)(2,1)} %bitcast.72, bf16[512,768]{1,0:T(8,128)(2,1)} %bitcast.70), kind=kOutput, calls=%fused_computation.10 | convolution fusion | flops 1211105280 | bytes 5505024 | tf_op jit(solution)/shard_map/dot_general | solution.py:144
  168.9 3.4 %bitcast_add_fusion = f32[512,768]{1,0:T(8,128)S(1)} fusion(f32[16,32,768]{2,1,0:T(8,128)} %all-to-all-done.2, bf16[1024,1280]{1,0:T(8,128)(2,1)} %bitcast.21), kind=kOutput, calls=%fused_computation.8 | convolution fusion | flops 805699584 | bytes 5767168 | tf_op jit(solution)/shard_map/dot_general | solution.py:144
  173.9 4.0 %add_subtract_fusion = f32[768,768]{1,0:T(8,128)} fusion(f32[768,768]{1,0:T(8,128)S(1)} %copy-done.2, f32[768,768]{1,0:T(8,128)S(1)} %copy-done.6, f32[512,768]{1,0:T(8,128)S(1)} %fusion, f32[512,768]{1,0:T(8,128)S(1)} %fusion.24), kind=kOutput, calls=%fused_computation | convolution fusion | flops 1813118976 | bytes 10223616 | tf_op jit(solution)/shard_map/dot_general | solution.py:240
  (111 shorter events, 37.2 us)
Async XLA Ops:
  2.2 16.4 %collective-permute-start.2 = (f32[4,32,768]{2,1,0:T(8,128)S(1)}, f32[4,32,768]{2,1,0:T(8,128)}, u32[]{:S(2)}, u32[]{:S(2)}) collective-permute-start(f32[4,32,768]{2,1,0:T(8,128)S(1)} %bitcast.77), channel_id=1, source_target_pairs={{0,32},{1,33},{2,34},{3,35},{4,36},{5,37},{6,38},{7,39},{128,160},... | collective-permute-start | bytes 1179656 | tf_op jit(solution)/shard_map/ppermute | solution.py:169
  7.0 15.4 %collective-permute-start.3 = (f32[4,32,768]{2,1,0:T(8,128)S(1)}, f32[4,32,768]{2,1,0:T(8,128)}, u32[]{:S(2)}, u32[]{:S(2)}) collective-permute-start(f32[4,32,768]{2,1,0:T(8,128)S(1)} %bitcast.76), channel_id=1, source_target_pairs={{0,64},{1,65},{2,66},{3,67},{4,68},{5,69},{6,70},{7,71},{128,192},... | collective-permute-start | bytes 1179656 | tf_op jit(solution)/shard_map/ppermute | solution.py:169
  10.0 12.4 %collective-permute-start.4 = (f32[4,32,768]{2,1,0:T(8,128)S(1)}, f32[4,32,768]{2,1,0:T(8,128)}, u32[]{:S(2)}, u32[]{:S(2)}) collective-permute-start(f32[4,32,768]{2,1,0:T(8,128)S(1)} %bitcast.75), channel_id=1, source_target_pairs={{0,96},{1,97},{2,98},{3,99},{4,100},{5,101},{6,102},{7,103},{128,2... | collective-permute-start | bytes 1179656 | tf_op jit(solution)/shard_map/ppermute | solution.py:169
  17.5 19.5 %collective-permute-start = (f32[4,128,256]{1,2,0:T(8,128)S(1)}, f32[4,128,256]{1,2,0:T(8,128)S(1)}, u32[]{:S(2)}, u32[]{:S(2)}) collective-permute-start(f32[4,128,256]{1,2,0:T(8,128)S(1)} %bitcast.73), channel_id=1, source_target_pairs={{0,128},{128,0},{1,129},{129,1},{2,130},{130,2},{3,131},{131,3},{4... | collective-permute-start | bytes 1572872 | tf_op jit(solution)/shard_map/ppermute | solution.py:186
  23.8 4.0 %collective-permute-start.6 = (f32[32,768]{1,0:T(8,128)S(1)}, f32[32,768]{1,0:T(8,128)S(1)}, u32[]{:S(2)}, u32[]{:S(2)}) collective-permute-start(f32[32,768]{1,0:T(8,128)S(1)} %get-tuple-element.24), channel_id=1, source_target_pairs={{0,16},{32,48},{64,80},{96,112},{1,17},{33,49},{65,81},{97,113},{2... | collective-permute-start | bytes 294920 | tf_op jit(solution)/shard_map/ppermute | solution.py:172
  26.4 3.0 %collective-permute-start.5 = (f32[32,768]{1,0:T(8,128)S(1)}, f32[32,768]{1,0:T(8,128)S(1)}, u32[]{:S(2)}, u32[]{:S(2)}) collective-permute-start(f32[32,768]{1,0:T(8,128)S(1)} %get-tuple-element.26), channel_id=1, source_target_pairs={{0,8},{32,40},{64,72},{96,104},{1,9},{33,41},{65,73},{97,105},{2,1... | collective-permute-start | bytes 294920 | tf_op jit(solution)/shard_map/ppermute | solution.py:172
  29.4 9.9 %collective-permute-start.8 = (f32[32,768]{1,0:T(8,128)S(1)}, f32[32,768]{1,0:T(8,128)S(1)}, u32[]{:S(2)}, u32[]{:S(2)}) collective-permute-start(f32[32,768]{1,0:T(8,128)S(1)} %fusion.16), channel_id=1, source_target_pairs={{0,0},{1,8},{2,16},{3,24},{4,32},{5,40},{6,48},{7,56},{128,64},{12... | collective-permute-start | bytes 294920 | tf_op jit(solution)/shard_map/ppermute | solution.py:206
  39.3 24.1 %collective-permute-start.11 = (f32[32,512]{1,0:T(8,128)S(1)}, f32[32,512]{1,0:T(8,128)S(1)}, u32[]{:S(2)}, u32[]{:S(2)}) collective-permute-start(f32[32,512]{1,0:T(8,128)S(1)} %slice.147), channel_id=1, source_target_pairs={{0,96},{1,97},{2,98},{3,99},{4,100},{5,101},{6,102},{7,103},{128,2... | collective-permute-start | bytes 196616 | tf_op jit(solution)/shard_map/ppermute | solution.py:209
  46.2 17.2 %collective-permute-start.10 = (f32[32,512]{1,0:T(8,128)S(1)}, f32[32,512]{1,0:T(8,128)S(1)}, u32[]{:S(2)}, u32[]{:S(2)}) collective-permute-start(f32[32,512]{1,0:T(8,128)S(1)} %slice.147), channel_id=1, source_target_pairs={{0,64},{1,65},{2,66},{3,67},{4,68},{5,69},{6,70},{7,71},{128,192},... | collective-permute-start | bytes 196616 | tf_op jit(solution)/shard_map/ppermute | solution.py:209
  47.5 15.9 %collective-permute-start.9 = (f32[32,512]{1,0:T(8,128)S(1)}, f32[32,512]{1,0:T(8,128)S(1)}, u32[]{:S(2)}, u32[]{:S(2)}) collective-permute-start(f32[32,512]{1,0:T(8,128)S(1)} %slice.147), channel_id=1, source_target_pairs={{0,32},{1,33},{2,34},{3,35},{4,36},{5,37},{6,38},{7,39},{128,160},... | collective-permute-start | bytes 196616 | tf_op jit(solution)/shard_map/ppermute | solution.py:209
  49.9 21.4 %all-to-all-start = ((bf16[16,4,1280]{2,1,0:T(4,128)(2,1)}), bf16[16,4,1280]{2,1,0:T(4,128)(2,1)S(1)}, u32[]{:S(2)}, u32[]{:S(2)}) async-start(bf16[16,4,1280]{2,1,0:T(4,128)(2,1)} %copy.25), calls=%async_computation | async-start | bytes 327680 | tf_op jit(solution)/shard_map/all_to_all | solution.py:198
  63.5 3.9 %collective-permute-start.14 = (f32[32,512]{1,0:T(8,128)S(1)}, f32[32,512]{1,0:T(8,128)S(1)}, u32[]{:S(2)}, u32[]{:S(2)}) collective-permute-start(f32[32,512]{1,0:T(8,128)S(1)} %add_select_fusion.2), channel_id=1, source_target_pairs={{0,24},{32,56},{64,88},{96,120},{1,25},{33,57},{65,89},{97,121},{2... | collective-permute-start | bytes 196616 | tf_op jit(solution)/shard_map/ppermute | solution.py:213
  71.3 10.8 %collective-permute-start.1 = (bf16[64,768]{1,0:T(8,128)(2,1)S(1)}, bf16[64,768]{1,0:T(8,128)(2,1)S(1)}, u32[]{:S(2)}, u32[]{:S(2)}) collective-permute-start(bf16[64,768]{1,0:T(8,128)(2,1)S(1)} %slice.142), channel_id=1, source_target_pairs={{0,0},{1,8},{2,16},{3,24},{4,32},{5,40},{6,48},{7,56},{128,64},{12... | collective-permute-start | bytes 294920 | tf_op jit(solution)/shard_map/ppermute | solution.py:217
  75.3 52.5 %all-to-all-start.1 = ((bf16[16,64,1280]{2,1,0:T(8,128)(2,1)}), bf16[16,64,1280]{2,1,0:T(8,128)(2,1)}, u32[]{:S(2)}, u32[]{:S(2)}) async-start(bf16[16,64,1280]{2,1,0:T(8,128)(2,1)} %broadcast_in_dim.55), calls=%async_computation.1 | async-start | bytes 5242880 | tf_op jit(solution)/shard_map/all_to_all | solution.py:117
  82.2 32.9 %collective-permute-start.18 = (bf16[64,2048]{1,0:T(8,128)(2,1)S(1)}, bf16[64,2048]{1,0:T(8,128)(2,1)S(1)}, u32[]{:S(2)}, u32[]{:S(2)}) collective-permute-start(bf16[64,2048]{1,0:T(8,128)(2,1)S(1)} %maximum_maximum_fusion), channel_id=1, source_target_pairs={{0,7},{1,0},{2,1},{3,2},{4,3},{5,4},{6,5},{7,6},{8,15},{9,8},{10,9... | collective-permute-start | bytes 786440 | tf_op jit(solution)/shard_map/ppermute | solution.py:125
  90.9 23.4 %collective-permute-start.17 = (bf16[64,2048]{1,0:T(8,128)(2,1)S(1)}, bf16[64,2048]{1,0:T(8,128)(2,1)S(1)}, u32[]{:S(2)}, u32[]{:S(2)}) collective-permute-start(bf16[64,2048]{1,0:T(8,128)(2,1)S(1)} %maximum_maximum_fusion), channel_id=1, source_target_pairs={{0,1},{1,2},{2,3},{3,4},{4,5},{5,6},{6,7},{7,0},{8,9},{9,10},{10,1... | collective-permute-start | bytes 786440 | tf_op jit(solution)/shard_map/ppermute | solution.py:125
  90.9 16.4 %collective-permute-start.16 = (bf16[64,2048]{1,0:T(8,128)(2,1)S(1)}, bf16[64,2048]{1,0:T(8,128)(2,1)S(1)}, u32[]{:S(2)}, u32[]{:S(2)}) collective-permute-start(bf16[64,2048]{1,0:T(8,128)(2,1)S(1)} %maximum_maximum_fusion), channel_id=1, source_target_pairs={{0,6},{1,7},{2,0},{3,1},{4,2},{5,3},{6,4},{7,5},{8,14},{9,15},{10,... | collective-permute-start | bytes 786440 | tf_op jit(solution)/shard_map/ppermute | solution.py:125
  92.1 21.0 %collective-permute-start.15 = (bf16[64,2048]{1,0:T(8,128)(2,1)S(1)}, bf16[64,2048]{1,0:T(8,128)(2,1)S(1)}, u32[]{:S(2)}, u32[]{:S(2)}) collective-permute-start(bf16[64,2048]{1,0:T(8,128)(2,1)S(1)} %maximum_maximum_fusion), channel_id=1, source_target_pairs={{0,2},{1,3},{2,4},{3,5},{4,6},{5,7},{6,0},{7,1},{8,10},{9,11},{10,... | collective-permute-start | bytes 786440 | tf_op jit(solution)/shard_map/ppermute | solution.py:125
  107.3 19.3 %collective-permute-start.22 = (bf16[32,2048]{1,0:T(8,128)(2,1)S(1)}, bf16[32,2048]{1,0:T(8,128)(2,1)S(1)}, u32[]{:S(2)}, u32[]{:S(2)}) collective-permute-start(bf16[32,2048]{1,0:T(8,128)(2,1)S(1)} %slice.149), channel_id=1, source_target_pairs={{0,6},{1,7},{2,0},{3,1},{4,2},{5,3},{6,4},{7,5},{8,14},{9,15},{10,... | collective-permute-start | bytes 393224 | tf_op jit(solution)/shard_map/ppermute | solution.py:125
  113.1 13.5 %collective-permute-start.21 = (bf16[32,2048]{1,0:T(8,128)(2,1)S(1)}, bf16[32,2048]{1,0:T(8,128)(2,1)S(1)}, u32[]{:S(2)}, u32[]{:S(2)}) collective-permute-start(bf16[32,2048]{1,0:T(8,128)(2,1)S(1)} %slice.148), channel_id=1, source_target_pairs={{0,2},{1,3},{2,4},{3,5},{4,6},{5,7},{6,0},{7,1},{8,10},{9,11},{10,... | collective-permute-start | bytes 393224 | tf_op jit(solution)/shard_map/ppermute | solution.py:125
  113.2 13.4 %collective-permute-start.20 = (bf16[64,2048]{1,0:T(8,128)(2,1)S(1)}, bf16[64,2048]{1,0:T(8,128)(2,1)S(1)}, u32[]{:S(2)}, u32[]{:S(2)}) collective-permute-start(bf16[64,2048]{1,0:T(8,128)(2,1)S(1)} %collective-permute-done.16), channel_id=1, source_target_pairs={{0,7},{1,0},{2,1},{3,2},{4,3},{5,4},{6,5},{7,6},{8,15},{9,8},{10,9... | collective-permute-start | bytes 786440 | tf_op jit(solution)/shard_map/ppermute | solution.py:125
  114.3 12.3 %collective-permute-start.19 = (bf16[64,2048]{1,0:T(8,128)(2,1)S(1)}, bf16[64,2048]{1,0:T(8,128)(2,1)S(1)}, u32[]{:S(2)}, u32[]{:S(2)}) collective-permute-start(bf16[64,2048]{1,0:T(8,128)(2,1)S(1)} %collective-permute-done.15), channel_id=1, source_target_pairs={{0,1},{1,2},{2,3},{3,4},{4,5},{5,6},{6,7},{7,0},{8,9},{9,10},{10,1... | collective-permute-start | bytes 786440 | tf_op jit(solution)/shard_map/ppermute | solution.py:125
  126.7 6.9 %collective-permute-start.23 = (bf16[8,64,2048]{2,1,0:T(8,128)(2,1)S(1)}, bf16[8,64,2048]{2,1,0:T(8,128)(2,1)}, u32[]{:S(2)}, u32[]{:S(2)}) collective-permute-start(bf16[8,64,2048]{2,1,0:T(8,128)(2,1)S(1)} %fusion.13), channel_id=1, source_target_pairs={{0,128},{128,0},{1,129},{129,1},{2,130},{130,2},{3,131},{131,3},{4... | collective-permute-start | bytes 6291464 | tf_op jit(solution)/shard_map/ppermute | solution.py:223
  129.2 39.7 %all-to-all-start.2 = ((f32[16,32,768]{2,1,0:T(8,128)}), f32[16,32,768]{2,1,0:T(8,128)}, u32[]{:S(2)}, u32[]{:S(2)}) async-start(f32[16,32,768]{2,1,0:T(8,128)} %broadcast_in_dim.56), calls=%async_computation.2 | async-start | bytes 3145728 | tf_op jit(solution)/shard_map/all_to_all | solution.py:117
  (16 other events, 92.1 us)
